TPU v7x, 128 devices: a whole 4x4x4 slice. The times are simulated.
128 devices in a mesh: dom: 16 (over x, y), grp: 8 (over z, core).
Axes of the slice: x: 4, y: 4, z: 4, core: 2. Of those that a mesh axis runs over, the one named last changes fastest.
Arguments:
- valence: float32 [128, 64, 1024], P('dom', None, 'grp')
- start_potential: float32 [128, 64, 1024], P('dom', None, 'grp'), may hold values from -3 to 3
- atom_tiles: float32 [32768, 512], P(('dom', 'grp')), may hold values from -12 to 12
- atom_home: int32 [32768, 1], P(('dom', 'grp')), may hold values from 0 to 127; in each aligned block of 256 rows (0 to 255, 256 to 511, ...) at most 4 rows name the same one
- atom_offset_x: int32 [32768, 1], P(('dom', 'grp')), may hold values from 0 to 7
- atom_offset_y: int32 [32768, 1], P(('dom', 'grp')), may hold values from 0 to 63
- atom_offset_z: int32 [32768, 1], P(('dom', 'grp')), may hold values from 0 to 120
- atom_size: int32 [32768, 1], P(('dom', 'grp')), may hold values from 4 to 8
Outputs:
- potential: float32 [128, 64, 1024], P('dom', None, 'grp')
- stress: float32 [6], replicated
Inputs may be any that keep to these rules, and one draw needn't show every extreme that they name: `atom_home`: at most 4 atoms among the rows of one device share a home, and some home has exactly 4 of them.
All inputs are finite; a program needn't handle non-finite values.
Results may differ from a plain program's by a relative error of at most 0.00014.
Values sent between devices are 32-bit elements; how exact they have to be, the bound alone decides.
No kernel may reach another device: no remote copies, remote signals or barrier semaphores. Data moves between devices by JAX's collectives and lax.ppermute only.
A program may use at most 128 MiB of HBM per device.

v0:
```python
import functools

import jax
import jax.numpy as jnp
from jax import lax
from jax.sharding import Mesh
from jax.sharding import PartitionSpec as P

TE = 8
NU = 2
DOM_GRP = ("dom_0", "dom_1", "grp_0", "grp_1")
DOM = ("dom_0", "dom_1")
GRP = ("grp_0", "grp_1")


DAMPING = 2.0 / 3.0


def extended(value, sides, width):
    edges = {}
    for axis, dim in sides:
        peers, length = (lax.axis_size(axis), value.shape[dim])
        up = [(i, (i + 1) % peers) for i in range(peers - 1)]
        last = lax.slice_in_dim(value, length - width, length, axis=dim)
        leading = lax.slice_in_dim(value, 0, width, axis=dim)
        edges[dim] = (
            lax.ppermute(last, axis, up),
            lax.ppermute(leading, axis, [(b, a) for a, b in up]),
        )
    done = []
    for _, dim in sides:
        low, high = edges[dim]
        around = [(width, width) if d in done else (0, 0) for d in range(value.ndim)]
        value = jnp.concatenate([jnp.pad(low, around), value, jnp.pad(high, around)], axis=dim)
        done.append(dim)
    return value


def from_everyone(value, axis):
    peers = lax.axis_size(axis)
    return lax.all_to_all(
        jnp.broadcast_to(value[None], (peers, *value.shape)), axis, 0, 0, tiled=True
    )


def laid_out(tiles, dim):
    tiles = jnp.moveaxis(tiles, 0, dim)
    shape = tiles.shape
    return tiles.reshape(*shape[:dim], shape[dim] * shape[dim + 1], *shape[dim + 2 :])


def gather_directly(value, axis, dim):
    tiles = from_everyone(value, axis)
    return laid_out(tiles, dim)


def in_blocks(value, dim, peers):
    shape = value.shape
    tiles = value.reshape(*shape[:dim], peers, shape[dim] // peers, *shape[dim + 1 :])
    return jnp.moveaxis(tiles, dim, 0)


def one_exchange(value, axis, axes, splits, concats):
    sizes = [lax.axis_size(a) for a in axes]
    tiles = in_blocks(value, splits[0], sizes[0])
    tiles = jnp.moveaxis(in_blocks(tiles, splits[1] + 1, sizes[1]), 0, 1)
    inside = tiles.shape[2:]
    tiles = tiles.reshape(-1, *inside)
    tiles = lax.all_to_all(tiles, axis, split_axis=0, concat_axis=0, tiled=True)
    tiles = laid_out(tiles.reshape(*sizes, *inside), concats[0] + 1)
    return laid_out(tiles, concats[1])


def from_behind(block, axis, distance):
    devices = range(lax.axis_size(axis))
    route = [(i - distance, i) for i in devices if i - distance in devices]
    return lax.ppermute(block, axis, route)


def by_axis(value, axes):
    return functools.reduce(lax.psum, axes, value)


def sine_basis(length_now):
    steps_now = jnp.arange(length_now, dtype=jnp.float32)
    table = jnp.sqrt(2.0 / (length_now + 1)) * jnp.sin(
        jnp.pi * (steps_now[:, None] + 1.0) * (steps_now[None, :] + 1.0) / (length_now + 1)
    )
    values = 2.0 - 2.0 * jnp.cos(jnp.pi * (steps_now + 1.0) / (length_now + 1))
    return (table, values)


def cyclic_basis(length_now):
    steps_now = jnp.arange(length_now, dtype=jnp.float32)[:, None]
    column = jnp.arange(length_now, dtype=jnp.int32)[None, :]
    freqs = ((column + 1) // 2).astype(jnp.float32)
    angles = 2.0 * jnp.pi * freqs * steps_now / length_now
    use_sine = (column % 2 == 0) & (column > 0)
    edge_cols = (column == 0) | (column == length_now - 1)
    scales = jnp.where(edge_cols, jnp.sqrt(1.0 / length_now), jnp.sqrt(2.0 / length_now))
    table = scales * jnp.where(use_sine, jnp.sin(angles), jnp.cos(angles))
    values = 2.0 - 2.0 * jnp.cos(2.0 * jnp.pi * freqs[0] / length_now)
    return (table, values)


def exact_solve(source, spacing_sq):
    table_x, values_x = sine_basis(source.shape[0])
    table_y, values_y = cyclic_basis(source.shape[1])
    table_z, values_z = sine_basis(source.shape[2])
    highest = lax.Precision.HIGHEST
    modes = jnp.einsum("ia,ijk->ajk", table_x, source, precision=highest)
    modes = jnp.einsum("jb,ajk->abk", table_y, modes, precision=highest)
    modes = jnp.einsum("kc,abk->abc", table_z, modes, precision=highest)
    modes = (
        modes
        * spacing_sq
        / (values_x[:, None, None] + values_y[None, :, None] + values_z[None, None, :])
    )
    result = jnp.einsum("kc,abc->abk", table_z, modes, precision=highest)
    result = jnp.einsum("jb,abk->ajk", table_y, result, precision=highest)
    return jnp.einsum("ia,ajk->ijk", table_x, result, precision=highest)


def neighbours(current):
    return extended(current, ((DOM, 0), (GRP, 2)), 1)


def operate(current, spacing_sq):
    padded = neighbours(current)
    beside = padded[2:, :, 1:-1] + padded[:-2, :, 1:-1]
    beside = beside + jnp.roll(current, 1, axis=1) + jnp.roll(current, -1, axis=1)
    beside = beside + padded[1:-1, :, 2:] + padded[1:-1, :, :-2]
    return (6.0 * current - beside) / spacing_sq


def smooth(current, source, spacing_sq, sweeps):
    for step_index in range(sweeps):
        if current is None:
            current = DAMPING * spacing_sq / 6.0 * source
        else:
            current = current + DAMPING * spacing_sq / 6.0 * (source - operate(current, spacing_sq))
    return current


def restrict(residue):
    dims_now = residue.shape
    coarse = residue.reshape(dims_now[0] // 2, 2, dims_now[1] // 2, 2, dims_now[2] // 2, 2)
    return coarse.mean(axis=(1, 3, 5))


def prolong(correction):
    dims_now = correction.shape
    spread = jnp.broadcast_to(
        correction[:, None, :, None, :, None], (dims_now[0], 2, dims_now[1], 2, dims_now[2], 2)
    )
    return spread.reshape(dims_now[0] * 2, dims_now[1] * 2, dims_now[2] * 2)


def vcycle(level_index, current, source, layout, gather_level):
    if layout == "split" and level_index == gather_level:
        column = gather_directly(source, GRP, 2)
        whole_grid = gather_directly(column, DOM, 0)
        joined = vcycle(level_index, None, whole_grid, "whole", gather_level)
        own_width = source.shape[0]
        own_depth = source.shape[2]
        mine = lax.dynamic_slice_in_dim(joined, lax.axis_index(DOM) * own_width, own_width, 0)
        return lax.dynamic_slice_in_dim(mine, lax.axis_index(GRP) * own_depth, own_depth, 2)
    spacing_sq = 4.0**level_index
    if level_index == 3:
        return exact_solve(source, spacing_sq)
    current = smooth(current, source, spacing_sq, NU)
    residue = source - operate(current, spacing_sq)
    correction = vcycle(level_index + 1, None, restrict(residue), layout, gather_level)
    current = current + prolong(correction)
    return smooth(current, source, spacing_sq, NU)


def shards(
    valence,
    start_potential,
    atom_tiles,
    atom_home,
    atom_offset_x,
    atom_offset_y,
    atom_offset_z,
    atom_size,
):
    domain_count = lax.axis_size(DOM)
    group_count = lax.axis_size(GRP)
    device_count = domain_count * group_count
    atoms_here = atom_tiles.shape[0]
    tile_cells = atom_tiles.shape[1]
    capacity = 2 * atoms_here // device_count
    tile_index = jnp.arange(TE, dtype=jnp.int32)
    inside = tile_index[None, :] < atom_size
    inside_cube = inside[:, :, None, None] & inside[:, None, :, None] & inside[:, None, None, :]
    masked = atom_tiles * inside_cube.reshape(atom_tiles.shape).astype(jnp.float32)
    targets = jnp.arange(device_count, dtype=jnp.int32)
    matches = (atom_home == targets[None, :]).astype(jnp.int32)
    before = jnp.cumsum(matches, axis=0) - matches
    slot_rank = jnp.sum(before * matches, axis=1)
    slot_index = atom_home[:, 0] * capacity + slot_rank
    offsets = jnp.concatenate([atom_offset_x, atom_offset_y, atom_offset_z], axis=1)
    send_tiles = (
        jnp.zeros((device_count * capacity, tile_cells), jnp.float32).at[slot_index].set(masked)
    )
    send_offsets = jnp.zeros((device_count * capacity, 3), jnp.int32).at[slot_index].set(offsets)
    got_tiles, got_offsets = (
        one_exchange(
            send_tiles.reshape(domain_count, group_count, capacity, tile_cells),
            DOM_GRP,
            (DOM, GRP),
            (0, 1),
            (0, 1),
        ),
        one_exchange(
            send_offsets.reshape(domain_count, group_count, capacity, 3),
            DOM_GRP,
            (DOM, GRP),
            (0, 1),
            (0, 1),
        ),
    )
    got_tiles = got_tiles.reshape(-1, tile_cells)
    got_offsets = got_offsets.reshape(-1, 3)
    slot_count = got_tiles.shape[0]
    width_x, width_y, width_z = valence.shape
    cells_x = got_offsets[:, 0:1] + tile_index[None, :]
    cells_y = (got_offsets[:, 1:2] + tile_index[None, :]) % width_y
    cells_z = got_offsets[:, 2:3] + tile_index[None, :]
    tile_shape = (slot_count, TE, TE, TE)
    index_x = jnp.broadcast_to(cells_x[:, :, None, None], tile_shape)
    index_y = jnp.broadcast_to(cells_y[:, None, :, None], tile_shape)
    index_z = jnp.broadcast_to(cells_z[:, None, None, :], tile_shape)
    deposit_grid = (
        jnp.zeros((width_x + TE, width_y, width_z), jnp.float32)
        .at[index_x, index_y, index_z]
        .add(got_tiles.reshape(tile_shape))
    )
    spill_planes = deposit_grid[width_x:]
    incoming = from_behind(spill_planes, DOM, 1)
    local_grid = deposit_grid[:width_x].at[:TE].add(incoming)
    density = valence + local_grid
    gather_level = 3
    potential = vcycle(0, start_potential, density, "split", gather_level)
    padded = neighbours(potential)
    grad_x = 0.5 * (padded[2:, :, 1:-1] - padded[:-2, :, 1:-1])
    grad_y = 0.5 * (jnp.roll(potential, -1, axis=1) - jnp.roll(potential, 1, axis=1))
    grad_z = 0.5 * (padded[1:-1, :, 2:] - padded[1:-1, :, :-2])
    local_totals = jnp.stack(
        [
            jnp.sum(grad_x * grad_x),
            jnp.sum(grad_y * grad_y),
            jnp.sum(grad_z * grad_z),
            jnp.sum(grad_y * grad_z),
            jnp.sum(grad_x * grad_z),
            jnp.sum(grad_x * grad_y),
            jnp.sum(potential * density),
        ]
    )
    totals = by_axis(local_totals, DOM_GRP)
    cell_count = width_x * width_y * width_z * device_count
    products = totals[:6] / cell_count
    energy = 0.5 * totals[6] / cell_count
    diagonal_mask = jnp.array([1.0, 1.0, 1.0, 0.0, 0.0, 0.0], jnp.float32)
    stress = products - energy * diagonal_mask
    return (potential, stress)


def solution(mesh):
    split = Mesh(mesh.devices.reshape(4, 4, 4, 2), ("dom_0", "dom_1", "grp_0", "grp_1"))
    return jax.shard_map(
        shards,
        mesh=split,
        in_specs=(
            P(DOM, None, GRP),
            P(DOM, None, GRP),
            P(DOM_GRP, None),
            P(DOM_GRP, None),
            P(DOM_GRP, None),
            P(DOM_GRP, None),
            P(DOM_GRP, None),
            P(DOM_GRP, None),
        ),
        out_specs=(P(DOM, None, GRP), P()),
        check_vma=False,
    )
```

profile of v0, /device:TPU:1, one launch (start us, length us, event | category | flops | bytes accessed | tf_op | source)
XLA Modules:
  0.0 2182.1 jit_solution(1365932042346540308)
XLA Ops:
  7.0 11.5 all-to-all-start
  37.0 10.3 all-to-all-start.1
  49.5 13.5 copy.47
  63.0 11.8 reshape.462
  76.0 1785.5 %scatter_custom_fusion.2 = f32[131072]{0:T(1024)S(1)} fusion(s32[262144]{0:T(1024)S(1)} %reshape.462, f32[262144]{0:T(1024)} %bitcast.98, f32[]{:T(128)} %constant.192.clone.1), kind=kCustom, calls=%fused_computation.124 | custom fusion | flops 262144 | bytes 524800
  1867.7 7.4 collective-permute-start.7
  1878.5 4.9 collective-permute-start.6
  1890.5 4.1 collective-permute-start.10
  1900.2 18.1 reshape.435
  1918.3 7.0 reduce_sum.110
  1928.0 4.7 collective-permute-start.16
  1946.0 6.5 collective-permute-start.18
  1962.9 6.1 collective-permute-start.22
  1976.8 6.1 collective-permute-start.26
  1984.7 6.1 all-to-all-start.2
  1990.8 4.5 all-to-all-done.2
  1997.3 15.3 all-to-all-start.3
  2012.6 6.5 all-to-all-done.3
  2021.8 4.0 collective-permute-start.31
  2041.1 4.4 collective-permute-start.34
  2055.4 4.2 collective-permute-start.38
  2067.6 4.5 collective-permute-start.42
  2072.8 6.5 broadcast_in_dim.139
  2079.3 12.6 reshape.439
  2099.1 5.2 collective-permute-start.46
  2112.6 6.5 collective-permute-start.50
  2127.5 6.3 collective-permute-start.54
  2135.9 4.6 stack.31
  2140.5 17.9 psum.28
  2158.4 6.0 psum.29
  2164.4 6.4 psum.30
  2170.8 9.5 psum.31
  (280 shorter events, 150.5 us)
Async XLA Ops:
  7.0 30.0 %all-to-all-start = ((s32[128,1,1,4,3]{3,2,4,1,0:T(1,128)}), s32[128,1,1,4,3]{3,2,4,1,0:T(1,128)S(1)}, u32[]{:S(2)}, u32[]{:S(2)}) async-start(s32[128,1,1,4,3]{3,2,4,1,0:T(1,128)} %copy.45), calls=%async_computation | async-start | bytes 393216 | tf_op jit(solution)/shard_map/all_to_all | solution.py:69
  19.3 1843.7 %collective-permute-start.2 = (f32[1,64,128]{2,1,0:T(8,128)S(1)}, f32[1,64,128]{2,1,0:T(8,128)S(1)}, u32[]{:S(2)}, u32[]{:S(2)}) collective-permute-start(f32[1,64,128]{2,1,0:T(8,128)S(1)} %get-tuple-element.80), channel_id=1, source_target_pairs={{0,8},{8,16},{16,24},{24,32},{32,40},{40,48},{48,56},{56,64},{64,7... | collective-permute-start | bytes 98312 | tf_op jit(solution)/shard_map/ppermute | solution.py:27
  22.5 1840.5 %collective-permute-start.1 = (f32[1,64,128]{2,1,0:T(8,128)S(1)}, f32[1,64,128]{2,1,0:T(8,128)S(1)}, u32[]{:S(2)}, u32[]{:S(2)}) collective-permute-start(f32[1,64,128]{2,1,0:T(8,128)S(1)} %get-tuple-element.79), channel_id=1, source_target_pairs={{8,0},{16,8},{24,16},{32,24},{40,32},{48,40},{56,48},{64,56},{72,6... | collective-permute-start | bytes 98312 | tf_op jit(solution)/shard_map/ppermute | solution.py:28
  25.7 1837.3 %collective-permute-start.3 = (f32[8,64,1]{2,1,0:T(8,128)}, f32[8,64,1]{2,1,0:T(8,128)}, u32[]{:S(2)}, u32[]{:S(2)}) collective-permute-start(f32[8,64,1]{2,1,0:T(8,128)} %get-tuple-element.77), channel_id=1, source_target_pairs={{1,0},{2,1},{3,2},{4,3},{5,4},{6,5},{7,6},{9,8},{10,9},{11,10},{12... | collective-permute-start | bytes 6152 | tf_op jit(solution)/shard_map/ppermute | solution.py:28
  28.3 1834.7 %collective-permute-start.4 = (f32[8,64,1]{2,1,0:T(8,128)}, f32[8,64,1]{2,1,0:T(8,128)}, u32[]{:S(2)}, u32[]{:S(2)}) collective-permute-start(f32[8,64,1]{2,1,0:T(8,128)} %get-tuple-element.78), channel_id=1, source_target_pairs={{0,1},{1,2},{2,3},{3,4},{4,5},{5,6},{6,7},{8,9},{9,10},{10,11},{11... | collective-permute-start | bytes 6152 | tf_op jit(solution)/shard_map/ppermute | solution.py:27
  37.0 37.7 %all-to-all-start.1 = ((f32[128,1,1,4,512]{4,3,2,1,0:T(4,128)}), f32[128,1,1,4,512]{4,3,2,1,0:T(4,128)S(1)}, u32[]{:S(2)}, u32[]{:S(2)}) async-start(f32[128,1,1,4,512]{4,3,2,1,0:T(4,128)} %bitcast.17), calls=%async_computation.1 | async-start | bytes 2097152 | tf_op jit(solution)/shard_map/all_to_all | solution.py:69
  1867.7 15.7 collective-permute-start.7
  1875.1 8.3 collective-permute-start.8
  1884.9 11.0 collective-permute-start.11
  1925.4 12.6 collective-permute-start.15
  1928.0 10.1 collective-permute-start.16
  1939.2 13.4 collective-permute-start.19
  1941.1 11.4 collective-permute-start.20
  1956.0 13.0 collective-permute-start.23
  1957.9 11.1 collective-permute-start.24
  1969.9 13.0 collective-permute-start.27
  1971.8 11.1 collective-permute-start.28
  1984.7 10.6 all-to-all-start.2
  1997.3 21.8 all-to-all-start.3
  2021.8 11.4 collective-permute-start.31
  2034.2 11.3 collective-permute-start.35
  2037.6 8.0 collective-permute-start.36
  2048.5 11.1 collective-permute-start.39
  2051.6 8.1 collective-permute-start.40
  2060.7 11.4 collective-permute-start.43
  2063.7 8.4 collective-permute-start.44
  2092.2 12.1 collective-permute-start.47
  2095.1 9.2 collective-permute-start.48
  2105.7 13.4 collective-permute-start.51
  2107.7 11.5 collective-permute-start.52
  2120.7 13.2 collective-permute-start.55
  2122.6 11.3 collective-permute-start.56
  (43 other events, 2643.6 us)
where the time goes:
time: 2180 us
  other arithmetic  1800 us (83%)
  starting transfers between devices  217 us (10%)
  local copies, waits for them, and re-layouts  87.2 us (4%)
  blocking collectives  39.9 us (2%)
  waiting for transfers between devices  28 us (1%)
    unnamed x4, other arithmetic  1790 us
    ppermute x28, starting transfers between devices, extended(): lax.ppermute(last, axis, up)  113 us
    ppermute x28, starting transfers between devices, extended(): lax.ppermute(leading, axis, [(b, a) for a, b in up])  59.8 us
  transfers between devices with their start and end apart: 61, of which 16 were waited for; matrix products, arithmetic and copies ran while one was open for 84% of the time, Pallas kernels for 0%

commit v1 on v0

v1 whole, which is shorter than its diff:
```python
import functools

import jax
import jax.numpy as jnp
import numpy as np
from jax import lax
from jax.experimental import pallas as pl
from jax.experimental.pallas import tpu as pltpu
from jax.sharding import Mesh
from jax.sharding import PartitionSpec as P

TE = 8
CAP = 4
DOM = ("dom_0", "dom_1")
GRP = ("grp_0", "grp_1")
ALL = DOM + GRP
F32 = jnp.float32
I32 = jnp.int32
HI = lax.Precision.HIGHEST
VM = pl.BlockSpec(memory_space=pltpu.VMEM)
SM = pl.BlockSpec(memory_space=pltpu.SMEM)

CX, CY, CZ = 8, 64, 128
NDOM, NGRP = 16, 8
NDEV = NDOM * NGRP
ATOMS = 256
TILE_ROWS = 4
LANES = 128
MSG = CAP * TILE_ROWS * LANES + LANES
PAR = pltpu.CompilerParams(vmem_limit_bytes=48 * 1024 * 1024)


def sds(*shape, dtype=F32):
    return jax.ShapeDtypeStruct(shape, dtype)


def lanes_of(shape):
    return lax.broadcasted_iota(I32, shape, len(shape) - 1)


def rows_of(shape):
    return lax.broadcasted_iota(I32, shape, len(shape) - 2)


def dot(a, b):
    return lax.dot_general(
        a, b, (((1,), (0,)), ((), ())), precision=HI, preferred_element_type=F32
    )


def pack_kernel(scal, tiles, out, rows, slots, corners, count):
    corners[...] = jnp.zeros_like(corners)
    for r in range(TILE_ROWS):
        for g in range(ATOMS // 8):
            rows[pl.ds(g * 8 * TILE_ROWS + r, 8, stride=TILE_ROWS), :] = tiles[
                g * 8 : g * 8 + 8, r * LANES : (r + 1) * LANES
            ]

    def clear(i, c):
        count[i] = 0
        return c

    lax.fori_loop(0, NDEV, clear, 0, unroll=8)
    lane = lanes_of((1, LANES))

    def one(n, c):
        home = scal[n]
        rank = count[home]
        count[home] = rank + 1
        slots[pl.ds(home * (CAP * TILE_ROWS) + rank * TILE_ROWS, TILE_ROWS), :] = rows[
            pl.ds(n * TILE_ROWS, TILE_ROWS), :
        ]
        first = rank * 4
        old = corners[pl.ds(home, 1), :]
        for i in range(4):
            value = scal[ATOMS * (i + 1) + n].astype(F32)
            old = jnp.where(lane == first + i, value, old)
        corners[pl.ds(home, 1), :] = old
        return c

    lax.fori_loop(0, ATOMS, one, 0, unroll=4)
    for g in range(NDEV // 8):
        for j in range(CAP * TILE_ROWS):
            out[g * 8 : g * 8 + 8, j * LANES : (j + 1) * LANES] = slots[
                pl.ds(g * 8 * CAP * TILE_ROWS + j, 8, stride=CAP * TILE_ROWS), :
            ]
    out[:, CAP * TILE_ROWS * LANES :] = corners[...]


def pack_atoms(scal, tiles):
    return pl.pallas_call(
        pack_kernel,
        out_shape=sds(NDEV, MSG),
        in_specs=[SM, VM],
        out_specs=VM,
        scratch_shapes=[
            pltpu.VMEM((ATOMS * TILE_ROWS, LANES), F32),
            pltpu.VMEM((NDEV * CAP * TILE_ROWS, LANES), F32),
            pltpu.VMEM((NDEV, LANES), F32),
            pltpu.SMEM((NDEV,), I32),
        ],
        compiler_params=PAR,
        name="pack_atoms",
    )(scal, tiles)


ZB = CZ // 8 + 1
YB = 4


def deposit_kernel(got, grid, up2, down, tiles, acc, corner_v, corner_s, sem):
    corner_v[...] = got[:, CAP * TILE_ROWS * LANES :].astype(I32)
    copy = pltpu.make_async_copy(corner_v, corner_s, sem)
    copy.start()
    def spread(g, c):
        for k in range(CAP):
            for r in range(TILE_ROWS):
                j = k * TILE_ROWS + r
                col = got[pl.ds(pl.multiple_of(g * 8, 8), 8), j * LANES : (j + 1) * LANES]
                base = g * 8 * CAP * TE + k * TE + 2 * r
                tiles[pl.ds(base, 8, stride=CAP * TE), :] = col
                tiles[pl.ds(base + 1, 8, stride=CAP * TE), :] = pltpu.roll(col, 64, 1)
        return c

    lax.fori_loop(0, NDEV // 8, spread, 0)

    def clear(i, c):
        acc[pl.ds(pl.multiple_of(i * 16, 16), 16), :] = jnp.zeros((16, LANES), F32)
        return c

    lax.fori_loop(0, YB * ZB, clear, 0, unroll=4)
    copy.wait()
    lane = lanes_of((8, LANES))
    tile_a = rows_of((8, LANES))
    tile_b = lane // 8
    tile_c = lane % 8
    need = jnp.maximum(jnp.maximum(tile_a, tile_b), tile_c)
    need = jnp.where(lane < 64, need, 99)

    def one(src, c):
        for k in range(CAP):
            ox = corner_s[src, 4 * k]
            oy = corner_s[src, 4 * k + 1]
            oz = corner_s[src, 4 * k + 2]
            size = corner_s[src, 4 * k + 3]
            value = tiles[pl.ds(pl.multiple_of((src * CAP + k) * TE, 8), TE), :]
            value = jnp.where(need < size, value, 0.0)
            z_in, z_block = oz & 7, oz >> 3
            y_in, y_block = oy & 15, oy >> 4
            near = jnp.where(tile_c < 8 - z_in, value, 0.0)
            far = jnp.where(tile_c < 8 - z_in, 0.0, value)
            shift = y_in * 8 + z_in
            near = pltpu.roll(near, shift, 1)
            far = pltpu.roll(far, (shift + 120) & 127, 1)
            same = lane >= y_in * 8
            row = (y_block * ZB + z_block) * 16 + ox
            wrapped = (((y_block + 1) & 3) * ZB + z_block) * 16 + ox
            acc[pl.ds(row, 8), :] += jnp.where(same, near, 0.0)
            acc[pl.ds(row + 16, 8), :] += jnp.where(same, far, 0.0)
            acc[pl.ds(wrapped, 8), :] += jnp.where(same, 0.0, near)
            acc[pl.ds(wrapped + 16, 8), :] += jnp.where(same, 0.0, far)
        return c

    lax.fori_loop(0, NDEV, one, 0)
    group = lane // 8

    def lay_out(yb, c):
        for xg in range(2):
            blocks = [
                acc[pl.ds(pl.multiple_of((yb * ZB + zb) * 16 + xg * 8, 8), 8), :]
                for zb in range(CZ // 8)
            ]
            for yy in range(16):
                row = jnp.zeros((8, LANES), F32)
                for zb in range(CZ // 8):
                    moved = pltpu.roll(blocks[zb], (8 * zb - 8 * yy) % 128, 1)
                    row = jnp.where(group == zb, moved, row)
                grid[pl.ds(xg * 8 * CY + yb * 16 + yy, 8, stride=CY), :] = row
        return c

    lax.fori_loop(0, YB, lay_out, 0)
    up2[...] = grid[10 * CY : 15 * CY, :]
    down[...] = grid[0 : 6 * CY, :]


def deposit(got):
    return pl.pallas_call(
        deposit_kernel,
        out_shape=(sds(16 * CY, LANES), sds(5 * CY, LANES), sds(6 * CY, LANES)),
        in_specs=[VM],
        out_specs=(VM, VM, VM),
        scratch_shapes=[
            pltpu.VMEM((NDEV * CAP * TE, LANES), F32),
            pltpu.VMEM((YB * ZB * 16, LANES), F32),
            pltpu.VMEM((NDEV, LANES), I32),
            pltpu.SMEM((NDEV, LANES), I32),
            pltpu.SemaphoreType.DMA,
        ],
        compiler_params=PAR,
        name="deposit",
    )(got)


HU, HF = 7, 6
NU_, NF = CX + 2 * HU, CX + 2 * HF
PACKED = NU_ + NF
ZGROUPS = -(-PACKED // 8)


def join_kernel(grid, from1, from2, above, valence, v_lo, v_hi, start, u_lo, u_hi, f, u, left, right):
    u[0:HU] = u_lo[...]
    u[HU : HU + CX] = start[...]
    u[HU + CX :] = u_hi[...]
    for p in range(NF):
        x = p - HF
        if x < 0:
            total = v_lo[p] + from1[x + 6]
            if x < -1:
                total = total + from2[x + 6]
        elif x < CX:
            total = valence[x] + grid[x * CY : (x + 1) * CY, :]
            if x < 7:
                total = total + from1[x + 6]
        else:
            total = v_hi[x - CX] + above[x - CX]
            if x < 15:
                total = total + grid[x * CY : (x + 1) * CY, :]
        f[p] = total
    slot = lanes_of((CY, LANES)) // 16
    for g in range(ZGROUPS):
        lo = jnp.zeros((CY, LANES), F32)
        hi = jnp.zeros((CY, LANES), F32)
        for k in range(8):
            p = g * 8 + k
            if p < PACKED:
                plane = u[p] if p < NU_ else f[p - NU_]
                lo = jnp.where(slot == k, pltpu.roll(plane, (16 * k) % 128, 1) if k else plane, lo)
                shift = (16 * k - 112) % 128
                hi = jnp.where(slot == k, pltpu.roll(plane, shift, 1) if shift else plane, hi)
        left[g] = lo
        right[g] = hi


def join(*args):
    return pl.pallas_call(
        join_kernel,
        out_shape=(
            sds(NF, CY, LANES),
            sds(NU_, CY, LANES),
            sds(ZGROUPS, CY, LANES),
            sds(ZGROUPS, CY, LANES),
        ),
        in_specs=[VM] * 10,
        out_specs=(VM,) * 4,
        compiler_params=PAR,
        name="join",
    )(*args)


W0 = 256
X1, Y1, Z1 = 4, 32, 64
X2, Y2, Z2 = 2, 16, 32


def beside(ref, p):
    c = ref[p]
    n, w = c.shape
    return c, (
        ref[p + 1]
        + ref[p - 1]
        + (pltpu.roll(c, 1, 0) + pltpu.roll(c, n - 1, 0))
        + (pltpu.roll(c, 1, 1) + pltpu.roll(c, w - 1, 1))
    )


def z_mask(width, own, grp, total):
    lane = lanes_of((1, width))
    split = own + (width - own) // 2
    z = grp * own + jnp.where(lane < split, lane, lane - width)
    return ((z >= 0) & (z < total)).astype(F32)


def x_ok(x, total):
    return jnp.where((x >= 0) & (x < total), 1.0, 0.0).astype(F32)


def halves(n):
    r = lax.broadcasted_iota(I32, (n, 2 * n), 0)
    c = lax.broadcasted_iota(I32, (n, 2 * n), 1)
    return ((c // 2) == r).astype(F32)


def doubles(n):
    r = lax.broadcasted_iota(I32, (2 * n, n), 0)
    c = lax.broadcasted_iota(I32, (2 * n, n), 1)
    return ((r // 2) == c).astype(F32)


def lane_halves(n):
    r = lax.broadcasted_iota(I32, (2 * n, n), 0)
    c = lax.broadcasted_iota(I32, (2 * n, n), 1)
    return ((r // 2) == c).astype(F32)


def before_kernel(place, f_in, u_in, from_left, from_right, u2, f, f1, chunk, u, ua, ub, pairs, v1, r1):
    dom, grp = place[0], place[1]
    lane = lanes_of((CY, LANES))
    for p in range(PACKED):
        g, k = p // 8, p % 8
        right = from_right[g]
        right = pltpu.roll(right, (-16 * k) % 128, 1) if k else right
        left = from_left[g]
        shift = (112 - 16 * k) % 128
        left = pltpu.roll(left, shift, 1) if shift else left
        edge = jnp.where(lane < 16, right, jnp.where(lane >= 112, left, 0.0))
        if p < NU_:
            u[p, :, 0:LANES] = u_in[p]
            u[p, :, LANES:] = edge
        else:
            f[p - NU_, :, 0:LANES] = f_in[p - NU_]
            f[p - NU_, :, LANES:] = edge
    mask = z_mask(W0, CZ, grp, NGRP * CZ)

    def sweep1(p, c):
        centre, around = beside(u, p + 1)
        new = (3.0 * centre + around + f[p]) * (1.0 / 9.0)
        ua[p] = new * (mask * x_ok(dom * CX + p - HF, NDOM * CX))
        return c

    lax.fori_loop(0, NF, sweep1, 0)

    def sweep2(p, c):
        centre, around = beside(ua, p + 1)
        new = (3.0 * centre + around + f[p + 1]) * (1.0 / 9.0)
        u2[p] = new * (mask * x_ok(dom * CX + p - 5, NDOM * CX))
        return c

    lax.fori_loop(0, NF - 2, sweep2, 0)

    def residue0(q, c):
        total = None
        for i in range(2):
            p = 2 * q + i + 1
            centre, around = beside(u2, p)
            r = f[p + 1] - (6.0 * centre - around)
            total = r if total is None else total + r
        pairs[pl.ds(pl.multiple_of(q * CY, CY), CY), :] = total
        return c

    lax.fori_loop(0, 8, residue0, 0)
    summed = dot(pairs[...], lane_halves(LANES))
    half_y = halves(Y1) * 0.125
    mask1 = z_mask(LANES, Z1, grp, NGRP * Z1)
    for q in range(8):
        part = dot(half_y, summed[q * CY : (q + 1) * CY, :])
        f1[q] = part * (mask1 * x_ok(dom * X1 + q - 2, NDOM * X1))
    for q in range(8):
        v1[q] = f1[q] * (4.0 / 9.0)
    for q in range(1, 7):
        centre, around = beside(v1, q)
        new = (3.0 * centre + around + 4.0 * f1[q]) * (1.0 / 9.0)
        r1[q] = new * (mask1 * x_ok(dom * X1 + q - 2, NDOM * X1))
    half_y2 = halves(Y2) * 0.125
    lane_half = lane_halves(LANES // 2)
    rows = []
    for i in range(2):
        total = None
        for j in range(2):
            q = 2 + 2 * i + j
            centre, around = beside(r1, q)
            r = f1[q] - (6.0 * centre - around) * 0.25
            total = r if total is None else total + r
        rows.append(total)
    both = dot(jnp.concatenate(rows, axis=0), jnp.concatenate([lane_half, jnp.zeros_like(lane_half)], axis=1))
    packed = jnp.zeros((8, LANES), F32)
    slot = lanes_of((8, LANES)) // 32
    for i in range(2):
        part = dot(half_y2, both[i * Y1 : (i + 1) * Y1, :])
        for yb in range(2):
            s = 2 * i + yb
            piece = part[yb * 8 : yb * 8 + 8, :]
            piece = pltpu.roll(piece, 32 * s, 1) if s else piece
            packed = jnp.where(slot == s, piece, packed)

    def spread(d, c):
        chunk[d] = packed
        return c

    lax.fori_loop(0, NDEV, spread, 0, unroll=8)


def before(place, f, u, from_left, from_right):
    return pl.pallas_call(
        before_kernel,
        out_shape=(
            sds(NF - 2, CY, W0),
            sds(NF, CY, W0),
            sds(8, Y1, LANES),
            sds(NDEV, 8, LANES),
        ),
        in_specs=[SM, VM, VM, VM, VM],
        out_specs=(VM,) * 4,
        scratch_shapes=[
            pltpu.VMEM((NU_, CY, W0), F32),
            pltpu.VMEM((NF, CY, W0), F32),
            pltpu.VMEM((8, LANES), F32),
            pltpu.VMEM((8 * CY, W0), F32),
            pltpu.VMEM((8, Y1, LANES), F32),
            pltpu.VMEM((8, Y1, LANES), F32),
        ],
        compiler_params=PAR,
        name="before",
    )(place, f, u, from_left, from_right)


NX2, NZ2 = NDOM * X2, NGRP * Z2
NX3, NY3, NZ3 = NX2 // 2, Y2 // 2, NZ2 // 2
PAD2 = 4


def tables():
    def sine(n):
        k = np.arange(n) + 1.0
        t = np.sqrt(2.0 / (n + 1)) * np.sin(np.pi * np.outer(k, k) / (n + 1))
        return t, 2.0 - 2.0 * np.cos(np.pi * k / (n + 1))

    def cyclic(n):
        j = np.arange(n)[:, None]
        col = np.arange(n)[None, :]
        freq = (col + 1) // 2
        angle = 2.0 * np.pi * freq * j / n
        use_sine = (col % 2 == 0) & (col > 0)
        edge = (col == 0) | (col == n - 1)
        t = np.where(edge, np.sqrt(1.0 / n), np.sqrt(2.0 / n)) * np.where(
            use_sine, np.sin(angle), np.cos(angle)
        )
        return t, 2.0 - 2.0 * np.cos(2.0 * np.pi * freq[0] / n)

    tx, lx = sine(NX3)
    ty, ly = cyclic(NY3)
    tz, lz = sine(NZ3)
    txy = np.kron(tx, ty)
    lxy = (lx[:, None] + ly[None, :]).reshape(-1)
    scale = 64.0 / (lxy[:, None] + lz[None, :])
    return tuple(np.asarray(a, np.float32) for a in (txy, np.ascontiguousarray(txy.T), tz, scale))


def after_kernel(
    place, got, txy, txy_t, tz, scale, f1_own, f1_lo, f1_hi, u2, f,
    potential, totals, g, w, r, f3, e, e2, a1, b1, f1, ext, s1,
):
    dom, grp = place[0], place[1]
    zero2 = jnp.zeros((Y2, NZ2), F32)
    for p in range(PAD2):
        g[p] = zero2
        g[PAD2 + NX2 + p] = zero2
        w[p] = zero2
        w[PAD2 + NX2 + p] = zero2
        r[p] = zero2
        r[PAD2 + NX2 + p] = zero2
    slot = lanes_of((8, LANES)) // 32

    def gather(d, c):
        for i in range(2):
            for yb in range(2):
                s = 2 * i + yb
                for t in range(2):
                    row = None
                    for q in range(4):
                        piece = got[d * NGRP + 4 * t + q]
                        shift = (32 * (q - s)) % 128
                        piece = pltpu.roll(piece, shift, 1) if shift else piece
                        row = piece if row is None else jnp.where(slot == q, piece, row)
                    g[PAD2 + 2 * d + i, yb * 8 : yb * 8 + 8, t * LANES : (t + 1) * LANES] = row
        return c

    lax.fori_loop(0, NDOM, gather, 0)
    lane2 = lanes_of((1, NZ2))
    not_first = (lane2 > 0).astype(F32)
    not_last = (lane2 < NZ2 - 1).astype(F32)

    def beside2(ref, p):
        c = ref[p]
        around = (
            ref[p + 1]
            + ref[p - 1]
            + (pltpu.roll(c, 1, 0) + pltpu.roll(c, Y2 - 1, 0))
            + (pltpu.roll(c, 1, 1) * not_first + pltpu.roll(c, NZ2 - 1, 1) * not_last)
        )
        return c, around

    def start2(p, c):
        w[PAD2 + p] = g[PAD2 + p] * (16.0 / 9.0)
        return c

    lax.fori_loop(0, NX2, start2, 0)

    def sweep2(p, c):
        centre, around = beside2(w, PAD2 + p)
        r[PAD2 + p] = (3.0 * centre + around + 16.0 * g[PAD2 + p]) * (1.0 / 9.0)
        return c

    lax.fori_loop(0, NX2, sweep2, 0)

    def residue2(q, c):
        total = None
        for i in range(2):
            p = PAD2 + 2 * q + i
            centre, around = beside2(r, p)
            res = g[p] - (6.0 * centre - around) * (1.0 / 16.0)
            total = res if total is None else total + res
        f3[pl.ds(pl.multiple_of(q * Y2, Y2), Y2), :] = total
        return c

    lax.fori_loop(0, NX3, residue2, 0)
    z_sums = dot(f3[...], lane_halves(NZ3))
    n3 = NX3 * NY3
    ri = lax.broadcasted_iota(I32, (n3, 2 * n3), 0)
    ci = lax.broadcasted_iota(I32, (n3, 2 * n3), 1)
    source = dot(((ci // 2) == ri).astype(F32) * 0.125, z_sums)
    modes = dot(dot(txy_t[...], source), tz[...]) * scale[...]
    solved = dot(txy[...], dot(modes, tz[...]))
    rr = lax.broadcasted_iota(I32, (NZ3, NZ2), 0)
    cc = lax.broadcasted_iota(I32, (NZ3, NZ2), 1)
    wide = dot(solved, ((cc // 2) == rr).astype(F32))
    tall = dot(((lax.broadcasted_iota(I32, (2 * n3, n3), 0) // 2) == lax.broadcasted_iota(I32, (2 * n3, n3), 1)).astype(F32), wide)
    f3[...] = tall

    def add_coarse(q, c):
        for i in range(2):
            p = PAD2 + 2 * q + i
            r[p] = r[p] + f3[pl.ds(pl.multiple_of(q * Y2, Y2), Y2), :]
        return c

    lax.fori_loop(0, NX3, add_coarse, 0)
    first2 = 2 * dom

    def post2(src, dst, n, skip):
        for p in range(n):
            q = first2 + skip + p
            centre, around = beside2(src, q)
            new = (3.0 * centre + around + 16.0 * g[q]) * (1.0 / 9.0)
            dst[q] = new * x_ok(q - PAD2, NX2)

    post2(r, w, 8, 1)
    post2(w, r, 6, 2)
    lane = lanes_of((NZ2, LANES))
    signed = jnp.where(lane < 96, lane, lane - LANES)
    place_z = ((grp * Z1 + signed + 2 * NZ2) // 2 - NZ2 == rows_of((NZ2, LANES))).astype(F32)
    double_y = doubles(Y2)
    f1[0:3] = f1_lo[...]
    f1[3:11] = f1_own[...]
    f1[11:14] = f1_hi[...]
    mask1 = z_mask(LANES, Z1, grp, NGRP * Z1)

    def ok1(p):
        return mask1 * x_ok(dom * X1 + p - 5, NDOM * X1)

    for p in range(14):
        b1[p] = f1[p] * (4.0 / 9.0)
    fine = []
    for p in range(6):
        level2 = dot(r[first2 + 2 + p], place_z)
        fine.append(dot(double_y, level2))
    for p in range(1, 13):
        centre, around = beside(b1, p)
        new = (3.0 * centre + around + 4.0 * f1[p]) * (1.0 / 9.0)
        a1[p] = new * ok1(p) + fine[(p - 1) // 2] * mask1
    for p in range(2, 12):
        centre, around = beside(a1, p)
        b1[p] = (3.0 * centre + around + 4.0 * f1[p]) * (1.0 / 9.0) * ok1(p)
    for p in range(3, 11):
        centre, around = beside(b1, p)
        s1[(p - 3) * Y1 : (p - 2) * Y1, :] = (
            (3.0 * centre + around + 4.0 * f1[p]) * (1.0 / 9.0) * ok1(p)
        )
    r0 = lax.broadcasted_iota(I32, (LANES, W0), 0)
    c0 = lax.broadcasted_iota(I32, (LANES, W0), 1)
    spread0 = dot(s1[...], ((c0 // 2) == r0).astype(F32))
    double_y0 = doubles(Y1)
    for q in range(8):
        ext[q] = dot(double_y0, spread0[q * Y1 : (q + 1) * Y1, :])
    mask = z_mask(W0, CZ, grp, NGRP * CZ)

    def add_fine(p, c):
        e[p] = u2[p + 2] + ext[(p + 1) // 2] * mask
        return c

    lax.fori_loop(0, 14, add_fine, 0)

    def last1(p, c):
        centre, around = beside(e, p + 1)
        new = (3.0 * centre + around + f[p + 4]) * (1.0 / 9.0)
        e2[p] = new * (mask * x_ok(dom * CX + p - 2, NDOM * CX))
        return c

    lax.fori_loop(0, 12, last1, 0)

    def last2(p, c):
        centre, around = beside(e2, p + 1)
        new = (3.0 * centre + around + f[p + 5]) * (1.0 / 9.0)
        e[p] = new * (mask * x_ok(dom * CX + p - 1, NDOM * CX))
        return c

    lax.fori_loop(0, 10, last2, 0)

    def sums(x, carry):
        p = x + 1
        c = e[p]
        own = c[:, 0:LANES]
        potential[x] = own
        gx = 0.5 * (e[p + 1, :, 0:LANES] - e[p - 1, :, 0:LANES])
        gy = 0.5 * (pltpu.roll(own, CY - 1, 0) - pltpu.roll(own, 1, 0))
        gz = 0.5 * (pltpu.roll(c, W0 - 1, 1) - pltpu.roll(c, 1, 1))[:, 0:LANES]
        density = f[x + 6, :, 0:LANES]
        new = (gx * gx, gy * gy, gz * gz, gy * gz, gx * gz, gx * gy, own * density)
        return tuple(
            s + jnp.sum(v.reshape(8, 8, LANES), axis=0) for s, v in zip(carry, new)
        )

    zero = jnp.zeros((8, LANES), F32)
    parts = lax.fori_loop(0, CX, sums, (zero,) * 7)
    lane8 = lanes_of((1, LANES))
    line = jnp.zeros((1, LANES), F32)
    for i, part in enumerate(parts):
        line = jnp.where(lane8 == i, jnp.sum(part), line)
    totals[...] = jnp.broadcast_to(line, (NDEV, LANES))


def after(place, got, f1_own, f1_lo, f1_hi, u2, f):
    consts = [jnp.asarray(t) for t in tables()]
    return pl.pallas_call(
        after_kernel,
        out_shape=(sds(CX, CY, CZ), sds(NDEV, LANES)),
        in_specs=[SM] + [VM] * 10,
        out_specs=(VM, VM),
        scratch_shapes=[
            pltpu.VMEM((NX2 + 2 * PAD2, Y2, NZ2), F32),
            pltpu.VMEM((NX2 + 2 * PAD2, Y2, NZ2), F32),
            pltpu.VMEM((NX2 + 2 * PAD2, Y2, NZ2), F32),
            pltpu.VMEM((NX3 * Y2, NZ2), F32),
            pltpu.VMEM((14, CY, W0), F32),
            pltpu.VMEM((12, CY, W0), F32),
            pltpu.VMEM((14, Y1, LANES), F32),
            pltpu.VMEM((14, Y1, LANES), F32),
            pltpu.VMEM((14, Y1, LANES), F32),
            pltpu.VMEM((8, CY, W0), F32),
            pltpu.VMEM((8 * Y1, LANES), F32),
        ],
        input_output_aliases={},
        compiler_params=PAR,
        name="after",
    )(place, got, *consts, f1_own, f1_lo, f1_hi, u2, f)


def stress_kernel(got, out):
    total = jnp.sum(got[...], axis=0, keepdims=True)
    lane = lanes_of((1, LANES))
    energy = jnp.sum(jnp.where(lane == 6, total, 0.0))
    cells = float(NDOM * CX * CY * NGRP * CZ)
    out[...] = total / cells - jnp.where(lane < 3, 0.5 * energy / cells, 0.0)


def stress_of(got):
    return pl.pallas_call(
        stress_kernel,
        out_shape=sds(1, LANES),
        in_specs=[VM],
        out_specs=VM,
        name="stress",
    )(got)


def shift(value, axis, distance):
    n = lax.axis_size(axis)
    route = [(i, i + distance) for i in range(n) if 0 <= i + distance < n]
    return lax.ppermute(value, axis, route)


def shards(valence, start, tiles, home, ox, oy, oz, size):
    place = jnp.stack([lax.axis_index(DOM), lax.axis_index(GRP)]).astype(I32)
    scal = jnp.concatenate([v.reshape(-1) for v in (home, ox, oy, oz, size)])
    message = pack_atoms(scal, tiles)
    got = lax.all_to_all(message, ALL, 0, 0, tiled=True)
    lower = shift(jnp.concatenate([start[CX - HU :], valence[CX - HF :]]), DOM, 1)
    upper = shift(jnp.concatenate([start[:HU], valence[:HF]]), DOM, -1)
    grid, up2, down = deposit(got)
    from1 = shift(grid[2 * CY : 15 * CY].reshape(13, CY, LANES), DOM, 1)
    from2 = shift(up2.reshape(5, CY, LANES), DOM, 2)
    above = shift(down.reshape(6, CY, LANES), DOM, -1)
    f, u, left, right = join(
        grid, from1, from2, above, valence, lower[HU:], upper[HU:], start, lower[:HU], upper[:HU]
    )
    from_right = shift(left, GRP, -1)
    from_left = shift(right, GRP, 1)
    u2, fe, f1, chunk = before(place, f, u, from_left, from_right)
    everything = lax.all_to_all(chunk, ALL, 0, 0, tiled=True)
    f1_lo = shift(f1[1:4], DOM, 1)
    f1_hi = shift(f1[4:7], DOM, -1)
    potential, totals = after(place, everything, f1, f1_lo, f1_hi, u2, fe)
    sums = lax.all_to_all(totals, ALL, 0, 0, tiled=True)
    return potential, stress_of(sums)[0, :6]


def solution(mesh):
    split = Mesh(mesh.devices.reshape(4, 4, 4, 2), ("dom_0", "dom_1", "grp_0", "grp_1"))
    atoms = P(DOM + GRP, None)
    return jax.shard_map(
        shards,
        mesh=split,
        in_specs=(P(DOM, None, GRP), P(DOM, None, GRP)) + (atoms,) * 6,
        out_specs=(P(DOM, None, GRP), P()),
        check_vma=False,
    )
```

time: 2180 us -> 155 us (0.07)
  other arithmetic: 1800 us -> 0.14 us
  starting transfers between devices: 217 us -> 44 us
  local copies, waits for them, and re-layouts: 87.2 us -> 12 us
  Pallas kernels: 0 us -> 47.8 us
  blocking collectives: 39.9 us -> 16.1 us
    unnamed x4 -> x1, other arithmetic: 1790 us -> 0.01 us
    ppermute x57 -> x9, starting transfers between devices: 174 us -> 23.7 us  [shift(): return lax.ppermute(value, axis, route)]
    pallas_call x0 -> x6, Pallas kernels: none -> 47.8 us  [the longest x1 16.5 us: deposit(): pl.pallas_call(deposit_kernel, out_shape=(sds(16 * CY, LANES), sds(5 * CY...]
    psum x4 -> x0, blocking collectives: 39.9 us -> none  [by_axis(): return functools.reduce(lax.psum, axes, value)]
    reshape x5 -> x0, local copies, waits for them, and re-layouts: 34.5 us -> none  [the longest x2 20.2 us: restrict(): residue.reshape(dims_now[0] // 2, 2, dims_now[1] // 2, 2, dims_now[2] //...]
    all_to_all x4 -> x2, starting transfers between devices: 43.1 us -> 20.4 us  [the longest x1 11.5 us: shards(): got = lax.all_to_all(message, ALL, 0, 0, tiled=True)]
  transfers between devices with their start and end apart: 61 -> 11, of which waited for: 16 -> 6; matrix products, arithmetic and copies ran while one was open for 84% -> 0% of each run, Pallas kernels for 0% -> 11%
where the time goes in v1:
time: 155 us; the launch traced here: 154 us
  Pallas kernels  47.8 us (31%)
  starting transfers between devices  44 us (28%)
  waiting for transfers between devices  33.2 us (21%)
  blocking collectives  16.1 us (10%)
  local copies, waits for them, and re-layouts  12 us (8%)
    ppermute x9, starting transfers between devices, shift(): return lax.ppermute(value, axis, route)  23.7 us
    pallas_call x1, Pallas kernels, deposit(): pl.pallas_call(deposit_kernel, out_shape=(sds(16 * CY, LANES), sds(5 * CY...  16.5 us
    pallas_call x1, Pallas kernels, after(): pl.pallas_call(after_kernel, out_shape=(sds(CX, CY, CZ), sds(NDEV, LANES)...  16.2 us
    all_to_all x1, blocking collectives, shards(): sums = lax.all_to_all(totals, ALL, 0, 0, tiled=True)  16.1 us
    all_to_all x1, waiting for transfers between devices, shards(): got = lax.all_to_all(message, ALL, 0, 0, tiled=True)  15.1 us
    ppermute x9, waiting for transfers between devices, shift(): return lax.ppermute(value, axis, route)  13.3 us
    all_to_all x1, starting transfers between devices, shards(): got = lax.all_to_all(message, ALL, 0, 0, tiled=True)  11.5 us
    pallas_call x1, Pallas kernels, before(): pl.pallas_call(before_kernel, out_shape=(sds(NF - 2, CY, W0), sds(NF, CY,...  9.68 us
  transfers between devices with their start and end apart: 11, of which 6 were waited for; matrix products, arithmetic and copies ran while one was open for 0% of the time, Pallas kernels for 11%

profile of v1, /device:TPU:1, one launch (start us, length us, event | category | flops | bytes accessed | tf_op | source)
XLA Modules:
  0.0 154.2 jit_solution(12391443340879347110)
XLA Ops:
  1.3 0.7 constant_dynamic-update-slice_fusion.3
  2.0 0.7 constant_dynamic-update-slice_fusion.2
  4.1 1.0 copy-done.6
  5.1 3.2 %pack_atoms.1 = f32[128,2176]{1,0:T(8,128)S(1)} custom-call(s32[1280]{0:T(1024)S(1)} %constant_dynamic-update-slice_fusion.scal, f32[256,512]{1,0:T(8,128)S(1)} %copy-done.6), custom_call_target="tpu_custom_call" | custom-call | tf_op jit(solution)/shard_map/pack_atoms/pallas_call | solution.py:91
  8.3 2.2 %copy.14 = f32[128,1,2176]{2,1,0:T(1,128)} copy(f32[128,1,2176]{2,0,1:T(8,128)S(1)} %bitcast.21) | data formatting | bytes 2228224 | tf_op jit(solution)/shard_map/all_to_all | solution.py:684
  10.5 11.5 %all-to-all-start = ((f32[128,1,2176]{2,1,0:T(1,128)}), f32[128,1,2176]{2,1,0:T(1,128)S(1)}, u32[]{:S(2)}, u32[]{:S(2)}) async-start(f32[128,1,2176]{2,1,0:T(1,128)} %copy.14), calls=%async_computation | async-start | bytes 2228224 | tf_op jit(solution)/shard_map/all_to_all | solution.py:684
  22.1 3.3 %collective-permute-start.3 = (f32[13,64,128]{2,1,0:T(8,128)S(1)}, f32[13,64,128]{2,1,0:T(8,128)S(1)}, u32[]{:S(2)}, u32[]{:S(2)}) collective-permute-start(f32[13,64,128]{2,1,0:T(8,128)S(1)} %pad_maximum_fusion), channel_id=1, source_target_pairs={{0,8},{8,16},{16,24},{24,32},{32,40},{40,48},{48,56},{56,64},{64,7... | collective-permute-start | bytes 1277960 | tf_op jit(solution)/shard_map/ppermute | solution.py:677
  25.5 1.3 collective-permute-start.4
  26.8 15.1 %all-to-all-done = f32[128,1,2176]{2,1,0:T(1,128)S(1)} async-done(((f32[128,1,2176]{2,1,0:T(1,128)}), f32[128,1,2176]{2,1,0:T(1,128)S(1)}, u32[]{:S(2)}, u32[]{:S(2)}) %all-to-all-start) | async-done | bytes 1114144 | tf_op jit(solution)/shard_map/all_to_all | solution.py:684
  41.9 16.5 %deposit.1 = (f32[1024,128]{1,0:T(8,128)S(1)}, f32[320,128]{1,0:T(8,128)S(1)}, f32[384,128]{1,0:T(8,128)S(1)}) custom-call(f32[128,2176]{1,0:T(8,128)S(1)} %bitcast.20), custom_call_target="tpu_custom_call" | custom-call | tf_op jit(solution)/shard_map/deposit/pallas_call | solution.py:187
  58.5 2.1 %collective-permute-start = (f32[13,64,128]{2,1,0:T(8,128)S(1)}, f32[13,64,128]{2,1,0:T(8,128)S(1)}, u32[]{:S(2)}, u32[]{:S(2)}) collective-permute-start(f32[13,64,128]{2,1,0:T(8,128)S(1)} %bitcast.25), channel_id=1, source_target_pairs={{0,8},{8,16},{16,24},{24,32},{32,40},{40,48},{48,56},{56,64},{64,7... | collective-permute-start | bytes 1277960 | tf_op jit(solution)/shard_map/ppermute | solution.py:677
  60.6 1.3 collective-permute-start.2
  61.9 4.5 %collective-permute-start.1 = (f32[5,64,128]{2,1,0:T(8,128)S(1)}, f32[5,64,128]{2,1,0:T(8,128)S(1)}, u32[]{:S(2)}, u32[]{:S(2)}) collective-permute-start(f32[5,64,128]{2,1,0:T(8,128)S(1)} %bitcast.24), channel_id=1, source_target_pairs={{0,16},{8,24},{16,32},{24,40},{32,48},{40,56},{48,64},{56,72},{64,... | collective-permute-start | bytes 491528 | tf_op jit(solution)/shard_map/ppermute | solution.py:677
  66.5 4.9 %collective-permute-done.1.from2 = f32[5,64,128]{2,1,0:T(8,128)S(1)} collective-permute-done((f32[5,64,128]{2,1,0:T(8,128)S(1)}, f32[5,64,128]{2,1,0:T(8,128)S(1)}, u32[]{:S(2)}, u32[]{:S(2)}) %collective-permute-start.1) | collective-permute-done | bytes 163872 | tf_op jit(solution)/shard_map/ppermute | solution.py:677
  71.4 0.7 join.1
  72.2 0.9 copy-done.2
  73.0 0.9 copy-done.4
  73.9 4.0 %collective-permute-start.5 = (f32[6,64,128]{2,1,0:T(8,128)S(1)}, f32[6,64,128]{2,1,0:T(8,128)S(1)}, u32[]{:S(2)}, u32[]{:S(2)}) collective-permute-start(f32[6,64,128]{2,1,0:T(8,128)S(1)} %get-tuple-element.20), channel_id=1, source_target_pairs={{0,1},{1,2},{2,3},{3,4},{4,5},{5,6},{6,7},{8,9},{9,10},{10,11},{11... | collective-permute-start | bytes 589832 | tf_op jit(solution)/shard_map/ppermute | solution.py:677
  77.9 1.9 %collective-permute-start.6 = (f32[6,64,128]{2,1,0:T(8,128)S(1)}, f32[6,64,128]{2,1,0:T(8,128)S(1)}, u32[]{:S(2)}, u32[]{:S(2)}) collective-permute-start(f32[6,64,128]{2,1,0:T(8,128)S(1)} %get-tuple-element.21), channel_id=1, source_target_pairs={{1,0},{2,1},{3,2},{4,3},{5,4},{6,5},{7,6},{9,8},{10,9},{11,10},{12... | collective-permute-start | bytes 589832 | tf_op jit(solution)/shard_map/ppermute | solution.py:677
  80.5 4.4 %collective-permute-done.6.from_right = f32[6,64,128]{2,1,0:T(8,128)S(1)} collective-permute-done((f32[6,64,128]{2,1,0:T(8,128)S(1)}, f32[6,64,128]{2,1,0:T(8,128)S(1)}, u32[]{:S(2)}, u32[]{:S(2)}) %collective-permute-start.6) | collective-permute-done | bytes 196640 | tf_op jit(solution)/shard_map/ppermute | solution.py:677
  84.9 1.1 copy-done.3
  86.0 1.1 copy-done.5
  87.1 9.7 %before.1 = (f32[18,64,256]{2,1,0:T(8,128)S(1)}, f32[20,64,256]{2,1,0:T(8,128)S(1)}, f32[8,32,128]{2,1,0:T(8,128)S(1)}, f32[128,8,128]{2,1,0:T(8,128)}) custom-call(s32[2]{0:T(128)S(1)} %pad_add_fusion.place, f32[20,64,128]{2,1,0:T(8,128)S(1)} %copy-done.5, f32[22,64,128]{2,1,0:T(8,128)S(1)} %copy-done.3, ...), custom_call_target="tpu_custom_call" | custom-call | tf_op jit(solution)/shard_map/before/pallas_call | solution.py:393
  96.8 8.9 %all-to-all-start.1 = ((f32[128,8,128]{2,1,0:T(8,128)}), f32[128,8,128]{2,1,0:T(8,128)S(1)}, u32[]{:S(2)}, u32[]{:S(2)}) async-start(f32[128,8,128]{2,1,0:T(8,128)} %get-tuple-element.22), calls=%async_computation.1 | async-start | bytes 1048576 | tf_op jit(solution)/shard_map/all_to_all | solution.py:697
  105.7 1.3 collective-permute-start.8
  107.0 4.0 %collective-permute-start.7 = (f32[3,32,128]{2,1,0:T(8,128)S(1)}, f32[3,32,128]{2,1,0:T(8,128)S(1)}, u32[]{:S(2)}, u32[]{:S(2)}) collective-permute-start(f32[3,32,128]{2,1,0:T(8,128)S(1)} %get-tuple-element.33), channel_id=1, source_target_pairs={{0,8},{8,16},{16,24},{24,32},{32,40},{40,48},{48,56},{56,64},{64,7... | collective-permute-start | bytes 147464 | tf_op jit(solution)/shard_map/ppermute | solution.py:677
  111.0 3.4 %collective-permute-done.8.f1_hi = f32[3,32,128]{2,1,0:T(8,128)S(1)} collective-permute-done((f32[3,32,128]{2,1,0:T(8,128)S(1)}, f32[3,32,128]{2,1,0:T(8,128)S(1)}, u32[]{:S(2)}, u32[]{:S(2)}) %collective-permute-start.8) | collective-permute-done | bytes 49184 | tf_op jit(solution)/shard_map/ppermute | solution.py:677
  114.4 4.8 %all-to-all-done.1.got = f32[128,8,128]{2,1,0:T(8,128)S(1)} async-done(((f32[128,8,128]{2,1,0:T(8,128)}), f32[128,8,128]{2,1,0:T(8,128)S(1)}, u32[]{:S(2)}, u32[]{:S(2)}) %all-to-all-start.1) | async-done | bytes 524320 | tf_op jit(solution)/shard_map/all_to_all | solution.py:697
  119.2 16.2 %after.1 = (f32[8,64,128]{2,1,0:T(8,128)}, f32[128,128]{1,0:T(8,128)S(1)}) custom-call(s32[2]{0:T(128)S(1)} %pad_add_fusion.place, f32[128,8,128]{2,1,0:T(8,128)S(1)} %all-to-all-done.1.got, f32[128,128]{1,0:T(8,128)S(1)} %copy-done.10, f32[128,128]{1,0:T(8,128)S(1)} %copy-done.9, f32[128,128]{1,0:T(8,128)S(1)} %copy-done.8, f32[128,128]{1,0:T(8,128)S(1)} %copy-done.7, ...), custom_call_target="tpu_custom_call" | custom-call | tf_op jit(solution)/shard_map/after/pallas_call | solution.py:632
  135.4 16.1 %all_to_all.27 = f32[128,1,128]{2,1,0:T(1,128)} all-to-all(f32[128,1,128]{2,1,0:T(1,128)S(1)} %bitcast.22), channel_id=1, replica_groups=mesh['dom_0'=4,'dom_1'=4,'grp_0'=4,'grp_1'=2] {'dom_0','dom_1','grp_0','..., dimensions={0} | all-to-all | bytes 131072 | tf_op jit(solution)/shard_map/all_to_all | solution.py:701
  151.5 1.5 stress.1
  153.0 1.1 slice_bitcast_fusion
  (39 shorter events, 3.0 us)
Async XLA Ops:
  4.1 1.0 copy-start.6
  10.5 11.5 %copy-start.1 = (f32[8,64,128]{2,1,0:T(8,128)S(1)}, f32[8,64,128]{2,1,0:T(8,128)}, u32[]{:S(2)}) copy-start(f32[8,64,128]{2,1,0:T(8,128)} %valence.1) | copy-start | bytes 786436
  10.5 11.5 %copy-start = (f32[8,64,128]{2,1,0:T(8,128)S(1)}, f32[8,64,128]{2,1,0:T(8,128)}, u32[]{:S(2)}) copy-start(f32[8,64,128]{2,1,0:T(8,128)} %start.1) | copy-start | bytes 786436
  10.5 31.4 %all-to-all-start = ((f32[128,1,2176]{2,1,0:T(1,128)}), f32[128,1,2176]{2,1,0:T(1,128)S(1)}, u32[]{:S(2)}, u32[]{:S(2)}) async-start(f32[128,1,2176]{2,1,0:T(1,128)} %copy.14), calls=%async_computation | async-start | bytes 2228224 | tf_op jit(solution)/shard_map/all_to_all | solution.py:684
  22.1 44.3 %collective-permute-start.3 = (f32[13,64,128]{2,1,0:T(8,128)S(1)}, f32[13,64,128]{2,1,0:T(8,128)S(1)}, u32[]{:S(2)}, u32[]{:S(2)}) collective-permute-start(f32[13,64,128]{2,1,0:T(8,128)S(1)} %pad_maximum_fusion), channel_id=1, source_target_pairs={{0,8},{8,16},{16,24},{24,32},{32,40},{40,48},{48,56},{56,64},{64,7... | collective-permute-start | bytes 1277960 | tf_op jit(solution)/shard_map/ppermute | solution.py:677
  25.5 41.0 %collective-permute-start.4 = (f32[13,64,128]{2,1,0:T(8,128)S(1)}, f32[13,64,128]{2,1,0:T(8,128)S(1)}, u32[]{:S(2)}, u32[]{:S(2)}) collective-permute-start(f32[13,64,128]{2,1,0:T(8,128)S(1)} %pad_maximum_fusion.1), channel_id=1, source_target_pairs={{8,0},{16,8},{24,16},{32,24},{40,32},{48,40},{56,48},{64,56},{72,6... | collective-permute-start | bytes 1277960 | tf_op jit(solution)/shard_map/ppermute | solution.py:677
  58.5 13.0 %collective-permute-start = (f32[13,64,128]{2,1,0:T(8,128)S(1)}, f32[13,64,128]{2,1,0:T(8,128)S(1)}, u32[]{:S(2)}, u32[]{:S(2)}) collective-permute-start(f32[13,64,128]{2,1,0:T(8,128)S(1)} %bitcast.25), channel_id=1, source_target_pairs={{0,8},{8,16},{16,24},{24,32},{32,40},{40,48},{48,56},{56,64},{64,7... | collective-permute-start | bytes 1277960 | tf_op jit(solution)/shard_map/ppermute | solution.py:677
  60.6 10.8 %collective-permute-start.2 = (f32[6,64,128]{2,1,0:T(8,128)S(1)}, f32[6,64,128]{2,1,0:T(8,128)S(1)}, u32[]{:S(2)}, u32[]{:S(2)}) collective-permute-start(f32[6,64,128]{2,1,0:T(8,128)S(1)} %bitcast.23), channel_id=1, source_target_pairs={{8,0},{16,8},{24,16},{32,24},{40,32},{48,40},{56,48},{64,56},{72,6... | collective-permute-start | bytes 589832 | tf_op jit(solution)/shard_map/ppermute | solution.py:677
  61.9 9.5 %collective-permute-start.1 = (f32[5,64,128]{2,1,0:T(8,128)S(1)}, f32[5,64,128]{2,1,0:T(8,128)S(1)}, u32[]{:S(2)}, u32[]{:S(2)}) collective-permute-start(f32[5,64,128]{2,1,0:T(8,128)S(1)} %bitcast.24), channel_id=1, source_target_pairs={{0,16},{8,24},{16,32},{24,40},{32,48},{40,56},{48,64},{56,72},{64,... | collective-permute-start | bytes 491528 | tf_op jit(solution)/shard_map/ppermute | solution.py:677
  72.1 0.9 copy-start.2
  73.0 0.9 copy-start.4
  73.9 6.6 %collective-permute-start.5 = (f32[6,64,128]{2,1,0:T(8,128)S(1)}, f32[6,64,128]{2,1,0:T(8,128)S(1)}, u32[]{:S(2)}, u32[]{:S(2)}) collective-permute-start(f32[6,64,128]{2,1,0:T(8,128)S(1)} %get-tuple-element.20), channel_id=1, source_target_pairs={{0,1},{1,2},{2,3},{3,4},{4,5},{5,6},{6,7},{8,9},{9,10},{10,11},{11... | collective-permute-start | bytes 589832 | tf_op jit(solution)/shard_map/ppermute | solution.py:677
  77.9 7.0 %collective-permute-start.6 = (f32[6,64,128]{2,1,0:T(8,128)S(1)}, f32[6,64,128]{2,1,0:T(8,128)S(1)}, u32[]{:S(2)}, u32[]{:S(2)}) collective-permute-start(f32[6,64,128]{2,1,0:T(8,128)S(1)} %get-tuple-element.21), channel_id=1, source_target_pairs={{1,0},{2,1},{3,2},{4,3},{5,4},{6,5},{7,6},{9,8},{10,9},{11,10},{12... | collective-permute-start | bytes 589832 | tf_op jit(solution)/shard_map/ppermute | solution.py:677
  84.9 1.1 copy-start.3
  86.0 1.1 copy-start.5
  87.1 32.1 %copy-start.7 = (f32[128,128]{1,0:T(8,128)S(1)}, f32[128,128]{1,0:T(8,128)}, u32[]{:S(2)}) copy-start(f32[128,128]{1,0:T(8,128)} %constant.30.clone.scale) | copy-start | bytes 196612
  87.1 32.1 %copy-start.8 = (f32[128,128]{1,0:T(8,128)S(1)}, f32[128,128]{1,0:T(8,128)}, u32[]{:S(2)}) copy-start(f32[128,128]{1,0:T(8,128)} %constant.29.clone.tz) | copy-start | bytes 196612
  87.1 32.1 %copy-start.9 = (f32[128,128]{1,0:T(8,128)S(1)}, f32[128,128]{1,0:T(8,128)}, u32[]{:S(2)}) copy-start(f32[128,128]{1,0:T(8,128)} %constant.28.clone.txy_t) | copy-start | bytes 196612
  87.1 32.1 %copy-start.10 = (f32[128,128]{1,0:T(8,128)S(1)}, f32[128,128]{1,0:T(8,128)}, u32[]{:S(2)}) copy-start(f32[128,128]{1,0:T(8,128)} %constant.27.clone.txy) | copy-start | bytes 196612
  96.8 22.4 %all-to-all-start.1 = ((f32[128,8,128]{2,1,0:T(8,128)}), f32[128,8,128]{2,1,0:T(8,128)S(1)}, u32[]{:S(2)}, u32[]{:S(2)}) async-start(f32[128,8,128]{2,1,0:T(8,128)} %get-tuple-element.22), calls=%async_computation.1 | async-start | bytes 1048576 | tf_op jit(solution)/shard_map/all_to_all | solution.py:697
  105.7 8.7 %collective-permute-start.8 = (f32[3,32,128]{2,1,0:T(8,128)S(1)}, f32[3,32,128]{2,1,0:T(8,128)S(1)}, u32[]{:S(2)}, u32[]{:S(2)}) collective-permute-start(f32[3,32,128]{2,1,0:T(8,128)S(1)} %get-tuple-element.32), channel_id=1, source_target_pairs={{8,0},{16,8},{24,16},{32,24},{40,32},{48,40},{56,48},{64,56},{72,6... | collective-permute-start | bytes 147464 | tf_op jit(solution)/shard_map/ppermute | solution.py:677
  107.0 7.4 %collective-permute-start.7 = (f32[3,32,128]{2,1,0:T(8,128)S(1)}, f32[3,32,128]{2,1,0:T(8,128)S(1)}, u32[]{:S(2)}, u32[]{:S(2)}) collective-permute-start(f32[3,32,128]{2,1,0:T(8,128)S(1)} %get-tuple-element.33), channel_id=1, source_target_pairs={{0,8},{8,16},{16,24},{24,32},{32,40},{40,48},{48,56},{56,64},{64,7... | collective-permute-start | bytes 147464 | tf_op jit(solution)/shard_map/ppermute | solution.py:677

commit v2 on v1

v2 whole, which is shorter than its diff:
```python
import functools

import jax
import jax.numpy as jnp
import numpy as np
from jax import lax
from jax.experimental import pallas as pl
from jax.experimental.pallas import tpu as pltpu
from jax.sharding import Mesh
from jax.sharding import PartitionSpec as P


CAP = 4
DOM = ("dom_0", "dom_1")
GRP = ("grp_0", "grp_1")
ALL = DOM + GRP
F32 = jnp.float32
I32 = jnp.int32
HI = lax.Precision.HIGHEST
VM = pl.BlockSpec(memory_space=pltpu.VMEM)
SM = pl.BlockSpec(memory_space=pltpu.SMEM)

CX, CY, CZ = 8, 64, 128
NDOM, NGRP = 16, 8
NDEV = NDOM * NGRP
ATOMS = 256
TILE_ROWS = 4
LANES = 128
PAR = pltpu.CompilerParams(vmem_limit_bytes=16 * 1024 * 1024)


def sds(*shape, dtype=F32):
    return jax.ShapeDtypeStruct(shape, dtype)


def lanes_of(shape):
    return lax.broadcasted_iota(I32, shape, len(shape) - 1)


def rows_of(shape):
    return lax.broadcasted_iota(I32, shape, len(shape) - 2)


def dot(a, b):
    return lax.dot_general(
        a, b, (((1,), (0,)), ((), ())), precision=HI, preferred_element_type=F32
    )


def dot_right(a, ones):
    hi = a.astype(jnp.bfloat16)
    lo = (a - hi.astype(F32)).astype(jnp.bfloat16)
    ones = ones.astype(jnp.bfloat16)
    return jnp.dot(hi, ones, preferred_element_type=F32) + jnp.dot(
        lo, ones, preferred_element_type=F32
    )


def dot_left(ones, a):
    hi = a.astype(jnp.bfloat16)
    lo = (a - hi.astype(F32)).astype(jnp.bfloat16)
    ones = ones.astype(jnp.bfloat16)
    return jnp.dot(ones, hi, preferred_element_type=F32) + jnp.dot(
        ones, lo, preferred_element_type=F32
    )


ROWS = CAP * TILE_ROWS + 1


def pack_kernel(
    home_h, ox_h, oy_h, oz_h, size_h, tiles_h, out, rows, count, home, ox, oy, oz, size, tiles, sem
):
    copies = [
        pltpu.make_async_copy(src, dst, sem.at[i])
        for i, (src, dst) in enumerate(
            ((home_h, home), (ox_h, ox), (oy_h, oy), (oz_h, oz), (size_h, size), (tiles_h, tiles))
        )
    ]
    for copy in copies:
        copy.start()

    def clear_out(i, c):
        out[pl.ds(pl.multiple_of(i * 8, 8), 8), :] = jnp.zeros((8, LANES), F32)
        return c

    lax.fori_loop(0, NDEV * ROWS // 8, clear_out, 0, unroll=8)

    def clear(i, c):
        count[i] = 0
        return c

    lax.fori_loop(0, NDEV, clear, 0, unroll=8)
    copies[5].wait()
    lower = lanes_of((8, LANES)) < 64
    for g in range(ATOMS // 8):
        old = [tiles[g * 8 : g * 8 + 8, r * LANES : (r + 1) * LANES] for r in range(4)]
        turned = [pltpu.roll(v, 64, 1) for v in old]
        new = (
            jnp.where(lower, old[0], turned[2]),
            jnp.where(lower, turned[0], old[2]),
            jnp.where(lower, old[1], turned[3]),
            jnp.where(lower, turned[1], old[3]),
        )
        for r in range(TILE_ROWS):
            rows[pl.ds(g * 8 * TILE_ROWS + r, 8, stride=TILE_ROWS), :] = new[r]

    for copy in copies[:5]:
        copy.wait()
    lane = lanes_of((TILE_ROWS, LANES))
    need = rows_of((TILE_ROWS, LANES)) + jnp.where(lane < 64, 0, 4)
    need = jnp.maximum(jnp.maximum(need, (lane // 8) % 8), lane % 8)
    tile_c = lane % 8
    lane1 = lanes_of((1, LANES))

    def several(step, c):
        placed = []
        for i in range(PER_STEP):
            n = step * PER_STEP + i
            z_in, y_in = oz[n] & 7, oy[n] & 15
            value = rows[pl.ds(pl.multiple_of(n * TILE_ROWS, 4), TILE_ROWS), :]
            value = jnp.where(need < size[n], value, 0.0)
            shift = y_in * 8 + z_in
            near = pltpu.roll(value, shift & 127, 1)
            far = pltpu.roll(value, (shift + 120) & 127, 1)
            placed.append(jnp.where(tile_c >= z_in, near, far))
        for i in range(PER_STEP):
            n = step * PER_STEP + i
            to = home[n]
            rank = count[to]
            count[to] = rank + 1
            base = to * ROWS
            out[pl.ds(base + rank * TILE_ROWS, TILE_ROWS), :] = placed[i]
            y_block, z_block = oy[n] >> 4, oz[n] >> 3
            row = (y_block * ZB + z_block) * 16 + ox[n]
            wrapped = (((y_block + 1) & 3) * ZB + z_block) * 16 + ox[n]
            line = jnp.where(lane1 & 3 == 0, row, wrapped)
            line = jnp.where(lane1 & 3 == 2, (oy[n] & 15) * 8, line)
            line = jnp.where(lane1 & 3 == 3, oz[n] & 7, line)
            pltpu.store(
                out.at[pl.ds(base + ROWS - 1, 1), :],
                line.astype(F32),
                mask=(lane1 >> 2) == rank,
            )
        return c

    lax.fori_loop(0, ATOMS // PER_STEP, several, 0)


PER_STEP = 16


def pack_atoms(scalars, tiles):
    return pl.pallas_call(
        pack_kernel,
        out_shape=sds(NDEV * ROWS, LANES),
        in_specs=[pl.BlockSpec(memory_space=pl.ANY)] * 6,
        out_specs=VM,
        scratch_shapes=[
            pltpu.VMEM((ATOMS * TILE_ROWS, LANES), F32),
            pltpu.SMEM((NDEV,), I32),
        ]
        + [pltpu.SMEM((ATOMS,), I32)] * 5
        + [pltpu.VMEM((ATOMS, TILE_ROWS * LANES), F32), pltpu.SemaphoreType.DMA((6,))],
        name="pack_atoms",
    )(*scalars, tiles)


ZB = CZ // 8 + 1
YB = 4


def deposit_kernel(got, valence, grid, up2, down, acc_a, acc_b, other, corner_v, corner_s, sem):
    for g in range(NDEV // 8):
        corner_v[g * 8 : g * 8 + 8, :] = got[
            pl.ds(g * 8 * ROWS + ROWS - 1, 8, stride=ROWS), :
        ].astype(I32)
    copy = pltpu.make_async_copy(corner_v, corner_s, sem)
    copy.start()

    def turn(i, c):
        at = pl.ds(pl.multiple_of(i * 32, 8), 32)
        other[at, :] = pltpu.roll(got[at, :], 64, 1)
        return c

    lax.fori_loop(0, NDEV * ROWS // 32, turn, 0, unroll=4)

    def clear(i, c):
        zero = jnp.zeros((16, LANES), F32)
        acc_a[pl.ds(pl.multiple_of(i * 16, 16), 16), :] = zero
        acc_b[pl.ds(pl.multiple_of(i * 16, 16), 16), :] = zero
        return c

    lax.fori_loop(0, YB * ZB, clear, 0, unroll=4)
    copy.wait()
    lane = lanes_of((8, LANES))
    z_of = lane % 8

    def one(src, c):
        for k in range(CAP):
            acc = acc_a if k % 2 == 0 else acc_b
            row = corner_s[src, 4 * k]
            wrapped = corner_s[src, 4 * k + 1]
            first = corner_s[src, 4 * k + 2]
            z_in = corner_s[src, 4 * k + 3]
            at = pl.ds(src * ROWS + k * TILE_ROWS, TILE_ROWS)
            value = jnp.concatenate([got[at, :], other[at, :]], axis=0)
            same = (lane >= first) & (lane < first + 64)
            here = jnp.where(same, value, 0.0)
            round_ = jnp.where(lane < first - 64, value, 0.0)
            near = z_of >= z_in
            a0 = acc[pl.ds(row, 8), :]
            a1 = acc[pl.ds(row + 16, 8), :]
            a2 = acc[pl.ds(wrapped, 8), :]
            a3 = acc[pl.ds(wrapped + 16, 8), :]
            acc[pl.ds(row, 8), :] = a0 + jnp.where(near, here, 0.0)
            acc[pl.ds(row + 16, 8), :] = a1 + jnp.where(near, 0.0, here)
            acc[pl.ds(wrapped, 8), :] = a2 + jnp.where(near, round_, 0.0)
            acc[pl.ds(wrapped + 16, 8), :] = a3 + jnp.where(near, 0.0, round_)
        return c

    lax.fori_loop(0, NDEV, one, 0)
    group = lane // 8

    def lay_out(yb, c):
        for xg in range(2):
            blocks = []
            for zb in range(CZ // 8):
                at = pl.ds(pl.multiple_of((yb * ZB + zb) * 16 + xg * 8, 8), 8)
                blocks.append(acc_a[at, :] + acc_b[at, :])
            for s in (8, 4, 2, 1):
                low = (group & s) == 0
                for i in range(16):
                    if i & s == 0:
                        one_, two = blocks[i], blocks[i + s]
                        blocks[i] = jnp.where(low, one_, pltpu.roll(two, 8 * s, 1))
                        blocks[i + s] = jnp.where(low, pltpu.roll(one_, 128 - 8 * s, 1), two)
            for yy in range(16):
                grid[pl.ds(xg * 8 * CY + yb * 16 + yy, 8, stride=CY), :] = blocks[yy]
        return c

    lax.fori_loop(0, YB, lay_out, 0)
    grid[0 : CX * CY, :] += valence[...]
    up2[...] = grid[10 * CY : 15 * CY, :]
    down[...] = grid[0 : 6 * CY, :]


def deposit(got, valence):
    return pl.pallas_call(
        deposit_kernel,
        out_shape=(sds(16 * CY, LANES), sds(5 * CY, LANES), sds(6 * CY, LANES)),
        in_specs=[VM, VM],
        out_specs=(VM, VM, VM),
        scratch_shapes=[
            pltpu.VMEM((YB * ZB * 16, LANES), F32),
            pltpu.VMEM((YB * ZB * 16, LANES), F32),
            pltpu.VMEM((NDEV * ROWS, LANES), F32),
            pltpu.VMEM((NDEV, LANES), I32),
            pltpu.SMEM((NDEV, LANES), I32),
            pltpu.SemaphoreType.DMA,
        ],
        compiler_params=PAR,
        name="deposit",
    )(got, valence.reshape(CX * CY, LANES))


HU, HF = 7, 6
NU_, NF = CX + 2 * HU, CX + 2 * HF
UGROUPS, FGROUPS = -(-NU_ // 8), -(-NF // 8)
ZGROUPS = UGROUPS + FGROUPS


def u_plane(p, u_lo, start, u_hi):
    if p < HU:
        return u_lo[p]
    return start[p - HU] if p < HU + CX else u_hi[p - HU - CX]


def pack_edges(planes, left, right, at):
    slot = lanes_of((CY, LANES)) // 16
    for g in range(-(-len(planes) // 8)):
        lo = jnp.zeros((CY, LANES), F32)
        hi = jnp.zeros((CY, LANES), F32)
        for k, plane in enumerate(planes[g * 8 : g * 8 + 8]):
            plane = plane()
            lo = jnp.where(slot == k, pltpu.roll(plane, 16 * k, 1) if k else plane, lo)
            shift_ = (16 * k - 112) % 128
            hi = jnp.where(slot == k, pltpu.roll(plane, shift_, 1) if shift_ else plane, hi)
        left[at + g] = lo
        right[at + g] = hi


def edges_kernel(start, u_lo, u_hi, left, right):
    pack_edges(
        [functools.partial(u_plane, p, u_lo, start, u_hi) for p in range(NU_)], left, right, 0
    )


def edges(start, u_lo, u_hi):
    return pl.pallas_call(
        edges_kernel,
        out_shape=(sds(UGROUPS, CY, LANES),) * 2,
        in_specs=[VM] * 3,
        out_specs=(VM,) * 2,
        compiler_params=PAR,
        name="edges",
    )(start, u_lo, u_hi)


def join_kernel(grid, from1, from2, above, u_left, u_right, f, left, right):
    left[0:UGROUPS] = u_left[...]
    right[0:UGROUPS] = u_right[...]
    for p in range(NF):
        x = p - HF
        if x < 0:
            total = from1[x + 6]
            if x < -1:
                total = total + from2[x + 6]
        elif x < CX:
            total = grid[x * CY : (x + 1) * CY, :]
            if x < 7:
                total = total + from1[x + 6]
        else:
            total = above[x - CX]
            if x < 15:
                total = total + grid[x * CY : (x + 1) * CY, :]
        f[p] = total
    pack_edges([functools.partial(lambda q: f[q], p) for p in range(NF)], left, right, UGROUPS)


def join(*args):
    return pl.pallas_call(
        join_kernel,
        out_shape=(
            sds(NF, CY, LANES),
            sds(ZGROUPS, CY, LANES),
            sds(ZGROUPS, CY, LANES),
        ),
        in_specs=[VM] * 6,
        out_specs=(VM,) * 3,
        compiler_params=PAR,
        name="join",
    )(*args)


W0 = 256
X1, Y1, Z1 = 4, 32, 64
X2, Y2, Z2 = 2, 16, 32


def beside(ref, p):
    c = ref[p]
    n, w = c.shape
    return c, (
        ref[p + 1]
        + ref[p - 1]
        + (pltpu.roll(c, 1, 0) + pltpu.roll(c, n - 1, 0))
        + (pltpu.roll(c, 1, 1) + pltpu.roll(c, w - 1, 1))
    )


def z_mask(width, own, grp, total):
    lane = lanes_of((1, width))
    split = own + (width - own) // 2
    z = grp * own + jnp.where(lane < split, lane, lane - width)
    return ((z >= 0) & (z < total)).astype(F32)


def x_ok(x, total):
    return jnp.where((x >= 0) & (x < total), 1.0, 0.0).astype(F32)


def halves(n):
    r = lax.broadcasted_iota(I32, (n, 2 * n), 0)
    c = lax.broadcasted_iota(I32, (n, 2 * n), 1)
    return ((c // 2) == r).astype(F32)


def doubles(n):
    r = lax.broadcasted_iota(I32, (2 * n, n), 0)
    c = lax.broadcasted_iota(I32, (2 * n, n), 1)
    return ((r // 2) == c).astype(F32)


def lane_halves(n):
    r = lax.broadcasted_iota(I32, (2 * n, n), 0)
    c = lax.broadcasted_iota(I32, (2 * n, n), 1)
    return ((r // 2) == c).astype(F32)


def before_kernel(
    place, f_in, u_lo, start, u_hi, from_left, from_right, u_out, f_out, f1, chunk, u, ua, f, u2, pairs, v1, r1
):
    dom, grp = place[0], place[1]
    lane = lanes_of((CY, LANES))
    for p in range(NU_ + NF):
        g, k = (p // 8, p % 8) if p < NU_ else (UGROUPS + (p - NU_) // 8, (p - NU_) % 8)
        right = from_right[g]
        right = pltpu.roll(right, (-16 * k) % 128, 1) if k else right
        left = from_left[g]
        shift = (112 - 16 * k) % 128
        left = pltpu.roll(left, shift, 1) if shift else left
        edge = jnp.where(lane < 16, right, jnp.where(lane >= 112, left, 0.0))
        if p < NU_:
            u[p, :, 0:LANES] = u_plane(p, u_lo, start, u_hi)
            u[p, :, LANES:] = edge
        else:
            f[p - NU_, :, 0:LANES] = f_in[p - NU_]
            f[p - NU_, :, LANES:] = edge
    mask = z_mask(W0, CZ, grp, NGRP * CZ)

    def sweep1(p, c):
        centre, around = beside(u, p + 1)
        new = (3.0 * centre + around + f[p]) * (1.0 / 9.0)
        ua[p] = new * (mask * x_ok(dom * CX + p - HF, NDOM * CX))
        return c

    lax.fori_loop(0, NF, sweep1, 0, unroll=4)

    def sweep2(p, c):
        centre, around = beside(ua, p + 1)
        new = (3.0 * centre + around + f[p + 1]) * (1.0 / 9.0)
        u2[p] = new * (mask * x_ok(dom * CX + p - 5, NDOM * CX))
        return c

    lax.fori_loop(0, NF - 2, sweep2, 0, unroll=3)

    u_out[...] = u2[2:16]
    f_out[...] = f[4:16]

    def residue0(q, c):
        total = None
        for i in range(2):
            p = 2 * q + i + 1
            centre, around = beside(u2, p)
            r = f[p + 1] - (6.0 * centre - around)
            total = r if total is None else total + r
        pairs[pl.ds(pl.multiple_of(q * CY, CY), CY), :] = total
        return c

    lax.fori_loop(0, 8, residue0, 0, unroll=2)
    summed = dot_right(pairs[...], lane_halves(LANES))
    half_y = halves(Y1) * 0.125
    mask1 = z_mask(LANES, Z1, grp, NGRP * Z1)
    for q in range(8):
        part = dot_left(half_y, summed[q * CY : (q + 1) * CY, :])
        f1[q] = part * (mask1 * x_ok(dom * X1 + q - 2, NDOM * X1))
    for q in range(8):
        v1[q] = f1[q] * (4.0 / 9.0)
    for q in range(1, 7):
        centre, around = beside(v1, q)
        new = (3.0 * centre + around + 4.0 * f1[q]) * (1.0 / 9.0)
        r1[q] = new * (mask1 * x_ok(dom * X1 + q - 2, NDOM * X1))
    half_y2 = halves(Y2) * 0.125
    lane_half = lane_halves(LANES // 2)
    rows = []
    for i in range(2):
        total = None
        for j in range(2):
            q = 2 + 2 * i + j
            centre, around = beside(r1, q)
            r = f1[q] - (6.0 * centre - around) * 0.25
            total = r if total is None else total + r
        rows.append(total)
    both = dot_right(jnp.concatenate(rows, axis=0), jnp.concatenate([lane_half, jnp.zeros_like(lane_half)], axis=1))
    packed = jnp.zeros((8, LANES), F32)
    slot = lanes_of((8, LANES)) // 32
    for i in range(2):
        part = dot_left(half_y2, both[i * Y1 : (i + 1) * Y1, :])
        for yb in range(2):
            s = 2 * i + yb
            piece = part[yb * 8 : yb * 8 + 8, :]
            piece = pltpu.roll(piece, 32 * s, 1) if s else piece
            packed = jnp.where(slot == s, piece, packed)

    def spread(d, c):
        chunk[d] = packed
        return c

    lax.fori_loop(0, NDEV, spread, 0, unroll=8)


def before(place, f, u_lo, start, u_hi, from_left, from_right):
    return pl.pallas_call(
        before_kernel,
        out_shape=(
            sds(14, CY, W0),
            sds(12, CY, W0),
            sds(8, Y1, LANES),
            sds(NDEV, 8, LANES),
        ),
        in_specs=[SM] + [VM] * 6,
        out_specs=(VM,) * 4,
        scratch_shapes=[
            pltpu.VMEM((NU_, CY, W0), F32),
            pltpu.VMEM((NF, CY, W0), F32),
            pltpu.VMEM((NF, CY, W0), F32),
            pltpu.VMEM((NF - 2, CY, W0), F32),
            pltpu.VMEM((8 * CY, W0), F32),
            pltpu.VMEM((8, Y1, LANES), F32),
            pltpu.VMEM((8, Y1, LANES), F32),
        ],
        compiler_params=PAR,
        name="before",
    )(place, f, u_lo, start, u_hi, from_left, from_right)


NX2, NZ2 = NDOM * X2, NGRP * Z2
NX3, NY3, NZ3 = NX2 // 2, Y2 // 2, NZ2 // 2
PAD2 = 4


def tables():
    def sine(n):
        k = np.arange(n) + 1.0
        t = np.sqrt(2.0 / (n + 1)) * np.sin(np.pi * np.outer(k, k) / (n + 1))
        return t, 2.0 - 2.0 * np.cos(np.pi * k / (n + 1))

    def cyclic(n):
        j = np.arange(n)[:, None]
        col = np.arange(n)[None, :]
        freq = (col + 1) // 2
        angle = 2.0 * np.pi * freq * j / n
        use_sine = (col % 2 == 0) & (col > 0)
        edge = (col == 0) | (col == n - 1)
        t = np.where(edge, np.sqrt(1.0 / n), np.sqrt(2.0 / n)) * np.where(
            use_sine, np.sin(angle), np.cos(angle)
        )
        return t, 2.0 - 2.0 * np.cos(2.0 * np.pi * freq[0] / n)

    tx, lx = sine(NX3)
    ty, ly = cyclic(NY3)
    tz, lz = sine(NZ3)
    txy = np.kron(tx, ty)
    lxy = (lx[:, None] + ly[None, :]).reshape(-1)
    scale = 64.0 / (lxy[:, None] + lz[None, :])
    return tuple(np.asarray(a, np.float32) for a in (txy, np.ascontiguousarray(txy.T), tz, scale))


def after_kernel(
    place, got, txy, txy_t, tz, scale, f1_own, f1_lo, f1_hi, u2, f,
    potential, totals, g, w, r, f3, e, e2, a1, b1, f1, ext, s1,
):
    dom, grp = place[0], place[1]
    zero2 = jnp.zeros((Y2, NZ2), F32)
    for p in range(PAD2):
        g[p] = zero2
        g[PAD2 + NX2 + p] = zero2
        w[p] = zero2
        w[PAD2 + NX2 + p] = zero2
        r[p] = zero2
        r[PAD2 + NX2 + p] = zero2
    slot = lanes_of((8, LANES)) // 32

    def gather(d, c):
        for i in range(2):
            for yb in range(2):
                s = 2 * i + yb
                for t in range(2):
                    row = None
                    for q in range(4):
                        piece = got[d * NGRP + 4 * t + q]
                        shift = (32 * (q - s)) % 128
                        piece = pltpu.roll(piece, shift, 1) if shift else piece
                        row = piece if row is None else jnp.where(slot == q, piece, row)
                    g[PAD2 + 2 * d + i, yb * 8 : yb * 8 + 8, t * LANES : (t + 1) * LANES] = row
        return c

    lax.fori_loop(0, NDOM, gather, 0, unroll=4)
    lane2 = lanes_of((1, NZ2))
    not_first = (lane2 > 0).astype(F32)
    not_last = (lane2 < NZ2 - 1).astype(F32)

    def beside2(ref, p):
        c = ref[p]
        around = (
            ref[p + 1]
            + ref[p - 1]
            + (pltpu.roll(c, 1, 0) + pltpu.roll(c, Y2 - 1, 0))
            + (pltpu.roll(c, 1, 1) * not_first + pltpu.roll(c, NZ2 - 1, 1) * not_last)
        )
        return c, around

    def start2(p, c):
        w[PAD2 + p] = g[PAD2 + p] * (16.0 / 9.0)
        return c

    lax.fori_loop(0, NX2, start2, 0, unroll=8)

    def sweep2(p, c):
        centre, around = beside2(w, PAD2 + p)
        r[PAD2 + p] = (3.0 * centre + around + 16.0 * g[PAD2 + p]) * (1.0 / 9.0)
        return c

    lax.fori_loop(0, NX2, sweep2, 0, unroll=8)

    def residue2(q, c):
        total = None
        for i in range(2):
            p = PAD2 + 2 * q + i
            centre, around = beside2(r, p)
            res = g[p] - (6.0 * centre - around) * (1.0 / 16.0)
            total = res if total is None else total + res
        f3[pl.ds(pl.multiple_of(q * Y2, Y2), Y2), :] = total
        return c

    lax.fori_loop(0, NX3, residue2, 0, unroll=4)
    z_sums = dot_right(f3[...], lane_halves(NZ3))
    n3 = NX3 * NY3
    ri = lax.broadcasted_iota(I32, (n3, 2 * n3), 0)
    ci = lax.broadcasted_iota(I32, (n3, 2 * n3), 1)
    source = dot_left(((ci // 2) == ri).astype(F32) * 0.125, z_sums)
    modes = dot(dot(txy_t[...], source), tz[...]) * scale[...]
    solved = dot(txy[...], dot(modes, tz[...]))
    rr = lax.broadcasted_iota(I32, (NZ3, NZ2), 0)
    cc = lax.broadcasted_iota(I32, (NZ3, NZ2), 1)
    wide = dot_right(solved, ((cc // 2) == rr).astype(F32))
    tall = dot_left(((lax.broadcasted_iota(I32, (2 * n3, n3), 0) // 2) == lax.broadcasted_iota(I32, (2 * n3, n3), 1)).astype(F32), wide)
    f3[...] = tall

    def add_coarse(q, c):
        for i in range(2):
            p = PAD2 + 2 * q + i
            r[p] = r[p] + f3[pl.ds(pl.multiple_of(q * Y2, Y2), Y2), :]
        return c

    lax.fori_loop(0, NX3, add_coarse, 0, unroll=4)
    first2 = 2 * dom

    def post2(src, dst, n, skip):
        for p in range(n):
            q = first2 + skip + p
            centre, around = beside2(src, q)
            new = (3.0 * centre + around + 16.0 * g[q]) * (1.0 / 9.0)
            dst[q] = new * x_ok(q - PAD2, NX2)

    post2(r, w, 8, 1)
    post2(w, r, 6, 2)
    lane = lanes_of((NZ2, LANES))
    signed = jnp.where(lane < 96, lane, lane - LANES)
    place_z = ((grp * Z1 + signed + 2 * NZ2) // 2 - NZ2 == rows_of((NZ2, LANES))).astype(F32)
    double_y = doubles(Y2)
    f1[0:3] = f1_lo[...]
    f1[3:11] = f1_own[...]
    f1[11:14] = f1_hi[...]
    mask1 = z_mask(LANES, Z1, grp, NGRP * Z1)

    def ok1(p):
        return mask1 * x_ok(dom * X1 + p - 5, NDOM * X1)

    for p in range(14):
        b1[p] = f1[p] * (4.0 / 9.0)
    fine = []
    for p in range(6):
        level2 = dot_right(r[first2 + 2 + p], place_z)
        fine.append(dot_left(double_y, level2))
    for p in range(1, 13):
        centre, around = beside(b1, p)
        new = (3.0 * centre + around + 4.0 * f1[p]) * (1.0 / 9.0)
        a1[p] = new * ok1(p) + fine[(p - 1) // 2] * mask1
    for p in range(2, 12):
        centre, around = beside(a1, p)
        b1[p] = (3.0 * centre + around + 4.0 * f1[p]) * (1.0 / 9.0) * ok1(p)
    for p in range(3, 11):
        centre, around = beside(b1, p)
        s1[(p - 3) * Y1 : (p - 2) * Y1, :] = (
            (3.0 * centre + around + 4.0 * f1[p]) * (1.0 / 9.0) * ok1(p)
        )
    r0 = lax.broadcasted_iota(I32, (LANES, W0), 0)
    c0 = lax.broadcasted_iota(I32, (LANES, W0), 1)
    spread0 = dot_right(s1[...], ((c0 // 2) == r0).astype(F32))
    double_y0 = doubles(Y1)
    for q in range(8):
        ext[q] = dot_left(double_y0, spread0[q * Y1 : (q + 1) * Y1, :])
    mask = z_mask(W0, CZ, grp, NGRP * CZ)

    def add_fine(p, c):
        e[p] = u2[p] + ext[(p + 1) // 2] * mask
        return c

    lax.fori_loop(0, 14, add_fine, 0, unroll=2)

    def last1(p, c):
        centre, around = beside(e, p + 1)
        new = (3.0 * centre + around + f[p]) * (1.0 / 9.0)
        e2[p] = new * (mask * x_ok(dom * CX + p - 2, NDOM * CX))
        return c

    lax.fori_loop(0, 12, last1, 0, unroll=4)

    def last2(p, c):
        centre, around = beside(e2, p + 1)
        new = (3.0 * centre + around + f[p + 1]) * (1.0 / 9.0)
        e[p] = new * (mask * x_ok(dom * CX + p - 1, NDOM * CX))
        return c

    lax.fori_loop(0, 10, last2, 0, unroll=5)

    def sums(x, carry):
        p = x + 1
        c = e[p]
        own = c[:, 0:LANES]
        potential[x] = own
        gx = 0.5 * (e[p + 1, :, 0:LANES] - e[p - 1, :, 0:LANES])
        gy = 0.5 * (pltpu.roll(own, CY - 1, 0) - pltpu.roll(own, 1, 0))
        gz = 0.5 * (pltpu.roll(c, W0 - 1, 1) - pltpu.roll(c, 1, 1))[:, 0:LANES]
        density = f[x + 2, :, 0:LANES]
        new = (gx * gx, gy * gy, gz * gz, gy * gz, gx * gz, gx * gy, own * density)
        return tuple(
            s + jnp.sum(v.reshape(8, 8, LANES), axis=0) for s, v in zip(carry, new)
        )

    zero = jnp.zeros((8, LANES), F32)
    parts = lax.fori_loop(0, CX, sums, (zero,) * 7, unroll=2)
    lane8 = lanes_of((1, LANES))
    line = jnp.zeros((1, LANES), F32)
    for i, part in enumerate(parts):
        line = jnp.where(lane8 == i, jnp.sum(part), line)
    totals[...] = jnp.broadcast_to(line, (NDEV, LANES))


def after(place, got, f1_own, f1_lo, f1_hi, u2, f):
    consts = [jnp.asarray(t) for t in tables()]
    return pl.pallas_call(
        after_kernel,
        out_shape=(sds(CX, CY, CZ), sds(NDEV, LANES)),
        in_specs=[SM] + [VM] * 10,
        out_specs=(VM, VM),
        scratch_shapes=[
            pltpu.VMEM((NX2 + 2 * PAD2, Y2, NZ2), F32),
            pltpu.VMEM((NX2 + 2 * PAD2, Y2, NZ2), F32),
            pltpu.VMEM((NX2 + 2 * PAD2, Y2, NZ2), F32),
            pltpu.VMEM((NX3 * Y2, NZ2), F32),
            pltpu.VMEM((14, CY, W0), F32),
            pltpu.VMEM((12, CY, W0), F32),
            pltpu.VMEM((14, Y1, LANES), F32),
            pltpu.VMEM((14, Y1, LANES), F32),
            pltpu.VMEM((14, Y1, LANES), F32),
            pltpu.VMEM((8, CY, W0), F32),
            pltpu.VMEM((8 * Y1, LANES), F32),
        ],
        input_output_aliases={},
        compiler_params=PAR,
        name="after",
    )(place, got, *consts, f1_own, f1_lo, f1_hi, u2, f)


def stress_kernel(got, out):
    total = jnp.sum(got[...], axis=0, keepdims=True)
    lane = lanes_of((1, LANES))
    energy = jnp.sum(jnp.where(lane == 6, total, 0.0))
    cells = float(NDOM * CX * CY * NGRP * CZ)
    line = total / cells - jnp.where(lane < 3, 0.5 * energy / cells, 0.0)
    out[...] = line[0, :6]


def stress_of(got):
    return pl.pallas_call(
        stress_kernel,
        out_shape=sds(6),
        in_specs=[VM],
        out_specs=VM,
        name="stress",
    )(got)


def shift(value, axis, distance):
    n = lax.axis_size(axis)
    route = [(i, i + distance) for i in range(n) if 0 <= i + distance < n]
    return lax.ppermute(value, axis, route)


def step(valence, start, tiles, home, ox, oy, oz, size):
    place = jnp.stack([lax.axis_index(DOM), lax.axis_index(GRP)]).astype(I32)
    lower = shift(start[CX - HU :], DOM, 1)
    upper = shift(start[:HU], DOM, -1)
    message = pack_atoms([v.reshape(-1) for v in (home, ox, oy, oz, size)], tiles)
    got = lax.all_to_all(message.reshape(NDEV, ROWS * LANES), ALL, 0, 0, tiled=True)
    got = got.reshape(NDEV * ROWS, LANES)
    u_left, u_right = edges(start, lower, upper)
    grid, up2, down = deposit(got, valence)
    from1 = shift(grid[2 * CY : 15 * CY].reshape(13, CY, LANES), DOM, 1)
    from2 = shift(up2.reshape(5, CY, LANES), DOM, 2)
    above = shift(down.reshape(6, CY, LANES), DOM, -1)
    f, left, right = join(
        grid, from1, from2, above, u_left, u_right
    )
    from_right = shift(left, GRP, -1)
    from_left = shift(right, GRP, 1)
    u2, fe, f1, chunk = before(place, f, lower, start, upper, from_left, from_right)
    f1_lo = shift(f1[1:4], DOM, 1)
    f1_hi = shift(f1[4:7], DOM, -1)
    everything = lax.all_to_all(chunk, ALL, 0, 0, tiled=True)
    potential, totals = after(place, everything, f1, f1_lo, f1_hi, u2, fe)
    sums = lax.all_to_all(totals, ALL, 0, 0, tiled=True)
    return potential, stress_of(sums)


def solution(mesh):
    split = Mesh(mesh.devices.reshape(4, 4, 4, 2), ("dom_0", "dom_1", "grp_0", "grp_1"))
    atoms = P(DOM + GRP, None)
    return jax.shard_map(
        step,
        mesh=split,
        in_specs=(P(DOM, None, GRP), P(DOM, None, GRP)) + (atoms,) * 6,
        out_specs=(P(DOM, None, GRP), P()),
        check_vma=False,
    )
```

time: 155 us -> 132 us (0.85)
  blocking collectives: 16.1 us -> 47.6 us
  Pallas kernels: 47.8 us -> 27.9 us
  waiting for transfers between devices: 33.2 us -> 17.6 us
  local copies, waits for them, and re-layouts: 12 us -> 2.49 us
  starting transfers between devices: 44 us -> 35 us
    all_to_all x1 -> x2, blocking collectives: 16.1 us -> 47.6 us  [the longest x1 31.4 us: step(): lax.all_to_all(message.reshape(NDEV, ROWS * LANES), ALL, 0, 0, tiled=True)]
    all_to_all x2 -> x1, waiting for transfers between devices: 19.9 us -> 4.85 us  [step(): everything = lax.all_to_all(chunk, ALL, 0, 0, tiled=True)]
    pallas_call x1, Pallas kernels: 16.5 us -> 5.59 us  [deposit(): pl.pallas_call(deposit_kernel, out_shape=(sds(16 * CY, LANES), sds(5 * CY...]
    all_to_all x2 -> x1, starting transfers between devices: 20.4 us -> 10.7 us  [step(): everything = lax.all_to_all(chunk, ALL, 0, 0, tiled=True)]
    pallas_call x1, Pallas kernels: 16.2 us -> 8.5 us  [after(): pl.pallas_call(after_kernel, out_shape=(sds(CX, CY, CZ), sds(NDEV, LANES)...]
    unnamed x27 -> x18, local copies, waits for them, and re-layouts: 7.8 us -> 2.42 us
    all_to_all x1 -> x0, local copies, waits for them, and re-layouts: 2.17 us -> none  [shards(): got = lax.all_to_all(message, ALL, 0, 0, tiled=True)]
    pallas_call x4 -> x5, Pallas kernels: 15.1 us -> 13.8 us  [the longest x1 6 us: pack_atoms(): pl.pallas_call(pack_kernel, out_shape=sds(NDEV * ROWS, LANES), in_specs=[...]
  transfers between devices with their start and end apart: 11 -> 10, of which waited for: 6 -> 6; matrix products, arithmetic and copies ran while one was open for 0% -> 0% of each run, Pallas kernels for 11% -> 0%
where the time goes in v2:
time: 132 us
  blocking collectives  47.6 us (36%)
  starting transfers between devices  35 us (27%)
  Pallas kernels  27.9 us (21%)
  waiting for transfers between devices  17.6 us (13%)
  local copies, waits for them, and re-layouts  2.49 us (2%)
    all_to_all x1, blocking collectives, step(): lax.all_to_all(message.reshape(NDEV, ROWS * LANES), ALL, 0, 0, tiled=True)  31.4 us
    ppermute x9, starting transfers between devices, shift(): return lax.ppermute(value, axis, route)  24.3 us
    all_to_all x1, blocking collectives, step(): sums = lax.all_to_all(totals, ALL, 0, 0, tiled=True)  16.2 us
    ppermute x9, waiting for transfers between devices, shift(): return lax.ppermute(value, axis, route)  12.7 us
    all_to_all x1, starting transfers between devices, step(): everything = lax.all_to_all(chunk, ALL, 0, 0, tiled=True)  10.7 us
    pallas_call x1, Pallas kernels, after(): pl.pallas_call(after_kernel, out_shape=(sds(CX, CY, CZ), sds(NDEV, LANES)...  8.5 us
    pallas_call x1, Pallas kernels, pack_atoms(): pl.pallas_call(pack_kernel, out_shape=sds(NDEV * ROWS, LANES), in_specs=[...  6 us
    pallas_call x1, Pallas kernels, before(): pl.pallas_call(before_kernel, out_shape=(sds(14, CY, W0), sds(12, CY, W0)...  5.6 us
  transfers between devices with their start and end apart: 10, of which 6 were waited for; matrix products, arithmetic and copies ran while one was open for 0% of the time, Pallas kernels for 0%

profile of v2, /device:TPU:1, one launch (start us, length us, event | category | flops | bytes accessed | tf_op | source)
XLA Modules:
  0.0 131.5 jit_solution(18379259836335908131)
XLA Ops:
  0.6 6.0 %pack_atoms.1 = f32[2176,128]{1,0:T(8,128)} custom-call(s32[256]{0:T(256)} %bitcast.25, s32[256]{0:T(256)} %bitcast.26, s32[256]{0:T(256)} %bitcast.27, s32[256]{0:T(256)} %bitcast.28, s32[256]{0:T(256)} %bitcast.29, f32[256,512]{1,0:T(8,128)} %tiles_h.1), custom_call_target="tpu_custom_call" | custom-call | tf_op jit(solution)/shard_map/pack_atoms/pallas_call | solution.py:154
  6.6 0.0 copy-start.2
  6.6 31.4 %all_to_all.25 = f32[128,1,2176]{2,1,0:T(1,128)S(1)} all-to-all(f32[128,1,2176]{2,1,0:T(1,128)} %bitcast.22), channel_id=1, replica_groups=mesh['dom_0'=4,'dom_1'=4,'grp_0'=4,'grp_1'=2] {'dom_0','dom_1','grp_0','..., dimensions={0} | all-to-all | bytes 2228224 | tf_op jit(solution)/shard_map/all_to_all | solution.py:778
  38.0 5.6 %deposit.1 = (f32[1024,128]{1,0:T(8,128)S(1)}, f32[320,128]{1,0:T(8,128)S(1)}, f32[384,128]{1,0:T(8,128)S(1)}) custom-call(f32[2176,128]{1,0:T(8,128)S(1)} %bitcast.17, f32[512,128]{1,0:T(8,128)S(1)} %bitcast.18), custom_call_target="tpu_custom_call" | custom-call | tf_op jit(solution)/shard_map/deposit/pallas_call | solution.py:249
  43.7 2.1 %collective-permute-start = (f32[13,64,128]{2,1,0:T(8,128)S(1)}, f32[13,64,128]{2,1,0:T(8,128)S(1)}, u32[]{:S(2)}, u32[]{:S(2)}) collective-permute-start(f32[13,64,128]{2,1,0:T(8,128)S(1)} %bitcast.23), channel_id=1, source_target_pairs={{0,8},{8,16},{16,24},{24,32},{32,40},{40,48},{48,56},{56,64},{64,7... | collective-permute-start | bytes 1277960 | tf_op jit(solution)/shard_map/ppermute | solution.py:770
  45.8 1.3 collective-permute-start.4
  47.1 4.0 %collective-permute-start.3 = (f32[7,64,128]{2,1,0:T(8,128)S(1)}, f32[7,64,128]{2,1,0:T(8,128)S(1)}, u32[]{:S(2)}, u32[]{:S(2)}) collective-permute-start(f32[7,64,128]{2,1,0:T(8,128)S(1)} %get-tuple-element.31), channel_id=1, source_target_pairs={{0,8},{8,16},{16,24},{24,32},{32,40},{40,48},{48,56},{56,64},{64,7... | collective-permute-start | bytes 688136 | tf_op jit(solution)/shard_map/ppermute | solution.py:770
  51.1 1.3 collective-permute-start.2
  52.4 4.8 %collective-permute-start.1 = (f32[5,64,128]{2,1,0:T(8,128)S(1)}, f32[5,64,128]{2,1,0:T(8,128)S(1)}, u32[]{:S(2)}, u32[]{:S(2)}) collective-permute-start(f32[5,64,128]{2,1,0:T(8,128)S(1)} %bitcast.21), channel_id=1, source_target_pairs={{0,16},{8,24},{16,32},{24,40},{32,48},{40,56},{48,64},{56,72},{64,... | collective-permute-start | bytes 491528 | tf_op jit(solution)/shard_map/ppermute | solution.py:770
  57.2 0.0 collective-permute-done.4.u_hi
  57.2 1.3 collective-permute-done.3.u_lo
  58.5 0.4 edges.1
  58.9 3.1 %collective-permute-done.1.from2 = f32[5,64,128]{2,1,0:T(8,128)S(1)} collective-permute-done((f32[5,64,128]{2,1,0:T(8,128)S(1)}, f32[5,64,128]{2,1,0:T(8,128)S(1)}, u32[]{:S(2)}, u32[]{:S(2)}) %collective-permute-start.1) | collective-permute-done | bytes 163872 | tf_op jit(solution)/shard_map/ppermute | solution.py:770
  62.0 0.0 collective-permute-done.from1
  62.0 0.4 join.1
  62.3 3.6 %collective-permute-start.5 = (f32[6,64,128]{2,1,0:T(8,128)S(1)}, f32[6,64,128]{2,1,0:T(8,128)S(1)}, u32[]{:S(2)}, u32[]{:S(2)}) collective-permute-start(f32[6,64,128]{2,1,0:T(8,128)S(1)} %get-tuple-element.22), channel_id=1, source_target_pairs={{0,1},{1,2},{2,3},{3,4},{4,5},{5,6},{6,7},{8,9},{9,10},{10,11},{11... | collective-permute-start | bytes 589832 | tf_op jit(solution)/shard_map/ppermute | solution.py:770
  66.0 1.9 %collective-permute-start.6 = (f32[6,64,128]{2,1,0:T(8,128)S(1)}, f32[6,64,128]{2,1,0:T(8,128)S(1)}, u32[]{:S(2)}, u32[]{:S(2)}) collective-permute-start(f32[6,64,128]{2,1,0:T(8,128)S(1)} %get-tuple-element.23), channel_id=1, source_target_pairs={{1,0},{2,1},{3,2},{4,3},{5,4},{6,5},{7,6},{9,8},{10,9},{11,10},{12... | collective-permute-start | bytes 589832 | tf_op jit(solution)/shard_map/ppermute | solution.py:770
  67.9 0.1 pad_add_fusion.place
  68.0 0.6 collective-permute-done.5.from_left
  68.6 4.4 %collective-permute-done.6.from_right = f32[6,64,128]{2,1,0:T(8,128)S(1)} collective-permute-done((f32[6,64,128]{2,1,0:T(8,128)S(1)}, f32[6,64,128]{2,1,0:T(8,128)S(1)}, u32[]{:S(2)}, u32[]{:S(2)}) %collective-permute-start.6) | collective-permute-done | bytes 196640 | tf_op jit(solution)/shard_map/ppermute | solution.py:770
  73.0 0.7 copy-done.3
  73.6 0.9 copy-done.4
  74.6 5.6 %before.1 = (f32[14,64,256]{2,1,0:T(8,128)S(1)}, f32[12,64,256]{2,1,0:T(8,128)S(1)}, f32[8,32,128]{2,1,0:T(8,128)S(1)}, f32[128,8,128]{2,1,0:T(8,128)S(1)}) custom-call(s32[2]{0:T(128)S(1)} %pad_add_fusion.place, f32[20,64,128]{2,1,0:T(8,128)S(1)} %get-tuple-element.21.f_in, f32[7,64,128]{2,1,0:T(8,128)S(1)} %collective-permute-done.3.u_lo, ...), custom_call_target="tpu_custom_call" | custom-call | tf_op jit(solution)/shard_map/before/pallas_call | solution.py:484
  80.2 0.8 copy-done.1
  81.0 10.7 %all-to-all-start.1 = ((f32[128,8,128]{2,1,0:T(8,128)}), f32[128,8,128]{2,1,0:T(8,128)S(1)}, u32[]{:S(2)}, u32[]{:S(2)}) async-start(f32[128,8,128]{2,1,0:T(8,128)} %copy-done.1), calls=%async_computation.1 | async-start | bytes 1048576 | tf_op jit(solution)/shard_map/all_to_all | solution.py:793
  91.7 1.3 collective-permute-start.8
  93.0 4.0 %collective-permute-start.7 = (f32[3,32,128]{2,1,0:T(8,128)S(1)}, f32[3,32,128]{2,1,0:T(8,128)S(1)}, u32[]{:S(2)}, u32[]{:S(2)}) collective-permute-start(f32[3,32,128]{2,1,0:T(8,128)S(1)} %get-tuple-element.33), channel_id=1, source_target_pairs={{0,8},{8,16},{16,24},{24,32},{32,40},{40,48},{48,56},{56,64},{64,7... | collective-permute-start | bytes 147464 | tf_op jit(solution)/shard_map/ppermute | solution.py:770
  97.0 3.4 %collective-permute-done.8.f1_hi = f32[3,32,128]{2,1,0:T(8,128)S(1)} collective-permute-done((f32[3,32,128]{2,1,0:T(8,128)S(1)}, f32[3,32,128]{2,1,0:T(8,128)S(1)}, u32[]{:S(2)}, u32[]{:S(2)}) %collective-permute-start.8) | collective-permute-done | bytes 49184 | tf_op jit(solution)/shard_map/ppermute | solution.py:770
  100.4 4.8 %all-to-all-done.1.got = f32[128,8,128]{2,1,0:T(8,128)S(1)} async-done(((f32[128,8,128]{2,1,0:T(8,128)}), f32[128,8,128]{2,1,0:T(8,128)S(1)}, u32[]{:S(2)}, u32[]{:S(2)}) %all-to-all-start.1) | async-done | bytes 524320 | tf_op jit(solution)/shard_map/all_to_all | solution.py:793
  105.3 8.5 %after.1 = (f32[8,64,128]{2,1,0:T(8,128)}, f32[128,128]{1,0:T(8,128)S(1)}) custom-call(s32[2]{0:T(128)S(1)} %pad_add_fusion.place, f32[128,8,128]{2,1,0:T(8,128)S(1)} %all-to-all-done.1.got, f32[128,128]{1,0:T(8,128)S(1)} %copy-done.8, f32[128,128]{1,0:T(8,128)S(1)} %copy-done.7, f32[128,128]{1,0:T(8,128)S(1)} %copy-done.6, f32[128,128]{1,0:T(8,128)S(1)} %copy-done.5, ...), custom_call_target="tpu_custom_call" | custom-call | tf_op jit(solution)/shard_map/after/pallas_call | solution.py:724
  113.8 16.2 %all_to_all.26 = f32[128,1,128]{2,1,0:T(1,128)} all-to-all(f32[128,1,128]{2,1,0:T(1,128)S(1)} %bitcast.19), channel_id=1, replica_groups=mesh['dom_0'=4,'dom_1'=4,'grp_0'=4,'grp_1'=2] {'dom_0','dom_1','grp_0','..., dimensions={0} | all-to-all | bytes 131072 | tf_op jit(solution)/shard_map/all_to_all | solution.py:795
  130.0 1.5 %stress.1 = f32[6]{0:T(128)} custom-call(f32[128,128]{1,0:T(8,128)} %bitcast.24), custom_call_target="tpu_custom_call" | custom-call | tf_op jit(solution)/shard_map/stress/pallas_call | solution.py:758
  (19 shorter events, 0.1 us)
Async XLA Ops:
  6.6 31.4 %copy-start.2 = (f32[8,64,128]{2,1,0:T(8,128)S(1)}, f32[8,64,128]{2,1,0:T(8,128)}, u32[]{:S(2)}) copy-start(f32[8,64,128]{2,1,0:T(8,128)} %param.12) | copy-start | bytes 786436
  38.0 7.7 %copy-start = (f32[8,64,128]{2,1,0:T(8,128)S(1)}, f32[8,64,128]{2,1,0:T(8,128)}, u32[]{:S(2)}) copy-start(f32[8,64,128]{2,1,0:T(8,128)} %start.3) | copy-start | bytes 786436
  43.7 18.3 %collective-permute-start = (f32[13,64,128]{2,1,0:T(8,128)S(1)}, f32[13,64,128]{2,1,0:T(8,128)S(1)}, u32[]{:S(2)}, u32[]{:S(2)}) collective-permute-start(f32[13,64,128]{2,1,0:T(8,128)S(1)} %bitcast.23), channel_id=1, source_target_pairs={{0,8},{8,16},{16,24},{24,32},{32,40},{40,48},{48,56},{56,64},{64,7... | collective-permute-start | bytes 1277960 | tf_op jit(solution)/shard_map/ppermute | solution.py:770
  45.8 11.4 %collective-permute-start.4 = (f32[7,64,128]{2,1,0:T(8,128)S(1)}, f32[7,64,128]{2,1,0:T(8,128)S(1)}, u32[]{:S(2)}, u32[]{:S(2)}) collective-permute-start(f32[7,64,128]{2,1,0:T(8,128)S(1)} %get-tuple-element.30), channel_id=1, source_target_pairs={{8,0},{16,8},{24,16},{32,24},{40,32},{48,40},{56,48},{64,56},{72,6... | collective-permute-start | bytes 688136 | tf_op jit(solution)/shard_map/ppermute | solution.py:770
  47.1 11.3 %collective-permute-start.3 = (f32[7,64,128]{2,1,0:T(8,128)S(1)}, f32[7,64,128]{2,1,0:T(8,128)S(1)}, u32[]{:S(2)}, u32[]{:S(2)}) collective-permute-start(f32[7,64,128]{2,1,0:T(8,128)S(1)} %get-tuple-element.31), channel_id=1, source_target_pairs={{0,8},{8,16},{16,24},{24,32},{32,40},{40,48},{48,56},{56,64},{64,7... | collective-permute-start | bytes 688136 | tf_op jit(solution)/shard_map/ppermute | solution.py:770
  51.1 10.8 %collective-permute-start.2 = (f32[6,64,128]{2,1,0:T(8,128)S(1)}, f32[6,64,128]{2,1,0:T(8,128)S(1)}, u32[]{:S(2)}, u32[]{:S(2)}) collective-permute-start(f32[6,64,128]{2,1,0:T(8,128)S(1)} %bitcast.20), channel_id=1, source_target_pairs={{8,0},{16,8},{24,16},{32,24},{40,32},{48,40},{56,48},{64,56},{72,6... | collective-permute-start | bytes 589832 | tf_op jit(solution)/shard_map/ppermute | solution.py:770
  52.4 9.5 %collective-permute-start.1 = (f32[5,64,128]{2,1,0:T(8,128)S(1)}, f32[5,64,128]{2,1,0:T(8,128)S(1)}, u32[]{:S(2)}, u32[]{:S(2)}) collective-permute-start(f32[5,64,128]{2,1,0:T(8,128)S(1)} %bitcast.21), channel_id=1, source_target_pairs={{0,16},{8,24},{16,32},{24,40},{32,48},{40,56},{48,64},{56,72},{64,... | collective-permute-start | bytes 491528 | tf_op jit(solution)/shard_map/ppermute | solution.py:770
  62.3 6.2 %collective-permute-start.5 = (f32[6,64,128]{2,1,0:T(8,128)S(1)}, f32[6,64,128]{2,1,0:T(8,128)S(1)}, u32[]{:S(2)}, u32[]{:S(2)}) collective-permute-start(f32[6,64,128]{2,1,0:T(8,128)S(1)} %get-tuple-element.22), channel_id=1, source_target_pairs={{0,1},{1,2},{2,3},{3,4},{4,5},{5,6},{6,7},{8,9},{9,10},{10,11},{11... | collective-permute-start | bytes 589832 | tf_op jit(solution)/shard_map/ppermute | solution.py:770
  66.0 7.0 %collective-permute-start.6 = (f32[6,64,128]{2,1,0:T(8,128)S(1)}, f32[6,64,128]{2,1,0:T(8,128)S(1)}, u32[]{:S(2)}, u32[]{:S(2)}) collective-permute-start(f32[6,64,128]{2,1,0:T(8,128)S(1)} %get-tuple-element.23), channel_id=1, source_target_pairs={{1,0},{2,1},{3,2},{4,3},{5,4},{6,5},{7,6},{9,8},{10,9},{11,10},{12... | collective-permute-start | bytes 589832 | tf_op jit(solution)/shard_map/ppermute | solution.py:770
  73.0 0.7 copy-start.3
  73.6 0.9 copy-start.4
  74.6 30.7 %copy-start.5 = (f32[128,128]{1,0:T(8,128)S(1)}, f32[128,128]{1,0:T(8,128)}, u32[]{:S(2)}) copy-start(f32[128,128]{1,0:T(8,128)} %constant.30.clone.scale) | copy-start | bytes 196612
  74.6 30.7 %copy-start.6 = (f32[128,128]{1,0:T(8,128)S(1)}, f32[128,128]{1,0:T(8,128)}, u32[]{:S(2)}) copy-start(f32[128,128]{1,0:T(8,128)} %constant.29.clone.tz) | copy-start | bytes 196612
  80.2 0.8 copy-start.1
  81.0 24.3 %copy-start.7 = (f32[128,128]{1,0:T(8,128)S(1)}, f32[128,128]{1,0:T(8,128)}, u32[]{:S(2)}) copy-start(f32[128,128]{1,0:T(8,128)} %constant.28.clone.txy_t) | copy-start | bytes 196612
  81.0 24.3 %copy-start.8 = (f32[128,128]{1,0:T(8,128)S(1)}, f32[128,128]{1,0:T(8,128)}, u32[]{:S(2)}) copy-start(f32[128,128]{1,0:T(8,128)} %constant.27.clone.txy) | copy-start | bytes 196612
  81.0 24.3 %all-to-all-start.1 = ((f32[128,8,128]{2,1,0:T(8,128)}), f32[128,8,128]{2,1,0:T(8,128)S(1)}, u32[]{:S(2)}, u32[]{:S(2)}) async-start(f32[128,8,128]{2,1,0:T(8,128)} %copy-done.1), calls=%async_computation.1 | async-start | bytes 1048576 | tf_op jit(solution)/shard_map/all_to_all | solution.py:793
  91.7 8.7 %collective-permute-start.8 = (f32[3,32,128]{2,1,0:T(8,128)S(1)}, f32[3,32,128]{2,1,0:T(8,128)S(1)}, u32[]{:S(2)}, u32[]{:S(2)}) collective-permute-start(f32[3,32,128]{2,1,0:T(8,128)S(1)} %get-tuple-element.32), channel_id=1, source_target_pairs={{8,0},{16,8},{24,16},{32,24},{40,32},{48,40},{56,48},{64,56},{72,6... | collective-permute-start | bytes 147464 | tf_op jit(solution)/shard_map/ppermute | solution.py:770
  93.0 7.4 %collective-permute-start.7 = (f32[3,32,128]{2,1,0:T(8,128)S(1)}, f32[3,32,128]{2,1,0:T(8,128)S(1)}, u32[]{:S(2)}, u32[]{:S(2)}) collective-permute-start(f32[3,32,128]{2,1,0:T(8,128)S(1)} %get-tuple-element.33), channel_id=1, source_target_pairs={{0,8},{8,16},{16,24},{24,32},{32,40},{40,48},{48,56},{56,64},{64,7... | collective-permute-start | bytes 147464 | tf_op jit(solution)/shard_map/ppermute | solution.py:770

commit v3 on v2

--- a/solution.py
+++ b/solution.py
@@ -16,7 +16,6 @@
 ALL = DOM + GRP
 F32 = jnp.float32
 I32 = jnp.int32
-HI = lax.Precision.HIGHEST
 VM = pl.BlockSpec(memory_space=pltpu.VMEM)
 SM = pl.BlockSpec(memory_space=pltpu.SMEM)
 
@@ -41,10 +40,15 @@
     return lax.broadcasted_iota(I32, shape, len(shape) - 2)
 
 
-def dot(a, b):
-    return lax.dot_general(
-        a, b, (((1,), (0,)), ((), ())), precision=HI, preferred_element_type=F32
-    )
+def split(a):
+    hi = a.astype(jnp.bfloat16)
+    return hi, (a - hi.astype(F32)).astype(jnp.bfloat16)
+
+
+def dot3(a, b):
+    (ah, al), (bh, bl) = split(a), split(b)
+    low = jnp.dot(ah, bl, preferred_element_type=F32) + jnp.dot(al, bh, preferred_element_type=F32)
+    return jnp.dot(ah, bh, preferred_element_type=F32) + low
 
 
 def dot_right(a, ones):
@@ -111,40 +115,28 @@
     need = rows_of((TILE_ROWS, LANES)) + jnp.where(lane < 64, 0, 4)
     need = jnp.maximum(jnp.maximum(need, (lane // 8) % 8), lane % 8)
     tile_c = lane % 8
-    lane1 = lanes_of((1, LANES))
-
-    def several(step, c):
+    part1, slot1 = lanes_of((1, LANES)) & 3, lanes_of((1, LANES)) >> 2
+
+    for start in range(0, ATOMS, PER_STEP):
         placed = []
-        for i in range(PER_STEP):
-            n = step * PER_STEP + i
-            z_in, y_in = oz[n] & 7, oy[n] & 15
-            value = rows[pl.ds(pl.multiple_of(n * TILE_ROWS, 4), TILE_ROWS), :]
+        for n in range(start, start + PER_STEP):
+            z_in = oz[n] & 7
+            shift_ = (oy[n] & 15) * 8 + z_in
+            value = rows[n * TILE_ROWS : (n + 1) * TILE_ROWS, :]
             value = jnp.where(need < size[n], value, 0.0)
-            shift = y_in * 8 + z_in
-            near = pltpu.roll(value, shift & 127, 1)
-            far = pltpu.roll(value, (shift + 120) & 127, 1)
+            near = pltpu.roll(value, shift_, 1)
+            far = pltpu.roll(value, shift_ + 120, 1)
             placed.append(jnp.where(tile_c >= z_in, near, far))
-        for i in range(PER_STEP):
-            n = step * PER_STEP + i
+        for n in range(start, start + PER_STEP):
             to = home[n]
             rank = count[to]
             count[to] = rank + 1
             base = to * ROWS
-            out[pl.ds(base + rank * TILE_ROWS, TILE_ROWS), :] = placed[i]
-            y_block, z_block = oy[n] >> 4, oz[n] >> 3
-            row = (y_block * ZB + z_block) * 16 + ox[n]
-            wrapped = (((y_block + 1) & 3) * ZB + z_block) * 16 + ox[n]
-            line = jnp.where(lane1 & 3 == 0, row, wrapped)
-            line = jnp.where(lane1 & 3 == 2, (oy[n] & 15) * 8, line)
-            line = jnp.where(lane1 & 3 == 3, oz[n] & 7, line)
+            out[pl.ds(base + rank * TILE_ROWS, TILE_ROWS), :] = placed[n - start]
+            line = jnp.where(part1 == 0, ox[n], jnp.where(part1 == 1, oy[n], oz[n]))
             pltpu.store(
-                out.at[pl.ds(base + ROWS - 1, 1), :],
-                line.astype(F32),
-                mask=(lane1 >> 2) == rank,
+                out.at[pl.ds(base + ROWS - 1, 1), :], line.astype(F32), mask=slot1 == rank
             )
-        return c
-
-    lax.fori_loop(0, ATOMS // PER_STEP, several, 0)
 
 
 PER_STEP = 16
@@ -171,10 +163,18 @@
 
 
 def deposit_kernel(got, valence, grid, up2, down, acc_a, acc_b, other, corner_v, corner_s, sem):
+    part = lanes_of((8, LANES)) & 3
     for g in range(NDEV // 8):
-        corner_v[g * 8 : g * 8 + 8, :] = got[
-            pl.ds(g * 8 * ROWS + ROWS - 1, 8, stride=ROWS), :
-        ].astype(I32)
+        raw = got[pl.ds(g * 8 * ROWS + ROWS - 1, 8, stride=ROWS), :].astype(I32)
+        back, ahead, ahead2 = (pltpu.roll(raw, n, 1) for n in (1, 127, 126))
+        x = jnp.where(part == 0, raw, back)
+        y = jnp.where(part == 0, ahead, jnp.where(part == 1, raw, back))
+        z = jnp.where(part == 0, ahead2, jnp.where(part == 1, ahead, back))
+        y_block = jnp.where(part == 1, ((y >> 4) + 1) & 3, y >> 4)
+        row = (y_block * ZB + (z >> 3)) * 16 + x
+        corner_v[g * 8 : g * 8 + 8, :] = jnp.where(
+            part < 2, row, jnp.where(part == 2, (y & 15) * 8, z & 7)
+        )
     copy = pltpu.make_async_copy(corner_v, corner_s, sem)
     copy.start()
 
@@ -196,7 +196,7 @@
     lane = lanes_of((8, LANES))
     z_of = lane % 8
 
-    def one(src, c):
+    for src in range(NDEV):
         for k in range(CAP):
             acc = acc_a if k % 2 == 0 else acc_b
             row = corner_s[src, 4 * k]
@@ -217,9 +217,6 @@
             acc[pl.ds(row + 16, 8), :] = a1 + jnp.where(near, 0.0, here)
             acc[pl.ds(wrapped, 8), :] = a2 + jnp.where(near, round_, 0.0)
             acc[pl.ds(wrapped + 16, 8), :] = a3 + jnp.where(near, 0.0, round_)
-        return c
-
-    lax.fori_loop(0, NDEV, one, 0)
     group = lane // 8
 
     def lay_out(yb, c):
@@ -283,9 +280,9 @@
         hi = jnp.zeros((CY, LANES), F32)
         for k, plane in enumerate(planes[g * 8 : g * 8 + 8]):
             plane = plane()
-            lo = jnp.where(slot == k, pltpu.roll(plane, 16 * k, 1) if k else plane, lo)
-            shift_ = (16 * k - 112) % 128
-            hi = jnp.where(slot == k, pltpu.roll(plane, shift_, 1) if shift_ else plane, hi)
+            plane = pltpu.roll(plane, 16 * k, 1) if k else plane
+            lo = jnp.where(slot == k, plane, lo)
+            hi = jnp.where(slot == (k - 1) % 8, plane, hi)
         left[at + g] = lo
         right[at + g] = hi
 
@@ -388,54 +385,105 @@
     return ((r // 2) == c).astype(F32)
 
 
+STEP = CY + 16
+
+
+def half_at(p, h):
+    return (p * 2 + h) * STEP
+
+
+def whole(ref, p, h):
+    return ref[pl.ds(pl.multiple_of(half_at(p, h) + 8, 8), CY), :]
+
+
+def put(ref, p, h, value):
+    base = half_at(p, h)
+    ref[pl.ds(pl.multiple_of(base + 8, 8), CY), :] = value
+    ref[pl.ds(pl.multiple_of(base, 8), 8), :] = value[CY - 8 :]
+    ref[pl.ds(pl.multiple_of(base + 8 + CY, 8), 8), :] = value[:8]
+
+
+def moved(ref, p, h, by):
+    return ref[pl.ds(half_at(p, h) + 8 + by, CY), :]
+
+
+def z_sides(own, edge):
+    lane = lanes_of(own.shape)
+    first, last = lane == 0, lane == LANES - 1
+    own_up, edge_up = pltpu.roll(own, LANES - 1, 1), pltpu.roll(edge, LANES - 1, 1)
+    own_down, edge_down = pltpu.roll(own, 1, 1), pltpu.roll(edge, 1, 1)
+    return (
+        (jnp.where(last, edge_up, own_up), jnp.where(first, edge_down, own_down)),
+        (jnp.where(last, own_up, edge_up), jnp.where(first, own_down, edge_down)),
+    )
+
+
+def beside0(ref, p):
+    centre = [whole(ref, p, h) for h in range(2)]
+    sides = z_sides(*centre)
+    around = [
+        (whole(ref, p + 1, h) + whole(ref, p - 1, h))
+        + (moved(ref, p, h, 1) + moved(ref, p, h, -1))
+        + (sides[h][0] + sides[h][1])
+        for h in range(2)
+    ]
+    return centre, around
+
+
 def before_kernel(
-    place, f_in, u_lo, start, u_hi, from_left, from_right, u_out, f_out, f1, chunk, u, ua, f, u2, pairs, v1, r1
+    place, f_in, u_lo, start, u_hi, from_left, from_right, u_out, f_out, f1, chunk, u, ua, fe, u2, pairs, v1, r1
 ):
     dom, grp = place[0], place[1]
-    lane = lanes_of((CY, LANES))
+    slot = lanes_of((CY, LANES)) // 16
     for p in range(NU_ + NF):
         g, k = (p // 8, p % 8) if p < NU_ else (UGROUPS + (p - NU_) // 8, (p - NU_) % 8)
-        right = from_right[g]
-        right = pltpu.roll(right, (-16 * k) % 128, 1) if k else right
-        left = from_left[g]
-        shift = (112 - 16 * k) % 128
-        left = pltpu.roll(left, shift, 1) if shift else left
-        edge = jnp.where(lane < 16, right, jnp.where(lane >= 112, left, 0.0))
+        edge = jnp.where(slot == k, from_right[g], 0.0)
+        edge = jnp.where(slot == (k - 1) % 8, from_left[g], edge)
+        edge = pltpu.roll(edge, (-16 * k) % 128, 1) if k else edge
         if p < NU_:
-            u[p, :, 0:LANES] = u_plane(p, u_lo, start, u_hi)
-            u[p, :, LANES:] = edge
+            put(u, p, 0, u_plane(p, u_lo, start, u_hi))
+            put(u, p, 1, edge)
         else:
-            f[p - NU_, :, 0:LANES] = f_in[p - NU_]
-            f[p - NU_, :, LANES:] = edge
-    mask = z_mask(W0, CZ, grp, NGRP * CZ)
+            fe[p - NU_] = edge
+    f = (f_in, fe)
+    mask = z_mask(W0, CZ, grp, NGRP * CZ) * (1.0 / 9.0)
+    mask = (mask[:, :LANES], mask[:, LANES:])
 
     def sweep1(p, c):
-        centre, around = beside(u, p + 1)
-        new = (3.0 * centre + around + f[p]) * (1.0 / 9.0)
-        ua[p] = new * (mask * x_ok(dom * CX + p - HF, NDOM * CX))
+        centre, around = beside0(u, p + 1)
+        ok = x_ok(dom * CX + p - HF, NDOM * CX)
+        for h in range(2):
+            put(ua, p, h, (3.0 * centre[h] + around[h] + f[h][p]) * (mask[h] * ok))
         return c
 
     lax.fori_loop(0, NF, sweep1, 0, unroll=4)
 
     def sweep2(p, c):
-        centre, around = beside(ua, p + 1)
-        new = (3.0 * centre + around + f[p + 1]) * (1.0 / 9.0)
-        u2[p] = new * (mask * x_ok(dom * CX + p - 5, NDOM * CX))
+        centre, around = beside0(ua, p + 1)
+        ok = x_ok(dom * CX + p - 5, NDOM * CX)
+        for h in range(2):
+            put(u2, p, h, (3.0 * centre[h] + around[h] + f[h][p + 1]) * (mask[h] * ok))
         return c
 
     lax.fori_loop(0, NF - 2, sweep2, 0, unroll=3)
 
-    u_out[...] = u2[2:16]
-    f_out[...] = f[4:16]
+    for p in range(14):
+        for h in range(2):
+            u_out[p, h] = whole(u2, p + 2, h)
+    for p in range(12):
+        for h in range(2):
+            f_out[p, h] = f[h][p + 4]
 
     def residue0(q, c):
-        total = None
+        total = [None, None]
         for i in range(2):
             p = 2 * q + i + 1
-            centre, around = beside(u2, p)
-            r = f[p + 1] - (6.0 * centre - around)
-            total = r if total is None else total + r
-        pairs[pl.ds(pl.multiple_of(q * CY, CY), CY), :] = total
+            centre, around = beside0(u2, p)
+            for h in range(2):
+                r = f[h][p + 1] - (6.0 * centre[h] - around[h])
+                total[h] = r if total[h] is None else total[h] + r
+        for h in range(2):
+            pairs[pl.ds(pl.multiple_of(q * CY, CY), CY), h * LANES : (h + 1) * LANES] = total[h]
         return c
 
     lax.fori_loop(0, 8, residue0, 0, unroll=2)
@@ -473,29 +521,26 @@
             piece = pltpu.roll(piece, 32 * s, 1) if s else piece
             packed = jnp.where(slot == s, piece, packed)
 
-    def spread(d, c):
-        chunk[d] = packed
-        return c
-
-    lax.fori_loop(0, NDEV, spread, 0, unroll=8)
+    packed = pltpu.roll(packed, (grp & 3) * 32, 1)
+    chunk[...] = packed
 
 
 def before(place, f, u_lo, start, u_hi, from_left, from_right):
     return pl.pallas_call(
         before_kernel,
         out_shape=(
-            sds(14, CY, W0),
-            sds(12, CY, W0),
+            sds(14, 2, CY, LANES),
+            sds(12, 2, CY, LANES),
             sds(8, Y1, LANES),
-            sds(NDEV, 8, LANES),
+            sds(8, LANES),
         ),
         in_specs=[SM] + [VM] * 6,
         out_specs=(VM,) * 4,
         scratch_shapes=[
-            pltpu.VMEM((NU_, CY, W0), F32),
-            pltpu.VMEM((NF, CY, W0), F32),
-            pltpu.VMEM((NF, CY, W0), F32),
-            pltpu.VMEM((NF - 2, CY, W0), F32),
+            pltpu.VMEM((NU_ * 2 * STEP, LANES), F32),
+            pltpu.VMEM((NF * 2 * STEP, LANES), F32),
+            pltpu.VMEM((NF, CY, LANES), F32),
+            pltpu.VMEM(((NF - 2) * 2 * STEP, LANES), F32),
             pltpu.VMEM((8 * CY, W0), F32),
             pltpu.VMEM((8, Y1, LANES), F32),
             pltpu.VMEM((8, Y1, LANES), F32),
@@ -560,9 +605,8 @@
                     row = None
                     for q in range(4):
                         piece = got[d * NGRP + 4 * t + q]
-                        shift = (32 * (q - s)) % 128
-                        piece = pltpu.roll(piece, shift, 1) if shift else piece
-                        row = piece if row is None else jnp.where(slot == q, piece, row)
+                        row = piece if row is None else jnp.where(slot == (s + q) % 4, piece, row)
+                    row = pltpu.roll(row, (-32 * s) % 128, 1) if s else row
                     g[PAD2 + 2 * d + i, yb * 8 : yb * 8 + 8, t * LANES : (t + 1) * LANES] = row
         return c
 
@@ -610,8 +654,8 @@
     ri = lax.broadcasted_iota(I32, (n3, 2 * n3), 0)
     ci = lax.broadcasted_iota(I32, (n3, 2 * n3), 1)
     source = dot_left(((ci // 2) == ri).astype(F32) * 0.125, z_sums)
-    modes = dot(dot(txy_t[...], source), tz[...]) * scale[...]
-    solved = dot(txy[...], dot(modes, tz[...]))
+    modes = dot3(dot3(txy_t[...], source), tz[...]) * scale[...]
+    solved = dot3(txy[...], dot3(modes, tz[...]))
     rr = lax.broadcasted_iota(I32, (NZ3, NZ2), 0)
     cc = lax.broadcasted_iota(I32, (NZ3, NZ2), 1)
     wide = dot_right(solved, ((cc // 2) == rr).astype(F32))
@@ -639,7 +683,6 @@
     lane = lanes_of((NZ2, LANES))
     signed = jnp.where(lane < 96, lane, lane - LANES)
     place_z = ((grp * Z1 + signed + 2 * NZ2) // 2 - NZ2 == rows_of((NZ2, LANES))).astype(F32)
-    double_y = doubles(Y2)
     f1[0:3] = f1_lo[...]
     f1[3:11] = f1_own[...]
     f1[11:14] = f1_hi[...]
@@ -650,10 +693,9 @@
 
     for p in range(14):
         b1[p] = f1[p] * (4.0 / 9.0)
-    fine = []
-    for p in range(6):
-        level2 = dot_right(r[first2 + 2 + p], place_z)
-        fine.append(dot_left(double_y, level2))
+    level2 = dot_right(r[pl.ds(first2 + 2, 6)].reshape(6 * Y2, NZ2), place_z)
+    tall2 = dot_left(doubles(6 * Y2), level2)
+    fine = [tall2[p * Y1 : (p + 1) * Y1, :] for p in range(6)]
     for p in range(1, 13):
         centre, around = beside(b1, p)
         new = (3.0 * centre + around + 4.0 * f1[p]) * (1.0 / 9.0)
@@ -673,38 +715,44 @@
     for q in range(8):
         ext[q] = dot_left(double_y0, spread0[q * Y1 : (q + 1) * Y1, :])
     mask = z_mask(W0, CZ, grp, NGRP * CZ)
+    mask = (mask[:, :LANES], mask[:, LANES:])
+    mask9 = [m * (1.0 / 9.0) for m in mask]
 
     def add_fine(p, c):
-        e[p] = u2[p] + ext[(p + 1) // 2] * mask
+        for h in range(2):
+            fine0 = ext[(p + 1) // 2, :, h * LANES : (h + 1) * LANES]
+            put(e, p, h, u2[p, h] + fine0 * mask[h])
         return c
 
     lax.fori_loop(0, 14, add_fine, 0, unroll=2)
 
     def last1(p, c):
-        centre, around = beside(e, p + 1)
-        new = (3.0 * centre + around + f[p]) * (1.0 / 9.0)
-        e2[p] = new * (mask * x_ok(dom * CX + p - 2, NDOM * CX))
+        centre, around = beside0(e, p + 1)
+        ok = x_ok(dom * CX + p - 2, NDOM * CX)
+        for h in range(2):
+            put(e2, p, h, (3.0 * centre[h] + around[h] + f[p, h]) * (mask9[h] * ok))
         return c
 
     lax.fori_loop(0, 12, last1, 0, unroll=4)
 
     def last2(p, c):
-        centre, around = beside(e2, p + 1)
-        new = (3.0 * centre + around + f[p + 1]) * (1.0 / 9.0)
-        e[p] = new * (mask * x_ok(dom * CX + p - 1, NDOM * CX))
+        centre, around = beside0(e2, p + 1)
+        ok = x_ok(dom * CX + p - 1, NDOM * CX)
+        for h in range(2):
+            put(e, p, h, (3.0 * centre[h] + around[h] + f[p + 1, h]) * (mask9[h] * ok))
         return c
 
     lax.fori_loop(0, 10, last2, 0, unroll=5)
 
     def sums(x, carry):
         p = x + 1
-        c = e[p]
-        own = c[:, 0:LANES]
+        own = whole(e, p, 0)
         potential[x] = own
-        gx = 0.5 * (e[p + 1, :, 0:LANES] - e[p - 1, :, 0:LANES])
-        gy = 0.5 * (pltpu.roll(own, CY - 1, 0) - pltpu.roll(own, 1, 0))
-        gz = 0.5 * (pltpu.roll(c, W0 - 1, 1) - pltpu.roll(c, 1, 1))[:, 0:LANES]
-        density = f[x + 2, :, 0:LANES]
+        gx = 0.5 * (whole(e, p + 1, 0) - whole(e, p - 1, 0))
+        gy = 0.5 * (moved(e, p, 0, 1) - moved(e, p, 0, -1))
+        (up, down), _ = z_sides(own, whole(e, p, 1))
+        gz = 0.5 * (up - down)
+        density = f[x + 2, 0]
         new = (gx * gx, gy * gy, gz * gz, gy * gz, gx * gz, gx * gy, own * density)
         return tuple(
             s + jnp.sum(v.reshape(8, 8, LANES), axis=0) for s, v in zip(carry, new)
@@ -731,8 +779,8 @@
             pltpu.VMEM((NX2 + 2 * PAD2, Y2, NZ2), F32),
             pltpu.VMEM((NX2 + 2 * PAD2, Y2, NZ2), F32),
             pltpu.VMEM((NX3 * Y2, NZ2), F32),
-            pltpu.VMEM((14, CY, W0), F32),
-            pltpu.VMEM((12, CY, W0), F32),
+            pltpu.VMEM((14 * 2 * STEP, LANES), F32),
+            pltpu.VMEM((12 * 2 * STEP, LANES), F32),
             pltpu.VMEM((14, Y1, LANES), F32),
             pltpu.VMEM((14, Y1, LANES), F32),
             pltpu.VMEM((14, Y1, LANES), F32),
@@ -790,7 +838,8 @@
     u2, fe, f1, chunk = before(place, f, lower, start, upper, from_left, from_right)
     f1_lo = shift(f1[1:4], DOM, 1)
     f1_hi = shift(f1[4:7], DOM, -1)
-    everything = lax.all_to_all(chunk, ALL, 0, 0, tiled=True)
+    chunks = jnp.broadcast_to(chunk[None], (NDEV, 8, LANES))
+    everything = lax.all_to_all(chunks, ALL, 0, 0, tiled=True)
     potential, totals = after(place, everything, f1, f1_lo, f1_hi, u2, fe)
     sums = lax.all_to_all(totals, ALL, 0, 0, tiled=True)
     return potential, stress_of(sums)

time: 132 us -> 128 us (0.970)
  Pallas kernels: 27.9 us -> 23.3 us
    pallas_call x1, Pallas kernels: 6 us -> 4.07 us  [pack_atoms(): pl.pallas_call(pack_kernel, out_shape=sds(NDEV * ROWS, LANES), in_specs=[...]
where the time goes in v3:
time: 128 us; the launch traced here: 127 us
  blocking collectives  47.6 us (37%)
  starting transfers between devices  35 us (27%)
  Pallas kernels  23.3 us (18%)
  waiting for transfers between devices  17.7 us (14%)
  local copies, waits for them, and re-layouts  2.55 us (2%)
    all_to_all x1, blocking collectives, step(): lax.all_to_all(message.reshape(NDEV, ROWS * LANES), ALL, 0, 0, tiled=True)  31.4 us
    ppermute x9, starting transfers between devices, shift(): return lax.ppermute(value, axis, route)  24.3 us
    all_to_all x1, blocking collectives, step(): sums = lax.all_to_all(totals, ALL, 0, 0, tiled=True)  16.2 us
    ppermute x9, waiting for transfers between devices, shift(): return lax.ppermute(value, axis, route)  12.8 us
    all_to_all x1, starting transfers between devices, step(): everything = lax.all_to_all(chunks, ALL, 0, 0, tiled=True)  10.7 us
    pallas_call x1, Pallas kernels, after(): pl.pallas_call(after_kernel, out_shape=(sds(CX, CY, CZ), sds(NDEV, LANES)...  7.38 us
    pallas_call x1, Pallas kernels, before(): pl.pallas_call(before_kernel, out_shape=(sds(14, 2, CY, LANES), sds(12, 2...  5.16 us
    all_to_all x1, waiting for transfers between devices, step(): everything = lax.all_to_all(chunks, ALL, 0, 0, tiled=True)  4.85 us
  transfers between devices with their start and end apart: 10, of which 6 were waited for; matrix products, arithmetic and copies ran while one was open for 0% of the time, Pallas kernels for 0%

profile of v3, /device:TPU:1, one launch (start us, length us, event | category | flops | bytes accessed | tf_op | source)
XLA Modules:
  0.0 127.1 jit_solution(1443314143741335483)
XLA Ops:
  0.6 4.1 %pack_atoms.1 = f32[2176,128]{1,0:T(8,128)} custom-call(s32[256]{0:T(256)} %bitcast.25, s32[256]{0:T(256)} %bitcast.26, s32[256]{0:T(256)} %bitcast.27, s32[256]{0:T(256)} %bitcast.28, s32[256]{0:T(256)} %bitcast.29, f32[256,512]{1,0:T(8,128)} %tiles_h.1), custom_call_target="tpu_custom_call" | custom-call | tf_op jit(solution)/shard_map/pack_atoms/pallas_call | solution.py:146
  4.7 0.0 copy-start.1
  4.7 31.4 %all_to_all.25 = f32[128,1,2176]{2,1,0:T(1,128)S(1)} all-to-all(f32[128,1,2176]{2,1,0:T(1,128)} %bitcast.22), channel_id=1, replica_groups=mesh['dom_0'=4,'dom_1'=4,'grp_0'=4,'grp_1'=2] {'dom_0','dom_1','grp_0','..., dimensions={0} | all-to-all | bytes 2228224 | tf_op jit(solution)/shard_map/all_to_all | solution.py:826
  36.1 4.8 %deposit.1 = (f32[1024,128]{1,0:T(8,128)S(1)}, f32[320,128]{1,0:T(8,128)S(1)}, f32[384,128]{1,0:T(8,128)S(1)}) custom-call(f32[2176,128]{1,0:T(8,128)S(1)} %bitcast.17, f32[512,128]{1,0:T(8,128)S(1)} %bitcast.18), custom_call_target="tpu_custom_call" | custom-call | tf_op jit(solution)/shard_map/deposit/pallas_call | solution.py:246
  40.9 2.1 %collective-permute-start = (f32[13,64,128]{2,1,0:T(8,128)S(1)}, f32[13,64,128]{2,1,0:T(8,128)S(1)}, u32[]{:S(2)}, u32[]{:S(2)}) collective-permute-start(f32[13,64,128]{2,1,0:T(8,128)S(1)} %bitcast.23), channel_id=1, source_target_pairs={{0,8},{8,16},{16,24},{24,32},{32,40},{40,48},{48,56},{56,64},{64,7... | collective-permute-start | bytes 1277960 | tf_op jit(solution)/shard_map/ppermute | solution.py:818
  43.1 1.3 %collective-permute-start.4 = (f32[7,64,128]{2,1,0:T(8,128)S(1)}, f32[7,64,128]{2,1,0:T(8,128)S(1)}, u32[]{:S(2)}, u32[]{:S(2)}) collective-permute-start(f32[7,64,128]{2,1,0:T(8,128)S(1)} %get-tuple-element.30), channel_id=1, source_target_pairs={{8,0},{16,8},{24,16},{32,24},{40,32},{48,40},{56,48},{64,56},{72,6... | collective-permute-start | bytes 688136 | tf_op jit(solution)/shard_map/ppermute | solution.py:818
  44.4 4.0 %collective-permute-start.3 = (f32[7,64,128]{2,1,0:T(8,128)S(1)}, f32[7,64,128]{2,1,0:T(8,128)S(1)}, u32[]{:S(2)}, u32[]{:S(2)}) collective-permute-start(f32[7,64,128]{2,1,0:T(8,128)S(1)} %get-tuple-element.31), channel_id=1, source_target_pairs={{0,8},{8,16},{16,24},{24,32},{32,40},{40,48},{48,56},{56,64},{64,7... | collective-permute-start | bytes 688136 | tf_op jit(solution)/shard_map/ppermute | solution.py:818
  48.4 1.3 %collective-permute-start.2 = (f32[6,64,128]{2,1,0:T(8,128)S(1)}, f32[6,64,128]{2,1,0:T(8,128)S(1)}, u32[]{:S(2)}, u32[]{:S(2)}) collective-permute-start(f32[6,64,128]{2,1,0:T(8,128)S(1)} %bitcast.20), channel_id=1, source_target_pairs={{8,0},{16,8},{24,16},{32,24},{40,32},{48,40},{56,48},{64,56},{72,6... | collective-permute-start | bytes 589832 | tf_op jit(solution)/shard_map/ppermute | solution.py:818
  49.7 4.8 %collective-permute-start.1 = (f32[5,64,128]{2,1,0:T(8,128)S(1)}, f32[5,64,128]{2,1,0:T(8,128)S(1)}, u32[]{:S(2)}, u32[]{:S(2)}) collective-permute-start(f32[5,64,128]{2,1,0:T(8,128)S(1)} %bitcast.21), channel_id=1, source_target_pairs={{0,16},{8,24},{16,32},{24,40},{32,48},{40,56},{48,64},{56,72},{64,... | collective-permute-start | bytes 491528 | tf_op jit(solution)/shard_map/ppermute | solution.py:818
  54.5 0.0 collective-permute-done.4.u_hi
  54.5 1.2 collective-permute-done.3.u_lo
  55.7 0.2 edges.1
  55.9 3.3 %collective-permute-done.1.from2 = f32[5,64,128]{2,1,0:T(8,128)S(1)} collective-permute-done((f32[5,64,128]{2,1,0:T(8,128)S(1)}, f32[5,64,128]{2,1,0:T(8,128)S(1)}, u32[]{:S(2)}, u32[]{:S(2)}) %collective-permute-start.1) | collective-permute-done | bytes 163872 | tf_op jit(solution)/shard_map/ppermute | solution.py:818
  59.2 0.2 join.1
  59.4 3.7 %collective-permute-start.5 = (f32[6,64,128]{2,1,0:T(8,128)S(1)}, f32[6,64,128]{2,1,0:T(8,128)S(1)}, u32[]{:S(2)}, u32[]{:S(2)}) collective-permute-start(f32[6,64,128]{2,1,0:T(8,128)S(1)} %get-tuple-element.22), channel_id=1, source_target_pairs={{0,1},{1,2},{2,3},{3,4},{4,5},{5,6},{6,7},{8,9},{9,10},{10,11},{11... | collective-permute-start | bytes 589832 | tf_op jit(solution)/shard_map/ppermute | solution.py:818
  63.1 1.9 %collective-permute-start.6 = (f32[6,64,128]{2,1,0:T(8,128)S(1)}, f32[6,64,128]{2,1,0:T(8,128)S(1)}, u32[]{:S(2)}, u32[]{:S(2)}) collective-permute-start(f32[6,64,128]{2,1,0:T(8,128)S(1)} %get-tuple-element.23), channel_id=1, source_target_pairs={{1,0},{2,1},{3,2},{4,3},{5,4},{6,5},{7,6},{9,8},{10,9},{11,10},{12... | collective-permute-start | bytes 589832 | tf_op jit(solution)/shard_map/ppermute | solution.py:818
  65.0 0.1 pad_add_fusion.place
  65.1 0.6 collective-permute-done.5.from_left
  65.7 4.4 %collective-permute-done.6.from_right = f32[6,64,128]{2,1,0:T(8,128)S(1)} collective-permute-done((f32[6,64,128]{2,1,0:T(8,128)S(1)}, f32[6,64,128]{2,1,0:T(8,128)S(1)}, u32[]{:S(2)}, u32[]{:S(2)}) %collective-permute-start.6) | collective-permute-done | bytes 196640 | tf_op jit(solution)/shard_map/ppermute | solution.py:818
  70.1 0.7 copy-done.2
  70.8 0.9 copy-done.3
  71.7 5.2 %before.1 = (f32[14,2,64,128]{3,2,1,0:T(8,128)S(1)}, f32[12,2,64,128]{3,2,1,0:T(8,128)S(1)}, f32[8,32,128]{2,1,0:T(8,128)S(1)}, f32[8,128]{1,0:T(8,128)S(1)}) custom-call(s32[2]{0:T(128)S(1)} %pad_add_fusion.place, f32[20,64,128]{2,1,0:T(8,128)S(1)} %get-tuple-element.21.f_in, f32[7,64,128]{2,1,0:T(8,128)S(1)} %collective-permute-done.3.u_lo, ...), custom_call_target="tpu_custom_call" | custom-call | tf_op jit(solution)/shard_map/before/pallas_call | solution.py:529
  76.9 0.0 copy-start.7
  76.9 0.8 broadcast_in_dim.2
  77.7 10.7 %all-to-all-start.1 = ((f32[128,8,128]{2,1,0:T(8,128)}), f32[128,8,128]{2,1,0:T(8,128)S(1)}, u32[]{:S(2)}, u32[]{:S(2)}) async-start(f32[128,8,128]{2,1,0:T(8,128)} %broadcast_in_dim.2), calls=%async_computation.1 | async-start | bytes 1048576 | tf_op jit(solution)/shard_map/all_to_all | solution.py:842
  88.5 1.3 %collective-permute-start.8 = (f32[3,32,128]{2,1,0:T(8,128)S(1)}, f32[3,32,128]{2,1,0:T(8,128)S(1)}, u32[]{:S(2)}, u32[]{:S(2)}) collective-permute-start(f32[3,32,128]{2,1,0:T(8,128)S(1)} %get-tuple-element.32), channel_id=1, source_target_pairs={{8,0},{16,8},{24,16},{32,24},{40,32},{48,40},{56,48},{64,56},{72,6... | collective-permute-start | bytes 147464 | tf_op jit(solution)/shard_map/ppermute | solution.py:818
  89.8 4.0 %collective-permute-start.7 = (f32[3,32,128]{2,1,0:T(8,128)S(1)}, f32[3,32,128]{2,1,0:T(8,128)S(1)}, u32[]{:S(2)}, u32[]{:S(2)}) collective-permute-start(f32[3,32,128]{2,1,0:T(8,128)S(1)} %get-tuple-element.33), channel_id=1, source_target_pairs={{0,8},{8,16},{16,24},{24,32},{32,40},{40,48},{48,56},{56,64},{64,7... | collective-permute-start | bytes 147464 | tf_op jit(solution)/shard_map/ppermute | solution.py:818
  93.8 3.4 %collective-permute-done.8.f1_hi = f32[3,32,128]{2,1,0:T(8,128)S(1)} collective-permute-done((f32[3,32,128]{2,1,0:T(8,128)S(1)}, f32[3,32,128]{2,1,0:T(8,128)S(1)}, u32[]{:S(2)}, u32[]{:S(2)}) %collective-permute-start.8) | collective-permute-done | bytes 49184 | tf_op jit(solution)/shard_map/ppermute | solution.py:818
  97.1 4.8 %all-to-all-done.1.got = f32[128,8,128]{2,1,0:T(8,128)S(1)} async-done(((f32[128,8,128]{2,1,0:T(8,128)}), f32[128,8,128]{2,1,0:T(8,128)S(1)}, u32[]{:S(2)}, u32[]{:S(2)}) %all-to-all-start.1) | async-done | bytes 524320 | tf_op jit(solution)/shard_map/all_to_all | solution.py:842
  102.0 7.4 %after.1 = (f32[8,64,128]{2,1,0:T(8,128)}, f32[128,128]{1,0:T(8,128)S(1)}) custom-call(s32[2]{0:T(128)S(1)} %pad_add_fusion.place, f32[128,8,128]{2,1,0:T(8,128)S(1)} %all-to-all-done.1.got, f32[128,128]{1,0:T(8,128)S(1)} %copy-done.7, f32[128,128]{1,0:T(8,128)S(1)} %copy-done.6, f32[128,128]{1,0:T(8,128)S(1)} %copy-done.5, f32[128,128]{1,0:T(8,128)S(1)} %copy-done.4, ...), custom_call_target="tpu_custom_call" | custom-call | tf_op jit(solution)/shard_map/after/pallas_call | solution.py:772
  109.4 16.2 %all_to_all.26 = f32[128,1,128]{2,1,0:T(1,128)} all-to-all(f32[128,1,128]{2,1,0:T(1,128)S(1)} %bitcast.19), channel_id=1, replica_groups=mesh['dom_0'=4,'dom_1'=4,'grp_0'=4,'grp_1'=2] {'dom_0','dom_1','grp_0','..., dimensions={0} | all-to-all | bytes 131072 | tf_op jit(solution)/shard_map/all_to_all | solution.py:844
  125.6 1.5 %stress.1 = f32[6]{0:T(128)} custom-call(f32[128,128]{1,0:T(8,128)} %bitcast.24), custom_call_target="tpu_custom_call" | custom-call | tf_op jit(solution)/shard_map/stress/pallas_call | solution.py:806
  (18 shorter events, 0.1 us)
Async XLA Ops:
  4.7 31.4 %copy-start.1 = (f32[8,64,128]{2,1,0:T(8,128)S(1)}, f32[8,64,128]{2,1,0:T(8,128)}, u32[]{:S(2)}) copy-start(f32[8,64,128]{2,1,0:T(8,128)} %param.12) | copy-start | bytes 786436
  36.1 6.9 %copy-start = (f32[8,64,128]{2,1,0:T(8,128)S(1)}, f32[8,64,128]{2,1,0:T(8,128)}, u32[]{:S(2)}) copy-start(f32[8,64,128]{2,1,0:T(8,128)} %start.3) | copy-start | bytes 786436
  40.9 18.3 %collective-permute-start = (f32[13,64,128]{2,1,0:T(8,128)S(1)}, f32[13,64,128]{2,1,0:T(8,128)S(1)}, u32[]{:S(2)}, u32[]{:S(2)}) collective-permute-start(f32[13,64,128]{2,1,0:T(8,128)S(1)} %bitcast.23), channel_id=1, source_target_pairs={{0,8},{8,16},{16,24},{24,32},{32,40},{40,48},{48,56},{56,64},{64,7... | collective-permute-start | bytes 1277960 | tf_op jit(solution)/shard_map/ppermute | solution.py:818
  43.1 11.4 %collective-permute-start.4 = (f32[7,64,128]{2,1,0:T(8,128)S(1)}, f32[7,64,128]{2,1,0:T(8,128)S(1)}, u32[]{:S(2)}, u32[]{:S(2)}) collective-permute-start(f32[7,64,128]{2,1,0:T(8,128)S(1)} %get-tuple-element.30), channel_id=1, source_target_pairs={{8,0},{16,8},{24,16},{32,24},{40,32},{48,40},{56,48},{64,56},{72,6... | collective-permute-start | bytes 688136 | tf_op jit(solution)/shard_map/ppermute | solution.py:818
  44.4 11.3 %collective-permute-start.3 = (f32[7,64,128]{2,1,0:T(8,128)S(1)}, f32[7,64,128]{2,1,0:T(8,128)S(1)}, u32[]{:S(2)}, u32[]{:S(2)}) collective-permute-start(f32[7,64,128]{2,1,0:T(8,128)S(1)} %get-tuple-element.31), channel_id=1, source_target_pairs={{0,8},{8,16},{16,24},{24,32},{32,40},{40,48},{48,56},{56,64},{64,7... | collective-permute-start | bytes 688136 | tf_op jit(solution)/shard_map/ppermute | solution.py:818
  48.4 10.8 %collective-permute-start.2 = (f32[6,64,128]{2,1,0:T(8,128)S(1)}, f32[6,64,128]{2,1,0:T(8,128)S(1)}, u32[]{:S(2)}, u32[]{:S(2)}) collective-permute-start(f32[6,64,128]{2,1,0:T(8,128)S(1)} %bitcast.20), channel_id=1, source_target_pairs={{8,0},{16,8},{24,16},{32,24},{40,32},{48,40},{56,48},{64,56},{72,6... | collective-permute-start | bytes 589832 | tf_op jit(solution)/shard_map/ppermute | solution.py:818
  49.7 9.5 %collective-permute-start.1 = (f32[5,64,128]{2,1,0:T(8,128)S(1)}, f32[5,64,128]{2,1,0:T(8,128)S(1)}, u32[]{:S(2)}, u32[]{:S(2)}) collective-permute-start(f32[5,64,128]{2,1,0:T(8,128)S(1)} %bitcast.21), channel_id=1, source_target_pairs={{0,16},{8,24},{16,32},{24,40},{32,48},{40,56},{48,64},{56,72},{64,... | collective-permute-start | bytes 491528 | tf_op jit(solution)/shard_map/ppermute | solution.py:818
  59.4 6.3 %collective-permute-start.5 = (f32[6,64,128]{2,1,0:T(8,128)S(1)}, f32[6,64,128]{2,1,0:T(8,128)S(1)}, u32[]{:S(2)}, u32[]{:S(2)}) collective-permute-start(f32[6,64,128]{2,1,0:T(8,128)S(1)} %get-tuple-element.22), channel_id=1, source_target_pairs={{0,1},{1,2},{2,3},{3,4},{4,5},{5,6},{6,7},{8,9},{9,10},{10,11},{11... | collective-permute-start | bytes 589832 | tf_op jit(solution)/shard_map/ppermute | solution.py:818
  63.1 7.0 %collective-permute-start.6 = (f32[6,64,128]{2,1,0:T(8,128)S(1)}, f32[6,64,128]{2,1,0:T(8,128)S(1)}, u32[]{:S(2)}, u32[]{:S(2)}) collective-permute-start(f32[6,64,128]{2,1,0:T(8,128)S(1)} %get-tuple-element.23), channel_id=1, source_target_pairs={{1,0},{2,1},{3,2},{4,3},{5,4},{6,5},{7,6},{9,8},{10,9},{11,10},{12... | collective-permute-start | bytes 589832 | tf_op jit(solution)/shard_map/ppermute | solution.py:818
  70.1 0.7 copy-start.2
  70.8 0.9 copy-start.3
  76.8 25.1 %copy-start.4 = (f32[128,128]{1,0:T(8,128)S(1)}, f32[128,128]{1,0:T(8,128)}, u32[]{:S(2)}) copy-start(f32[128,128]{1,0:T(8,128)} %constant.30.clone.scale) | copy-start | bytes 196612
  76.9 25.1 %copy-start.5 = (f32[128,128]{1,0:T(8,128)S(1)}, f32[128,128]{1,0:T(8,128)}, u32[]{:S(2)}) copy-start(f32[128,128]{1,0:T(8,128)} %constant.29.clone.tz) | copy-start | bytes 196612
  76.9 25.1 %copy-start.6 = (f32[128,128]{1,0:T(8,128)S(1)}, f32[128,128]{1,0:T(8,128)}, u32[]{:S(2)}) copy-start(f32[128,128]{1,0:T(8,128)} %constant.28.clone.txy_t) | copy-start | bytes 196612
  76.9 25.1 %copy-start.7 = (f32[128,128]{1,0:T(8,128)S(1)}, f32[128,128]{1,0:T(8,128)}, u32[]{:S(2)}) copy-start(f32[128,128]{1,0:T(8,128)} %constant.27.clone.txy) | copy-start | bytes 196612
  77.7 24.3 %all-to-all-start.1 = ((f32[128,8,128]{2,1,0:T(8,128)}), f32[128,8,128]{2,1,0:T(8,128)S(1)}, u32[]{:S(2)}, u32[]{:S(2)}) async-start(f32[128,8,128]{2,1,0:T(8,128)} %broadcast_in_dim.2), calls=%async_computation.1 | async-start | bytes 1048576 | tf_op jit(solution)/shard_map/all_to_all | solution.py:842
  88.5 8.7 %collective-permute-start.8 = (f32[3,32,128]{2,1,0:T(8,128)S(1)}, f32[3,32,128]{2,1,0:T(8,128)S(1)}, u32[]{:S(2)}, u32[]{:S(2)}) collective-permute-start(f32[3,32,128]{2,1,0:T(8,128)S(1)} %get-tuple-element.32), channel_id=1, source_target_pairs={{8,0},{16,8},{24,16},{32,24},{40,32},{48,40},{56,48},{64,56},{72,6... | collective-permute-start | bytes 147464 | tf_op jit(solution)/shard_map/ppermute | solution.py:818
  89.8 7.4 %collective-permute-start.7 = (f32[3,32,128]{2,1,0:T(8,128)S(1)}, f32[3,32,128]{2,1,0:T(8,128)S(1)}, u32[]{:S(2)}, u32[]{:S(2)}) collective-permute-start(f32[3,32,128]{2,1,0:T(8,128)S(1)} %get-tuple-element.33), channel_id=1, source_target_pairs={{0,8},{8,16},{16,24},{24,32},{32,40},{40,48},{48,56},{56,64},{64,7... | collective-permute-start | bytes 147464 | tf_op jit(solution)/shard_map/ppermute | solution.py:818

commit v4 on v3

--- a/solution.py
+++ b/solution.py
@@ -113,8 +113,8 @@
         copy.wait()
     lane = lanes_of((TILE_ROWS, LANES))
     need = rows_of((TILE_ROWS, LANES)) + jnp.where(lane < 64, 0, 4)
-    need = jnp.maximum(jnp.maximum(need, (lane // 8) % 8), lane % 8)
-    tile_c = lane % 8
+    need = jnp.maximum(jnp.maximum(need, (lane >> 3) & 7), lane & 7)
+    tile_c = lane & 7
     part1, slot1 = lanes_of((1, LANES)) & 3, lanes_of((1, LANES)) >> 2
 
     for start in range(0, ATOMS, PER_STEP):
@@ -194,7 +194,7 @@
     lax.fori_loop(0, YB * ZB, clear, 0, unroll=4)
     copy.wait()
     lane = lanes_of((8, LANES))
-    z_of = lane % 8
+    z_of = lane & 7
 
     for src in range(NDEV):
         for k in range(CAP):
@@ -217,7 +217,7 @@
             acc[pl.ds(row + 16, 8), :] = a1 + jnp.where(near, 0.0, here)
             acc[pl.ds(wrapped, 8), :] = a2 + jnp.where(near, round_, 0.0)
             acc[pl.ds(wrapped + 16, 8), :] = a3 + jnp.where(near, 0.0, round_)
-    group = lane // 8
+    group = lane >> 3
 
     def lay_out(yb, c):
         for xg in range(2):
@@ -264,7 +264,6 @@
 HU, HF = 7, 6
 NU_, NF = CX + 2 * HU, CX + 2 * HF
 UGROUPS, FGROUPS = -(-NU_ // 8), -(-NF // 8)
-ZGROUPS = UGROUPS + FGROUPS
 
 
 def u_plane(p, u_lo, start, u_hi):
@@ -274,7 +273,7 @@
 
 
 def pack_edges(planes, left, right, at):
-    slot = lanes_of((CY, LANES)) // 16
+    slot = lanes_of((CY, LANES)) >> 4
     for g in range(-(-len(planes) // 8)):
         lo = jnp.zeros((CY, LANES), F32)
         hi = jnp.zeros((CY, LANES), F32)
@@ -304,9 +303,7 @@
     )(start, u_lo, u_hi)
 
 
-def join_kernel(grid, from1, from2, above, u_left, u_right, f, left, right):
-    left[0:UGROUPS] = u_left[...]
-    right[0:UGROUPS] = u_right[...]
+def join_kernel(grid, from1, from2, above, f, left, right):
     for p in range(NF):
         x = p - HF
         if x < 0:
@@ -322,7 +319,7 @@
             if x < 15:
                 total = total + grid[x * CY : (x + 1) * CY, :]
         f[p] = total
-    pack_edges([functools.partial(lambda q: f[q], p) for p in range(NF)], left, right, UGROUPS)
+    pack_edges([functools.partial(lambda q: f[q], p) for p in range(NF)], left, right, 0)
 
 
 def join(*args):
@@ -330,10 +327,10 @@
         join_kernel,
         out_shape=(
             sds(NF, CY, LANES),
-            sds(ZGROUPS, CY, LANES),
-            sds(ZGROUPS, CY, LANES),
+            sds(FGROUPS, CY, LANES),
+            sds(FGROUPS, CY, LANES),
         ),
-        in_specs=[VM] * 6,
+        in_specs=[VM] * 4,
         out_specs=(VM,) * 3,
         compiler_params=PAR,
         name="join",
@@ -370,19 +367,19 @@
 def halves(n):
     r = lax.broadcasted_iota(I32, (n, 2 * n), 0)
     c = lax.broadcasted_iota(I32, (n, 2 * n), 1)
-    return ((c // 2) == r).astype(F32)
+    return ((c >> 1) == r).astype(F32)
 
 
 def doubles(n):
     r = lax.broadcasted_iota(I32, (2 * n, n), 0)
     c = lax.broadcasted_iota(I32, (2 * n, n), 1)
-    return ((r // 2) == c).astype(F32)
+    return ((r >> 1) == c).astype(F32)
 
 
 def lane_halves(n):
     r = lax.broadcasted_iota(I32, (2 * n, n), 0)
     c = lax.broadcasted_iota(I32, (2 * n, n), 1)
-    return ((r // 2) == c).astype(F32)
+    return ((r >> 1) == c).astype(F32)
 
 
 STEP = CY + 16
@@ -392,19 +389,25 @@
     return (p * 2 + h) * STEP
 
 
-def whole(ref, p, h):
-    return ref[pl.ds(pl.multiple_of(half_at(p, h) + 8, 8), CY), :]
-
-
-def put(ref, p, h, value):
+PART = 32
+
+
+def whole(ref, p, h, row=0, n=CY):
+    return ref[pl.ds(pl.multiple_of(half_at(p, h) + 8 + row, 8), n), :]
+
+
+def put(ref, p, h, value, row=0):
     base = half_at(p, h)
-    ref[pl.ds(pl.multiple_of(base + 8, 8), CY), :] = value
-    ref[pl.ds(pl.multiple_of(base, 8), 8), :] = value[CY - 8 :]
-    ref[pl.ds(pl.multiple_of(base + 8 + CY, 8), 8), :] = value[:8]
-
-
-def moved(ref, p, h, by):
-    return ref[pl.ds(half_at(p, h) + 8 + by, CY), :]
+    n = value.shape[0]
+    ref[pl.ds(pl.multiple_of(base + 8 + row, 8), n), :] = value
+    if row + n == CY:
+        ref[pl.ds(pl.multiple_of(base, 8), 8), :] = value[n - 8 :]
+    if row == 0:
+        ref[pl.ds(pl.multiple_of(base + 8 + CY, 8), 8), :] = value[:8]
+
+
+def moved(ref, p, h, by, row=0, n=CY):
+    return ref[pl.ds(half_at(p, h) + 8 + row + by, n), :]
 
 
 def z_sides(own, edge):
@@ -418,25 +421,36 @@
     )
 
 
-def beside0(ref, p):
-    centre = [whole(ref, p, h) for h in range(2)]
+def beside0(ref, p, row):
+    centre = [whole(ref, p, h, row, PART) for h in range(2)]
     sides = z_sides(*centre)
     around = [
-        (whole(ref, p + 1, h) + whole(ref, p - 1, h))
-        + (moved(ref, p, h, 1) + moved(ref, p, h, -1))
+        (whole(ref, p + 1, h, row, PART) + whole(ref, p - 1, h, row, PART))
+        + (moved(ref, p, h, 1, row, PART) + moved(ref, p, h, -1, row, PART))
         + (sides[h][0] + sides[h][1])
         for h in range(2)
     ]
     return centre, around
 
 
+def sweep0(src, dst, f, p, shift_u, shift_f, mask, ok):
+    for row in range(0, CY, PART):
+        centre, around = beside0(src, p + shift_u, row)
+        for h in range(2):
+            new = 3.0 * centre[h] + around[h] + f(p + shift_f, h, row)
+            put(dst, p, h, new * (mask[h] * ok), row)
+
+
 def before_kernel(
-    place, f_in, u_lo, start, u_hi, from_left, from_right, u_out, f_out, f1, chunk, u, ua, fe, u2, pairs, v1, r1
+    place, f_in, u_lo, start, u_hi, u_from_left, u_from_right, f_from_left, f_from_right, u_out, f_out, f1, chunk, u, ua, fe, u2, pairs, v1, r1
 ):
     dom, grp = place[0], place[1]
-    slot = lanes_of((CY, LANES)) // 16
+    slot = lanes_of((CY, LANES)) >> 4
     for p in range(NU_ + NF):
-        g, k = (p // 8, p % 8) if p < NU_ else (UGROUPS + (p - NU_) // 8, (p - NU_) % 8)
+        if p < NU_:
+            g, k, from_left, from_right = p // 8, p % 8, u_from_left, u_from_right
+        else:
+            g, k, from_left, from_right = (p - NU_) // 8, (p - NU_) % 8, f_from_left, f_from_right
         edge = jnp.where(slot == k, from_right[g], 0.0)
         edge = jnp.where(slot == (k - 1) % 8, from_left[g], edge)
         edge = pltpu.roll(edge, (-16 * k) % 128, 1) if k else edge
@@ -446,23 +460,21 @@
         else:
             fe[p - NU_] = edge
     f = (f_in, fe)
+
+    def source(p, h, row):
+        return f[h][p, row : row + PART, :]
+
     mask = z_mask(W0, CZ, grp, NGRP * CZ) * (1.0 / 9.0)
     mask = (mask[:, :LANES], mask[:, LANES:])
 
     def sweep1(p, c):
-        centre, around = beside0(u, p + 1)
-        ok = x_ok(dom * CX + p - HF, NDOM * CX)
-        for h in range(2):
-            put(ua, p, h, (3.0 * centre[h] + around[h] + f[h][p]) * (mask[h] * ok))
+        sweep0(u, ua, source, p, 1, 0, mask, x_ok(dom * CX + p - HF, NDOM * CX))
         return c
 
     lax.fori_loop(0, NF, sweep1, 0, unroll=4)
 
     def sweep2(p, c):
-        centre, around = beside0(ua, p + 1)
-        ok = x_ok(dom * CX + p - 5, NDOM * CX)
-        for h in range(2):
-            put(u2, p, h, (3.0 * centre[h] + around[h] + f[h][p + 1]) * (mask[h] * ok))
+        sweep0(ua, u2, source, p, 1, 1, mask, x_ok(dom * CX + p - 5, NDOM * CX))
         return c
 
     lax.fori_loop(0, NF - 2, sweep2, 0, unroll=3)
@@ -475,15 +487,17 @@
             f_out[p, h] = f[h][p + 4]
 
     def residue0(q, c):
-        total = [None, None]
-        for i in range(2):
-            p = 2 * q + i + 1
-            centre, around = beside0(u2, p)
+        for row in range(0, CY, PART):
+            total = [None, None]
+            for i in range(2):
+                p = 2 * q + i + 1
+                centre, around = beside0(u2, p, row)
+                for h in range(2):
+                    r = source(p + 1, h, row) - (6.0 * centre[h] - around[h])
+                    total[h] = r if total[h] is None else total[h] + r
+            at = pl.ds(pl.multiple_of(q * CY + row, 8), PART)
             for h in range(2):
-                r = f[h][p + 1] - (6.0 * centre[h] - around[h])
-                total[h] = r if total[h] is None else total[h] + r
-        for h in range(2):
-            pairs[pl.ds(pl.multiple_of(q * CY, CY), CY), h * LANES : (h + 1) * LANES] = total[h]
+                pairs[at, h * LANES : (h + 1) * LANES] = total[h]
         return c
 
     lax.fori_loop(0, 8, residue0, 0, unroll=2)
@@ -497,7 +511,7 @@
         v1[q] = f1[q] * (4.0 / 9.0)
     for q in range(1, 7):
         centre, around = beside(v1, q)
-        new = (3.0 * centre + around + 4.0 * f1[q]) * (1.0 / 9.0)
+        new = centre * (4.0 / 3.0) + around * (1.0 / 9.0)
         r1[q] = new * (mask1 * x_ok(dom * X1 + q - 2, NDOM * X1))
     half_y2 = halves(Y2) * 0.125
     lane_half = lane_halves(LANES // 2)
@@ -512,7 +526,7 @@
         rows.append(total)
     both = dot_right(jnp.concatenate(rows, axis=0), jnp.concatenate([lane_half, jnp.zeros_like(lane_half)], axis=1))
     packed = jnp.zeros((8, LANES), F32)
-    slot = lanes_of((8, LANES)) // 32
+    slot = lanes_of((8, LANES)) >> 5
     for i in range(2):
         part = dot_left(half_y2, both[i * Y1 : (i + 1) * Y1, :])
         for yb in range(2):
@@ -525,7 +539,7 @@
     chunk[...] = packed
 
 
-def before(place, f, u_lo, start, u_hi, from_left, from_right):
+def before(place, *args):
     return pl.pallas_call(
         before_kernel,
         out_shape=(
@@ -534,7 +548,7 @@
             sds(8, Y1, LANES),
             sds(8, LANES),
         ),
-        in_specs=[SM] + [VM] * 6,
+        in_specs=[SM] + [VM] * 8,
         out_specs=(VM,) * 4,
         scratch_shapes=[
             pltpu.VMEM((NU_ * 2 * STEP, LANES), F32),
@@ -547,7 +561,7 @@
         ],
         compiler_params=PAR,
         name="before",
-    )(place, f, u_lo, start, u_hi, from_left, from_right)
+    )(place, *args)
 
 
 NX2, NZ2 = NDOM * X2, NGRP * Z2
@@ -595,7 +609,7 @@
         w[PAD2 + NX2 + p] = zero2
         r[p] = zero2
         r[PAD2 + NX2 + p] = zero2
-    slot = lanes_of((8, LANES)) // 32
+    slot = lanes_of((8, LANES)) >> 5
 
     def gather(d, c):
         for i in range(2):
@@ -633,7 +647,7 @@
 
     def sweep2(p, c):
         centre, around = beside2(w, PAD2 + p)
-        r[PAD2 + p] = (3.0 * centre + around + 16.0 * g[PAD2 + p]) * (1.0 / 9.0)
+        r[PAD2 + p] = centre * (4.0 / 3.0) + around * (1.0 / 9.0)
         return c
 
     lax.fori_loop(0, NX2, sweep2, 0, unroll=8)
@@ -653,13 +667,13 @@
     n3 = NX3 * NY3
     ri = lax.broadcasted_iota(I32, (n3, 2 * n3), 0)
     ci = lax.broadcasted_iota(I32, (n3, 2 * n3), 1)
-    source = dot_left(((ci // 2) == ri).astype(F32) * 0.125, z_sums)
+    source = dot_left(((ci >> 1) == ri).astype(F32) * 0.125, z_sums)
     modes = dot3(dot3(txy_t[...], source), tz[...]) * scale[...]
     solved = dot3(txy[...], dot3(modes, tz[...]))
     rr = lax.broadcasted_iota(I32, (NZ3, NZ2), 0)
     cc = lax.broadcasted_iota(I32, (NZ3, NZ2), 1)
-    wide = dot_right(solved, ((cc // 2) == rr).astype(F32))
-    tall = dot_left(((lax.broadcasted_iota(I32, (2 * n3, n3), 0) // 2) == lax.broadcasted_iota(I32, (2 * n3, n3), 1)).astype(F32), wide)
+    wide = dot_right(solved, ((cc >> 1) == rr).astype(F32))
+    tall = dot_left(((lax.broadcasted_iota(I32, (2 * n3, n3), 0) >> 1) == lax.broadcasted_iota(I32, (2 * n3, n3), 1)).astype(F32), wide)
     f3[...] = tall
 
     def add_coarse(q, c):
@@ -682,7 +696,7 @@
     post2(w, r, 6, 2)
     lane = lanes_of((NZ2, LANES))
     signed = jnp.where(lane < 96, lane, lane - LANES)
-    place_z = ((grp * Z1 + signed + 2 * NZ2) // 2 - NZ2 == rows_of((NZ2, LANES))).astype(F32)
+    place_z = ((grp * Z1 + signed) >> 1 == rows_of((NZ2, LANES))).astype(F32)
     f1[0:3] = f1_lo[...]
     f1[3:11] = f1_own[...]
     f1[11:14] = f1_hi[...]
@@ -698,7 +712,7 @@
     fine = [tall2[p * Y1 : (p + 1) * Y1, :] for p in range(6)]
     for p in range(1, 13):
         centre, around = beside(b1, p)
-        new = (3.0 * centre + around + 4.0 * f1[p]) * (1.0 / 9.0)
+        new = centre * (4.0 / 3.0) + around * (1.0 / 9.0)
         a1[p] = new * ok1(p) + fine[(p - 1) // 2] * mask1
     for p in range(2, 12):
         centre, around = beside(a1, p)
@@ -710,7 +724,7 @@
         )
     r0 = lax.broadcasted_iota(I32, (LANES, W0), 0)
     c0 = lax.broadcasted_iota(I32, (LANES, W0), 1)
-    spread0 = dot_right(s1[...], ((c0 // 2) == r0).astype(F32))
+    spread0 = dot_right(s1[...], ((c0 >> 1) == r0).astype(F32))
     double_y0 = doubles(Y1)
     for q in range(8):
         ext[q] = dot_left(double_y0, spread0[q * Y1 : (q + 1) * Y1, :])
@@ -718,28 +732,25 @@
     mask = (mask[:, :LANES], mask[:, LANES:])
     mask9 = [m * (1.0 / 9.0) for m in mask]
 
+    def source(p, h, row):
+        return f[p, h, row : row + PART, :]
+
     def add_fine(p, c):
         for h in range(2):
-            fine0 = ext[(p + 1) // 2, :, h * LANES : (h + 1) * LANES]
+            fine0 = ext[(p + 1) >> 1, :, h * LANES : (h + 1) * LANES]
             put(e, p, h, u2[p, h] + fine0 * mask[h])
         return c
 
     lax.fori_loop(0, 14, add_fine, 0, unroll=2)
 
     def last1(p, c):
-        centre, around = beside0(e, p + 1)
-        ok = x_ok(dom * CX + p - 2, NDOM * CX)
-        for h in range(2):
-            put(e2, p, h, (3.0 * centre[h] + around[h] + f[p, h]) * (mask9[h] * ok))
+        sweep0(e, e2, source, p, 1, 0, mask9, x_ok(dom * CX + p - 2, NDOM * CX))
         return c
 
     lax.fori_loop(0, 12, last1, 0, unroll=4)
 
     def last2(p, c):
-        centre, around = beside0(e2, p + 1)
-        ok = x_ok(dom * CX + p - 1, NDOM * CX)
-        for h in range(2):
-            put(e, p, h, (3.0 * centre[h] + around[h] + f[p + 1, h]) * (mask9[h] * ok))
+        sweep0(e2, e, source, p, 1, 1, mask9, x_ok(dom * CX + p - 1, NDOM * CX))
         return c
 
     lax.fori_loop(0, 10, last2, 0, unroll=5)
@@ -759,7 +770,7 @@
         )
 
     zero = jnp.zeros((8, LANES), F32)
-    parts = lax.fori_loop(0, CX, sums, (zero,) * 7, unroll=2)
+    parts = lax.fori_loop(0, CX, sums, (zero,) * 7, unroll=4)
     lane8 = lanes_of((1, LANES))
     line = jnp.zeros((1, LANES), F32)
     for i, part in enumerate(parts):
@@ -830,12 +841,16 @@
     from1 = shift(grid[2 * CY : 15 * CY].reshape(13, CY, LANES), DOM, 1)
     from2 = shift(up2.reshape(5, CY, LANES), DOM, 2)
     above = shift(down.reshape(6, CY, LANES), DOM, -1)
+    u_from_right = shift(u_left, GRP, -1)
+    u_from_left = shift(u_right, GRP, 1)
     f, left, right = join(
-        grid, from1, from2, above, u_left, u_right
+        grid, from1, from2, above
     )
     from_right = shift(left, GRP, -1)
     from_left = shift(right, GRP, 1)
-    u2, fe, f1, chunk = before(place, f, lower, start, upper, from_left, from_right)
+    u2, fe, f1, chunk = before(
+        place, f, lower, start, upper, u_from_left, u_from_right, from_left, from_right
+    )
     f1_lo = shift(f1[1:4], DOM, 1)
     f1_hi = shift(f1[4:7], DOM, -1)
     chunks = jnp.broadcast_to(chunk[None], (NDEV, 8, LANES))

time: 128 us -> 126 us (0.984)
  starting transfers between devices: 35 us -> 39.4 us
  waiting for transfers between devices: 17.7 us -> 13.3 us
  local copies, waits for them, and re-layouts: 2.55 us -> 0.95 us
    ppermute x9 -> x11, starting transfers between devices: 24.3 us -> 30.9 us  [shift(): return lax.ppermute(value, axis, route)]
    ppermute x9 -> x11, waiting for transfers between devices: 12.8 us -> 8.5 us  [shift(): return lax.ppermute(value, axis, route)]
    all_to_all x1, starting transfers between devices: 10.7 us -> 8.56 us  [step(): everything = lax.all_to_all(chunks, ALL, 0, 0, tiled=True)]
    unnamed x16 -> x12, local copies, waits for them, and re-layouts: 1.64 us -> 0.04 us
  transfers between devices with their start and end apart: 10 -> 12, of which waited for: 6 -> 4; matrix products, arithmetic and copies ran while one was open for 0% -> 0% of each run, Pallas kernels for 0% -> 0%
where the time goes in v4:
time: 126 us; the launch traced here: 125 us
  blocking collectives  47.6 us (38%)
  starting transfers between devices  39.4 us (31%)
  Pallas kernels  22.9 us (18%)
  waiting for transfers between devices  13.3 us (11%)
    all_to_all x1, blocking collectives, step(): lax.all_to_all(message.reshape(NDEV, ROWS * LANES), ALL, 0, 0, tiled=True)  31.4 us
    ppermute x11, starting transfers between devices, shift(): return lax.ppermute(value, axis, route)  30.9 us
    all_to_all x1, blocking collectives, step(): sums = lax.all_to_all(totals, ALL, 0, 0, tiled=True)  16.2 us
    all_to_all x1, starting transfers between devices, step(): everything = lax.all_to_all(chunks, ALL, 0, 0, tiled=True)  8.56 us
    ppermute x11, waiting for transfers between devices, shift(): return lax.ppermute(value, axis, route)  8.5 us
    pallas_call x1, Pallas kernels, after(): pl.pallas_call(after_kernel, out_shape=(sds(CX, CY, CZ), sds(NDEV, LANES)...  7.11 us
    pallas_call x1, Pallas kernels, before(): pl.pallas_call(before_kernel, out_shape=(sds(14, 2, CY, LANES), sds(12, 2...  5.02 us
    all_to_all x1, waiting for transfers between devices, step(): everything = lax.all_to_all(chunks, ALL, 0, 0, tiled=True)  4.85 us
  transfers between devices with their start and end apart: 12, of which 4 were waited for; matrix products, arithmetic and copies ran while one was open for 0% of the time, Pallas kernels for 0%

profile of v4, /device:TPU:1, one launch (start us, length us, event | category | flops | bytes accessed | tf_op | source)
XLA Modules:
  0.0 125.1 jit_solution(14471823861130574748)
XLA Ops:
  0.6 4.1 %pack_atoms.1 = f32[2176,128]{1,0:T(8,128)} custom-call(s32[256]{0:T(256)} %bitcast.25, s32[256]{0:T(256)} %bitcast.26, s32[256]{0:T(256)} %bitcast.27, s32[256]{0:T(256)} %bitcast.28, s32[256]{0:T(256)} %bitcast.29, f32[256,512]{1,0:T(8,128)} %tiles_h.1), custom_call_target="tpu_custom_call" | custom-call | tf_op jit(solution)/shard_map/pack_atoms/pallas_call | solution.py:146
  4.7 0.0 copy-start.1
  4.7 31.4 %all_to_all.25 = f32[128,1,2176]{2,1,0:T(1,128)S(1)} all-to-all(f32[128,1,2176]{2,1,0:T(1,128)} %bitcast.22), channel_id=1, replica_groups=mesh['dom_0'=4,'dom_1'=4,'grp_0'=4,'grp_1'=2] {'dom_0','dom_1','grp_0','..., dimensions={0} | all-to-all | bytes 2228224 | tf_op jit(solution)/shard_map/all_to_all | solution.py:837
  36.1 4.8 %deposit.1 = (f32[1024,128]{1,0:T(8,128)S(1)}, f32[320,128]{1,0:T(8,128)S(1)}, f32[384,128]{1,0:T(8,128)S(1)}) custom-call(f32[2176,128]{1,0:T(8,128)S(1)} %bitcast.17, f32[512,128]{1,0:T(8,128)S(1)} %bitcast.18), custom_call_target="tpu_custom_call" | custom-call | tf_op jit(solution)/shard_map/deposit/pallas_call | solution.py:246
  40.9 2.1 %collective-permute-start = (f32[13,64,128]{2,1,0:T(8,128)S(1)}, f32[13,64,128]{2,1,0:T(8,128)S(1)}, u32[]{:S(2)}, u32[]{:S(2)}) collective-permute-start(f32[13,64,128]{2,1,0:T(8,128)S(1)} %bitcast.23), channel_id=1, source_target_pairs={{0,8},{8,16},{16,24},{24,32},{32,40},{40,48},{48,56},{56,64},{64,7... | collective-permute-start | bytes 1277960 | tf_op jit(solution)/shard_map/ppermute | solution.py:829
  43.1 1.3 %collective-permute-start.4 = (f32[7,64,128]{2,1,0:T(8,128)S(1)}, f32[7,64,128]{2,1,0:T(8,128)S(1)}, u32[]{:S(2)}, u32[]{:S(2)}) collective-permute-start(f32[7,64,128]{2,1,0:T(8,128)S(1)} %get-tuple-element.30), channel_id=1, source_target_pairs={{8,0},{16,8},{24,16},{32,24},{40,32},{48,40},{56,48},{64,56},{72,6... | collective-permute-start | bytes 688136 | tf_op jit(solution)/shard_map/ppermute | solution.py:829
  44.4 4.0 %collective-permute-start.3 = (f32[7,64,128]{2,1,0:T(8,128)S(1)}, f32[7,64,128]{2,1,0:T(8,128)S(1)}, u32[]{:S(2)}, u32[]{:S(2)}) collective-permute-start(f32[7,64,128]{2,1,0:T(8,128)S(1)} %get-tuple-element.31), channel_id=1, source_target_pairs={{0,8},{8,16},{16,24},{24,32},{32,40},{40,48},{48,56},{56,64},{64,7... | collective-permute-start | bytes 688136 | tf_op jit(solution)/shard_map/ppermute | solution.py:829
  48.4 1.3 %collective-permute-start.2 = (f32[6,64,128]{2,1,0:T(8,128)S(1)}, f32[6,64,128]{2,1,0:T(8,128)S(1)}, u32[]{:S(2)}, u32[]{:S(2)}) collective-permute-start(f32[6,64,128]{2,1,0:T(8,128)S(1)} %bitcast.20), channel_id=1, source_target_pairs={{8,0},{16,8},{24,16},{32,24},{40,32},{48,40},{56,48},{64,56},{72,6... | collective-permute-start | bytes 589832 | tf_op jit(solution)/shard_map/ppermute | solution.py:829
  49.7 4.8 %collective-permute-start.1 = (f32[5,64,128]{2,1,0:T(8,128)S(1)}, f32[5,64,128]{2,1,0:T(8,128)S(1)}, u32[]{:S(2)}, u32[]{:S(2)}) collective-permute-start(f32[5,64,128]{2,1,0:T(8,128)S(1)} %bitcast.21), channel_id=1, source_target_pairs={{0,16},{8,24},{16,32},{24,40},{32,48},{40,56},{48,64},{56,72},{64,... | collective-permute-start | bytes 491528 | tf_op jit(solution)/shard_map/ppermute | solution.py:829
  54.5 0.0 collective-permute-done.4.u_hi
  54.5 1.2 collective-permute-done.3.u_lo
  55.7 0.2 edges.1
  55.9 4.6 %collective-permute-start.5 = (f32[3,64,128]{2,1,0:T(8,128)S(1)}, f32[3,64,128]{2,1,0:T(8,128)S(1)}, u32[]{:S(2)}, u32[]{:S(2)}) collective-permute-start(f32[3,64,128]{2,1,0:T(8,128)S(1)} %get-tuple-element.20), channel_id=1, source_target_pairs={{0,1},{1,2},{2,3},{3,4},{4,5},{5,6},{6,7},{8,9},{9,10},{10,11},{11... | collective-permute-start | bytes 294920 | tf_op jit(solution)/shard_map/ppermute | solution.py:829
  60.6 2.6 %collective-permute-start.6 = (f32[3,64,128]{2,1,0:T(8,128)S(1)}, f32[3,64,128]{2,1,0:T(8,128)S(1)}, u32[]{:S(2)}, u32[]{:S(2)}) collective-permute-start(f32[3,64,128]{2,1,0:T(8,128)S(1)} %get-tuple-element.21), channel_id=1, source_target_pairs={{1,0},{2,1},{3,2},{4,3},{5,4},{6,5},{7,6},{9,8},{10,9},{11,10},{12... | collective-permute-start | bytes 294920 | tf_op jit(solution)/shard_map/ppermute | solution.py:829
  63.1 0.0 collective-permute-done.2.above
  63.1 0.0 collective-permute-done.from1
  63.1 0.2 join.1
  63.4 3.0 %collective-permute-start.7 = (f32[3,64,128]{2,1,0:T(8,128)S(1)}, f32[3,64,128]{2,1,0:T(8,128)S(1)}, u32[]{:S(2)}, u32[]{:S(2)}) collective-permute-start(f32[3,64,128]{2,1,0:T(8,128)S(1)} %get-tuple-element.22), channel_id=1, source_target_pairs={{0,1},{1,2},{2,3},{3,4},{4,5},{5,6},{6,7},{8,9},{9,10},{10,11},{11... | collective-permute-start | bytes 294920 | tf_op jit(solution)/shard_map/ppermute | solution.py:829
  66.4 1.9 %collective-permute-start.8 = (f32[3,64,128]{2,1,0:T(8,128)S(1)}, f32[3,64,128]{2,1,0:T(8,128)S(1)}, u32[]{:S(2)}, u32[]{:S(2)}) collective-permute-start(f32[3,64,128]{2,1,0:T(8,128)S(1)} %get-tuple-element.23), channel_id=1, source_target_pairs={{1,0},{2,1},{3,2},{4,3},{5,4},{6,5},{7,6},{9,8},{10,9},{11,10},{12... | collective-permute-start | bytes 294920 | tf_op jit(solution)/shard_map/ppermute | solution.py:829
  68.3 0.1 pad_add_fusion.place
  68.4 3.9 %collective-permute-done.8.f_from_right = f32[3,64,128]{2,1,0:T(8,128)S(1)} collective-permute-done((f32[3,64,128]{2,1,0:T(8,128)S(1)}, f32[3,64,128]{2,1,0:T(8,128)S(1)}, u32[]{:S(2)}, u32[]{:S(2)}) %collective-permute-start.8) | collective-permute-done | bytes 98336 | tf_op jit(solution)/shard_map/ppermute | solution.py:829
  72.3 5.0 %before.1 = (f32[14,2,64,128]{3,2,1,0:T(8,128)S(1)}, f32[12,2,64,128]{3,2,1,0:T(8,128)S(1)}, f32[8,32,128]{2,1,0:T(8,128)S(1)}, f32[8,128]{1,0:T(8,128)S(1)}) custom-call(s32[2]{0:T(128)S(1)} %pad_add_fusion.place, f32[20,64,128]{2,1,0:T(8,128)S(1)} %get-tuple-element.19.f_in, f32[7,64,128]{2,1,0:T(8,128)S(1)} %collective-permute-done.3.u_lo, ...), custom_call_target="tpu_custom_call" | custom-call | tf_op jit(solution)/shard_map/before/pallas_call | solution.py:543
  77.3 0.0 copy-start.5
  77.4 0.8 broadcast_in_dim.2
  78.2 8.6 %all-to-all-start.1 = ((f32[128,8,128]{2,1,0:T(8,128)}), f32[128,8,128]{2,1,0:T(8,128)S(1)}, u32[]{:S(2)}, u32[]{:S(2)}) async-start(f32[128,8,128]{2,1,0:T(8,128)} %broadcast_in_dim.2), calls=%async_computation.1 | async-start | bytes 1048576 | tf_op jit(solution)/shard_map/all_to_all | solution.py:857
  86.8 1.3 %collective-permute-start.10 = (f32[3,32,128]{2,1,0:T(8,128)S(1)}, f32[3,32,128]{2,1,0:T(8,128)S(1)}, u32[]{:S(2)}, u32[]{:S(2)}) collective-permute-start(f32[3,32,128]{2,1,0:T(8,128)S(1)} %get-tuple-element.32), channel_id=1, source_target_pairs={{8,0},{16,8},{24,16},{32,24},{40,32},{48,40},{56,48},{64,56},{72,6... | collective-permute-start | bytes 147464 | tf_op jit(solution)/shard_map/ppermute | solution.py:829
  88.1 4.0 %collective-permute-start.9 = (f32[3,32,128]{2,1,0:T(8,128)S(1)}, f32[3,32,128]{2,1,0:T(8,128)S(1)}, u32[]{:S(2)}, u32[]{:S(2)}) collective-permute-start(f32[3,32,128]{2,1,0:T(8,128)S(1)} %get-tuple-element.33), channel_id=1, source_target_pairs={{0,8},{8,16},{16,24},{24,32},{32,40},{40,48},{48,56},{56,64},{64,7... | collective-permute-start | bytes 147464 | tf_op jit(solution)/shard_map/ppermute | solution.py:829
  92.1 3.4 %collective-permute-done.10.f1_hi = f32[3,32,128]{2,1,0:T(8,128)S(1)} collective-permute-done((f32[3,32,128]{2,1,0:T(8,128)S(1)}, f32[3,32,128]{2,1,0:T(8,128)S(1)}, u32[]{:S(2)}, u32[]{:S(2)}) %collective-permute-start.10) | collective-permute-done | bytes 49184 | tf_op jit(solution)/shard_map/ppermute | solution.py:829
  95.5 4.8 %all-to-all-done.1.got = f32[128,8,128]{2,1,0:T(8,128)S(1)} async-done(((f32[128,8,128]{2,1,0:T(8,128)}), f32[128,8,128]{2,1,0:T(8,128)S(1)}, u32[]{:S(2)}, u32[]{:S(2)}) %all-to-all-start.1) | async-done | bytes 524320 | tf_op jit(solution)/shard_map/all_to_all | solution.py:857
  100.3 7.1 %after.1 = (f32[8,64,128]{2,1,0:T(8,128)}, f32[128,128]{1,0:T(8,128)S(1)}) custom-call(s32[2]{0:T(128)S(1)} %pad_add_fusion.place, f32[128,8,128]{2,1,0:T(8,128)S(1)} %all-to-all-done.1.got, f32[128,128]{1,0:T(8,128)S(1)} %copy-done.5, f32[128,128]{1,0:T(8,128)S(1)} %copy-done.4, f32[128,128]{1,0:T(8,128)S(1)} %copy-done.3, f32[128,128]{1,0:T(8,128)S(1)} %copy-done.2, ...), custom_call_target="tpu_custom_call" | custom-call | tf_op jit(solution)/shard_map/after/pallas_call | solution.py:783
  107.5 16.2 %all_to_all.26 = f32[128,1,128]{2,1,0:T(1,128)} all-to-all(f32[128,1,128]{2,1,0:T(1,128)S(1)} %bitcast.19), channel_id=1, replica_groups=mesh['dom_0'=4,'dom_1'=4,'grp_0'=4,'grp_1'=2] {'dom_0','dom_1','grp_0','..., dimensions={0} | all-to-all | bytes 131072 | tf_op jit(solution)/shard_map/all_to_all | solution.py:859
  123.7 1.5 %stress.1 = f32[6]{0:T(128)} custom-call(f32[128,128]{1,0:T(8,128)} %bitcast.24), custom_call_target="tpu_custom_call" | custom-call | tf_op jit(solution)/shard_map/stress/pallas_call | solution.py:817
  (18 shorter events, 0.1 us)
Async XLA Ops:
  4.7 31.4 %copy-start.1 = (f32[8,64,128]{2,1,0:T(8,128)S(1)}, f32[8,64,128]{2,1,0:T(8,128)}, u32[]{:S(2)}) copy-start(f32[8,64,128]{2,1,0:T(8,128)} %param.12) | copy-start | bytes 786436
  36.1 6.9 %copy-start = (f32[8,64,128]{2,1,0:T(8,128)S(1)}, f32[8,64,128]{2,1,0:T(8,128)}, u32[]{:S(2)}) copy-start(f32[8,64,128]{2,1,0:T(8,128)} %start.3) | copy-start | bytes 786436
  40.9 22.2 %collective-permute-start = (f32[13,64,128]{2,1,0:T(8,128)S(1)}, f32[13,64,128]{2,1,0:T(8,128)S(1)}, u32[]{:S(2)}, u32[]{:S(2)}) collective-permute-start(f32[13,64,128]{2,1,0:T(8,128)S(1)} %bitcast.23), channel_id=1, source_target_pairs={{0,8},{8,16},{16,24},{24,32},{32,40},{40,48},{48,56},{56,64},{64,7... | collective-permute-start | bytes 1277960 | tf_op jit(solution)/shard_map/ppermute | solution.py:829
  43.1 11.4 %collective-permute-start.4 = (f32[7,64,128]{2,1,0:T(8,128)S(1)}, f32[7,64,128]{2,1,0:T(8,128)S(1)}, u32[]{:S(2)}, u32[]{:S(2)}) collective-permute-start(f32[7,64,128]{2,1,0:T(8,128)S(1)} %get-tuple-element.30), channel_id=1, source_target_pairs={{8,0},{16,8},{24,16},{32,24},{40,32},{48,40},{56,48},{64,56},{72,6... | collective-permute-start | bytes 688136 | tf_op jit(solution)/shard_map/ppermute | solution.py:829
  44.4 11.3 %collective-permute-start.3 = (f32[7,64,128]{2,1,0:T(8,128)S(1)}, f32[7,64,128]{2,1,0:T(8,128)S(1)}, u32[]{:S(2)}, u32[]{:S(2)}) collective-permute-start(f32[7,64,128]{2,1,0:T(8,128)S(1)} %get-tuple-element.31), channel_id=1, source_target_pairs={{0,8},{8,16},{16,24},{24,32},{32,40},{40,48},{48,56},{56,64},{64,7... | collective-permute-start | bytes 688136 | tf_op jit(solution)/shard_map/ppermute | solution.py:829
  48.4 14.8 %collective-permute-start.2 = (f32[6,64,128]{2,1,0:T(8,128)S(1)}, f32[6,64,128]{2,1,0:T(8,128)S(1)}, u32[]{:S(2)}, u32[]{:S(2)}) collective-permute-start(f32[6,64,128]{2,1,0:T(8,128)S(1)} %bitcast.20), channel_id=1, source_target_pairs={{8,0},{16,8},{24,16},{32,24},{40,32},{48,40},{56,48},{64,56},{72,6... | collective-permute-start | bytes 589832 | tf_op jit(solution)/shard_map/ppermute | solution.py:829
  49.7 13.4 %collective-permute-start.1 = (f32[5,64,128]{2,1,0:T(8,128)S(1)}, f32[5,64,128]{2,1,0:T(8,128)S(1)}, u32[]{:S(2)}, u32[]{:S(2)}) collective-permute-start(f32[5,64,128]{2,1,0:T(8,128)S(1)} %bitcast.21), channel_id=1, source_target_pairs={{0,16},{8,24},{16,32},{24,40},{32,48},{40,56},{48,64},{56,72},{64,... | collective-permute-start | bytes 491528 | tf_op jit(solution)/shard_map/ppermute | solution.py:829
  55.9 12.5 %collective-permute-start.5 = (f32[3,64,128]{2,1,0:T(8,128)S(1)}, f32[3,64,128]{2,1,0:T(8,128)S(1)}, u32[]{:S(2)}, u32[]{:S(2)}) collective-permute-start(f32[3,64,128]{2,1,0:T(8,128)S(1)} %get-tuple-element.20), channel_id=1, source_target_pairs={{0,1},{1,2},{2,3},{3,4},{4,5},{5,6},{6,7},{8,9},{9,10},{10,11},{11... | collective-permute-start | bytes 294920 | tf_op jit(solution)/shard_map/ppermute | solution.py:829
  60.6 7.9 %collective-permute-start.6 = (f32[3,64,128]{2,1,0:T(8,128)S(1)}, f32[3,64,128]{2,1,0:T(8,128)S(1)}, u32[]{:S(2)}, u32[]{:S(2)}) collective-permute-start(f32[3,64,128]{2,1,0:T(8,128)S(1)} %get-tuple-element.21), channel_id=1, source_target_pairs={{1,0},{2,1},{3,2},{4,3},{5,4},{6,5},{7,6},{9,8},{10,9},{11,10},{12... | collective-permute-start | bytes 294920 | tf_op jit(solution)/shard_map/ppermute | solution.py:829
  63.4 5.0 %collective-permute-start.7 = (f32[3,64,128]{2,1,0:T(8,128)S(1)}, f32[3,64,128]{2,1,0:T(8,128)S(1)}, u32[]{:S(2)}, u32[]{:S(2)}) collective-permute-start(f32[3,64,128]{2,1,0:T(8,128)S(1)} %get-tuple-element.22), channel_id=1, source_target_pairs={{0,1},{1,2},{2,3},{3,4},{4,5},{5,6},{6,7},{8,9},{9,10},{10,11},{11... | collective-permute-start | bytes 294920 | tf_op jit(solution)/shard_map/ppermute | solution.py:829
  66.4 5.9 %collective-permute-start.8 = (f32[3,64,128]{2,1,0:T(8,128)S(1)}, f32[3,64,128]{2,1,0:T(8,128)S(1)}, u32[]{:S(2)}, u32[]{:S(2)}) collective-permute-start(f32[3,64,128]{2,1,0:T(8,128)S(1)} %get-tuple-element.23), channel_id=1, source_target_pairs={{1,0},{2,1},{3,2},{4,3},{5,4},{6,5},{7,6},{9,8},{10,9},{11,10},{12... | collective-permute-start | bytes 294920 | tf_op jit(solution)/shard_map/ppermute | solution.py:829
  77.3 23.0 %copy-start.2 = (f32[128,128]{1,0:T(8,128)S(1)}, f32[128,128]{1,0:T(8,128)}, u32[]{:S(2)}) copy-start(f32[128,128]{1,0:T(8,128)} %constant.30.clone.scale) | copy-start | bytes 196612
  77.3 23.0 %copy-start.3 = (f32[128,128]{1,0:T(8,128)S(1)}, f32[128,128]{1,0:T(8,128)}, u32[]{:S(2)}) copy-start(f32[128,128]{1,0:T(8,128)} %constant.29.clone.tz) | copy-start | bytes 196612
  77.3 23.0 %copy-start.4 = (f32[128,128]{1,0:T(8,128)S(1)}, f32[128,128]{1,0:T(8,128)}, u32[]{:S(2)}) copy-start(f32[128,128]{1,0:T(8,128)} %constant.28.clone.txy_t) | copy-start | bytes 196612
  77.3 23.0 %copy-start.5 = (f32[128,128]{1,0:T(8,128)S(1)}, f32[128,128]{1,0:T(8,128)}, u32[]{:S(2)}) copy-start(f32[128,128]{1,0:T(8,128)} %constant.27.clone.txy) | copy-start | bytes 196612
  78.2 22.1 %all-to-all-start.1 = ((f32[128,8,128]{2,1,0:T(8,128)}), f32[128,8,128]{2,1,0:T(8,128)S(1)}, u32[]{:S(2)}, u32[]{:S(2)}) async-start(f32[128,8,128]{2,1,0:T(8,128)} %broadcast_in_dim.2), calls=%async_computation.1 | async-start | bytes 1048576 | tf_op jit(solution)/shard_map/all_to_all | solution.py:857
  86.8 8.7 %collective-permute-start.10 = (f32[3,32,128]{2,1,0:T(8,128)S(1)}, f32[3,32,128]{2,1,0:T(8,128)S(1)}, u32[]{:S(2)}, u32[]{:S(2)}) collective-permute-start(f32[3,32,128]{2,1,0:T(8,128)S(1)} %get-tuple-element.32), channel_id=1, source_target_pairs={{8,0},{16,8},{24,16},{32,24},{40,32},{48,40},{56,48},{64,56},{72,6... | collective-permute-start | bytes 147464 | tf_op jit(solution)/shard_map/ppermute | solution.py:829
  88.1 7.4 %collective-permute-start.9 = (f32[3,32,128]{2,1,0:T(8,128)S(1)}, f32[3,32,128]{2,1,0:T(8,128)S(1)}, u32[]{:S(2)}, u32[]{:S(2)}) collective-permute-start(f32[3,32,128]{2,1,0:T(8,128)S(1)} %get-tuple-element.33), channel_id=1, source_target_pairs={{0,8},{8,16},{16,24},{24,32},{32,40},{40,48},{48,56},{56,64},{64,7... | collective-permute-start | bytes 147464 | tf_op jit(solution)/shard_map/ppermute | solution.py:829

commit v5 on v4

--- a/solution.py
+++ b/solution.py
@@ -286,21 +286,37 @@
         right[at + g] = hi
 
 
-def edges_kernel(start, u_lo, u_hi, left, right):
-    pack_edges(
-        [functools.partial(u_plane, p, u_lo, start, u_hi) for p in range(NU_)], left, right, 0
-    )
-
-
-def edges(start, u_lo, u_hi):
+def own_edges_kernel(start, left, right):
+    pack_edges([functools.partial(lambda q: start[q], p) for p in range(CX)], left, right, 0)
+
+
+def own_edges(start):
+    return pl.pallas_call(
+        own_edges_kernel,
+        out_shape=(sds(1, CY, LANES),) * 2,
+        in_specs=[VM],
+        out_specs=(VM,) * 2,
+        compiler_params=PAR,
+        name="own_edges",
+    )(start)
+
+
+def edges_kernel(own_left, own_right, u_lo, u_hi, left, right):
+    left[0] = own_left[0]
+    right[0] = own_right[0]
+    pack_edges([functools.partial(lambda q: u_lo[q], p) for p in range(HU)], left, right, 1)
+    pack_edges([functools.partial(lambda q: u_hi[q], p) for p in range(HU)], left, right, 2)
+
+
+def edges(own_left, own_right, u_lo, u_hi):
     return pl.pallas_call(
         edges_kernel,
         out_shape=(sds(UGROUPS, CY, LANES),) * 2,
-        in_specs=[VM] * 3,
+        in_specs=[VM] * 4,
         out_specs=(VM,) * 2,
         compiler_params=PAR,
         name="edges",
-    )(start, u_lo, u_hi)
+    )(own_left, own_right, u_lo, u_hi)
 
 
 def join_kernel(grid, from1, from2, above, f, left, right):
@@ -448,7 +464,8 @@
     slot = lanes_of((CY, LANES)) >> 4
     for p in range(NU_ + NF):
         if p < NU_:
-            g, k, from_left, from_right = p // 8, p % 8, u_from_left, u_from_right
+            g, k = (1, p) if p < HU else (0, p - HU) if p < HU + CX else (2, p - HU - CX)
+            from_left, from_right = u_from_left, u_from_right
         else:
             g, k, from_left, from_right = (p - NU_) // 8, (p - NU_) % 8, f_from_left, f_from_right
         edge = jnp.where(slot == k, from_right[g], 0.0)
@@ -836,7 +853,7 @@
     message = pack_atoms([v.reshape(-1) for v in (home, ox, oy, oz, size)], tiles)
     got = lax.all_to_all(message.reshape(NDEV, ROWS * LANES), ALL, 0, 0, tiled=True)
     got = got.reshape(NDEV * ROWS, LANES)
-    u_left, u_right = edges(start, lower, upper)
+    u_left, u_right = edges(*own_edges(start), lower, upper)
     grid, up2, down = deposit(got, valence)
     from1 = shift(grid[2 * CY : 15 * CY].reshape(13, CY, LANES), DOM, 1)
     from2 = shift(up2.reshape(5, CY, LANES), DOM, 2)

time: 126 us -> 126 us (level)
  no operation moved by 1% of the time
where the time goes in v5:
time: 126 us; the launch traced here: 125 us
  blocking collectives  47.6 us (38%)
  starting transfers between devices  39.5 us (31%)
  Pallas kernels  22.9 us (18%)
  waiting for transfers between devices  13.2 us (10%)
    all_to_all x1, blocking collectives, step(): lax.all_to_all(message.reshape(NDEV, ROWS * LANES), ALL, 0, 0, tiled=True)  31.4 us
    ppermute x11, starting transfers between devices, shift(): return lax.ppermute(value, axis, route)  30.9 us
    all_to_all x1, blocking collectives, step(): sums = lax.all_to_all(totals, ALL, 0, 0, tiled=True)  16.2 us
    all_to_all x1, starting transfers between devices, step(): everything = lax.all_to_all(chunks, ALL, 0, 0, tiled=True)  8.68 us
    ppermute x11, waiting for transfers between devices, shift(): return lax.ppermute(value, axis, route)  8.37 us
    pallas_call x1, Pallas kernels, after(): pl.pallas_call(after_kernel, out_shape=(sds(CX, CY, CZ), sds(NDEV, LANES)...  7.11 us
    pallas_call x1, Pallas kernels, before(): pl.pallas_call(before_kernel, out_shape=(sds(14, 2, CY, LANES), sds(12, 2...  4.99 us
    all_to_all x1, waiting for transfers between devices, step(): everything = lax.all_to_all(chunks, ALL, 0, 0, tiled=True)  4.85 us
  transfers between devices with their start and end apart: 12, of which 4 were waited for; matrix products, arithmetic and copies ran while one was open for 0% of the time, Pallas kernels for 0%

profile of v5, /device:TPU:1, one launch (start us, length us, event | category | flops | bytes accessed | tf_op | source)
XLA Modules:
  0.0 125.2 jit_solution(13138093192675987373)
XLA Ops:
  0.6 4.1 %pack_atoms.1 = f32[2176,128]{1,0:T(8,128)} custom-call(s32[256]{0:T(256)} %bitcast.25, s32[256]{0:T(256)} %bitcast.26, s32[256]{0:T(256)} %bitcast.27, s32[256]{0:T(256)} %bitcast.28, s32[256]{0:T(256)} %bitcast.29, f32[256,512]{1,0:T(8,128)} %tiles_h.1), custom_call_target="tpu_custom_call" | custom-call | tf_op jit(solution)/shard_map/pack_atoms/pallas_call | solution.py:146
  4.7 0.0 copy-start.1
  4.7 31.4 %all_to_all.25 = f32[128,1,2176]{2,1,0:T(1,128)S(1)} all-to-all(f32[128,1,2176]{2,1,0:T(1,128)} %bitcast.22), channel_id=1, replica_groups=mesh['dom_0'=4,'dom_1'=4,'grp_0'=4,'grp_1'=2] {'dom_0','dom_1','grp_0','..., dimensions={0} | all-to-all | bytes 2228224 | tf_op jit(solution)/shard_map/all_to_all | solution.py:854
  36.1 4.8 %deposit.1 = (f32[1024,128]{1,0:T(8,128)S(1)}, f32[320,128]{1,0:T(8,128)S(1)}, f32[384,128]{1,0:T(8,128)S(1)}) custom-call(f32[2176,128]{1,0:T(8,128)S(1)} %bitcast.17, f32[512,128]{1,0:T(8,128)S(1)} %bitcast.18), custom_call_target="tpu_custom_call" | custom-call | tf_op jit(solution)/shard_map/deposit/pallas_call | solution.py:246
  40.9 2.1 %collective-permute-start = (f32[13,64,128]{2,1,0:T(8,128)S(1)}, f32[13,64,128]{2,1,0:T(8,128)S(1)}, u32[]{:S(2)}, u32[]{:S(2)}) collective-permute-start(f32[13,64,128]{2,1,0:T(8,128)S(1)} %bitcast.23), channel_id=1, source_target_pairs={{0,8},{8,16},{16,24},{24,32},{32,40},{40,48},{48,56},{56,64},{64,7... | collective-permute-start | bytes 1277960 | tf_op jit(solution)/shard_map/ppermute | solution.py:846
  43.1 1.3 %collective-permute-start.4 = (f32[7,64,128]{2,1,0:T(8,128)S(1)}, f32[7,64,128]{2,1,0:T(8,128)S(1)}, u32[]{:S(2)}, u32[]{:S(2)}) collective-permute-start(f32[7,64,128]{2,1,0:T(8,128)S(1)} %get-tuple-element.34), channel_id=1, source_target_pairs={{8,0},{16,8},{24,16},{32,24},{40,32},{48,40},{56,48},{64,56},{72,6... | collective-permute-start | bytes 688136 | tf_op jit(solution)/shard_map/ppermute | solution.py:846
  44.4 4.0 %collective-permute-start.3 = (f32[7,64,128]{2,1,0:T(8,128)S(1)}, f32[7,64,128]{2,1,0:T(8,128)S(1)}, u32[]{:S(2)}, u32[]{:S(2)}) collective-permute-start(f32[7,64,128]{2,1,0:T(8,128)S(1)} %get-tuple-element.35), channel_id=1, source_target_pairs={{0,8},{8,16},{16,24},{24,32},{32,40},{40,48},{48,56},{56,64},{64,7... | collective-permute-start | bytes 688136 | tf_op jit(solution)/shard_map/ppermute | solution.py:846
  48.4 1.3 %collective-permute-start.2 = (f32[6,64,128]{2,1,0:T(8,128)S(1)}, f32[6,64,128]{2,1,0:T(8,128)S(1)}, u32[]{:S(2)}, u32[]{:S(2)}) collective-permute-start(f32[6,64,128]{2,1,0:T(8,128)S(1)} %bitcast.20), channel_id=1, source_target_pairs={{8,0},{16,8},{24,16},{32,24},{40,32},{48,40},{56,48},{64,56},{72,6... | collective-permute-start | bytes 589832 | tf_op jit(solution)/shard_map/ppermute | solution.py:846
  49.7 4.8 %collective-permute-start.1 = (f32[5,64,128]{2,1,0:T(8,128)S(1)}, f32[5,64,128]{2,1,0:T(8,128)S(1)}, u32[]{:S(2)}, u32[]{:S(2)}) collective-permute-start(f32[5,64,128]{2,1,0:T(8,128)S(1)} %bitcast.21), channel_id=1, source_target_pairs={{0,16},{8,24},{16,32},{24,40},{32,48},{40,56},{48,64},{56,72},{64,... | collective-permute-start | bytes 491528 | tf_op jit(solution)/shard_map/ppermute | solution.py:846
  54.5 0.1 own_edges.1
  54.6 0.0 collective-permute-done.4.u_hi
  54.6 1.1 collective-permute-done.3.u_lo
  55.7 0.2 edges.1
  55.9 4.6 %collective-permute-start.5 = (f32[3,64,128]{2,1,0:T(8,128)S(1)}, f32[3,64,128]{2,1,0:T(8,128)S(1)}, u32[]{:S(2)}, u32[]{:S(2)}) collective-permute-start(f32[3,64,128]{2,1,0:T(8,128)S(1)} %get-tuple-element.24), channel_id=1, source_target_pairs={{0,1},{1,2},{2,3},{3,4},{4,5},{5,6},{6,7},{8,9},{9,10},{10,11},{11... | collective-permute-start | bytes 294920 | tf_op jit(solution)/shard_map/ppermute | solution.py:846
  60.5 2.6 %collective-permute-start.6 = (f32[3,64,128]{2,1,0:T(8,128)S(1)}, f32[3,64,128]{2,1,0:T(8,128)S(1)}, u32[]{:S(2)}, u32[]{:S(2)}) collective-permute-start(f32[3,64,128]{2,1,0:T(8,128)S(1)} %get-tuple-element.25), channel_id=1, source_target_pairs={{1,0},{2,1},{3,2},{4,3},{5,4},{6,5},{7,6},{9,8},{10,9},{11,10},{12... | collective-permute-start | bytes 294920 | tf_op jit(solution)/shard_map/ppermute | solution.py:846
  63.0 0.0 collective-permute-done.1.from2
  63.1 0.2 join.1
  63.3 3.0 %collective-permute-start.7 = (f32[3,64,128]{2,1,0:T(8,128)S(1)}, f32[3,64,128]{2,1,0:T(8,128)S(1)}, u32[]{:S(2)}, u32[]{:S(2)}) collective-permute-start(f32[3,64,128]{2,1,0:T(8,128)S(1)} %get-tuple-element.26), channel_id=1, source_target_pairs={{0,1},{1,2},{2,3},{3,4},{4,5},{5,6},{6,7},{8,9},{9,10},{10,11},{11... | collective-permute-start | bytes 294920 | tf_op jit(solution)/shard_map/ppermute | solution.py:846
  66.3 1.9 %collective-permute-start.8 = (f32[3,64,128]{2,1,0:T(8,128)S(1)}, f32[3,64,128]{2,1,0:T(8,128)S(1)}, u32[]{:S(2)}, u32[]{:S(2)}) collective-permute-start(f32[3,64,128]{2,1,0:T(8,128)S(1)} %get-tuple-element.27), channel_id=1, source_target_pairs={{1,0},{2,1},{3,2},{4,3},{5,4},{6,5},{7,6},{9,8},{10,9},{11,10},{12... | collective-permute-start | bytes 294920 | tf_op jit(solution)/shard_map/ppermute | solution.py:846
  68.3 0.1 pad_add_fusion.place
  68.3 3.9 %collective-permute-done.8.f_from_right = f32[3,64,128]{2,1,0:T(8,128)S(1)} collective-permute-done((f32[3,64,128]{2,1,0:T(8,128)S(1)}, f32[3,64,128]{2,1,0:T(8,128)S(1)}, u32[]{:S(2)}, u32[]{:S(2)}) %collective-permute-start.8) | collective-permute-done | bytes 98336 | tf_op jit(solution)/shard_map/ppermute | solution.py:846
  72.3 5.0 %before.1 = (f32[14,2,64,128]{3,2,1,0:T(8,128)S(1)}, f32[12,2,64,128]{3,2,1,0:T(8,128)S(1)}, f32[8,32,128]{2,1,0:T(8,128)S(1)}, f32[8,128]{1,0:T(8,128)S(1)}) custom-call(s32[2]{0:T(128)S(1)} %pad_add_fusion.place, f32[20,64,128]{2,1,0:T(8,128)S(1)} %get-tuple-element.21.f_in, f32[7,64,128]{2,1,0:T(8,128)S(1)} %collective-permute-done.3.u_lo, ...), custom_call_target="tpu_custom_call" | custom-call | tf_op jit(solution)/shard_map/before/pallas_call | solution.py:560
  77.3 0.0 copy-start.5
  77.3 0.8 broadcast_in_dim.2
  78.1 8.7 %all-to-all-start.1 = ((f32[128,8,128]{2,1,0:T(8,128)}), f32[128,8,128]{2,1,0:T(8,128)S(1)}, u32[]{:S(2)}, u32[]{:S(2)}) async-start(f32[128,8,128]{2,1,0:T(8,128)} %broadcast_in_dim.2), calls=%async_computation.1 | async-start | bytes 1048576 | tf_op jit(solution)/shard_map/all_to_all | solution.py:874
  86.8 1.3 %collective-permute-start.10 = (f32[3,32,128]{2,1,0:T(8,128)S(1)}, f32[3,32,128]{2,1,0:T(8,128)S(1)}, u32[]{:S(2)}, u32[]{:S(2)}) collective-permute-start(f32[3,32,128]{2,1,0:T(8,128)S(1)} %get-tuple-element.36), channel_id=1, source_target_pairs={{8,0},{16,8},{24,16},{32,24},{40,32},{48,40},{56,48},{64,56},{72,6... | collective-permute-start | bytes 147464 | tf_op jit(solution)/shard_map/ppermute | solution.py:846
  88.1 4.0 %collective-permute-start.9 = (f32[3,32,128]{2,1,0:T(8,128)S(1)}, f32[3,32,128]{2,1,0:T(8,128)S(1)}, u32[]{:S(2)}, u32[]{:S(2)}) collective-permute-start(f32[3,32,128]{2,1,0:T(8,128)S(1)} %get-tuple-element.37), channel_id=1, source_target_pairs={{0,8},{8,16},{16,24},{24,32},{32,40},{40,48},{48,56},{56,64},{64,7... | collective-permute-start | bytes 147464 | tf_op jit(solution)/shard_map/ppermute | solution.py:846
  92.1 3.4 %collective-permute-done.10.f1_hi = f32[3,32,128]{2,1,0:T(8,128)S(1)} collective-permute-done((f32[3,32,128]{2,1,0:T(8,128)S(1)}, f32[3,32,128]{2,1,0:T(8,128)S(1)}, u32[]{:S(2)}, u32[]{:S(2)}) %collective-permute-start.10) | collective-permute-done | bytes 49184 | tf_op jit(solution)/shard_map/ppermute | solution.py:846
  95.5 4.8 %all-to-all-done.1.got = f32[128,8,128]{2,1,0:T(8,128)S(1)} async-done(((f32[128,8,128]{2,1,0:T(8,128)}), f32[128,8,128]{2,1,0:T(8,128)S(1)}, u32[]{:S(2)}, u32[]{:S(2)}) %all-to-all-start.1) | async-done | bytes 524320 | tf_op jit(solution)/shard_map/all_to_all | solution.py:874
  100.4 7.1 %after.1 = (f32[8,64,128]{2,1,0:T(8,128)}, f32[128,128]{1,0:T(8,128)S(1)}) custom-call(s32[2]{0:T(128)S(1)} %pad_add_fusion.place, f32[128,8,128]{2,1,0:T(8,128)S(1)} %all-to-all-done.1.got, f32[128,128]{1,0:T(8,128)S(1)} %copy-done.5, f32[128,128]{1,0:T(8,128)S(1)} %copy-done.4, f32[128,128]{1,0:T(8,128)S(1)} %copy-done.3, f32[128,128]{1,0:T(8,128)S(1)} %copy-done.2, ...), custom_call_target="tpu_custom_call" | custom-call | tf_op jit(solution)/shard_map/after/pallas_call | solution.py:800
  107.5 16.2 %all_to_all.26 = f32[128,1,128]{2,1,0:T(1,128)} all-to-all(f32[128,1,128]{2,1,0:T(1,128)S(1)} %bitcast.19), channel_id=1, replica_groups=mesh['dom_0'=4,'dom_1'=4,'grp_0'=4,'grp_1'=2] {'dom_0','dom_1','grp_0','..., dimensions={0} | all-to-all | bytes 131072 | tf_op jit(solution)/shard_map/all_to_all | solution.py:876
  123.7 1.5 %stress.1 = f32[6]{0:T(128)} custom-call(f32[128,128]{1,0:T(8,128)} %bitcast.24), custom_call_target="tpu_custom_call" | custom-call | tf_op jit(solution)/shard_map/stress/pallas_call | solution.py:834
  (19 shorter events, 0.1 us)
Async XLA Ops:
  4.7 31.4 %copy-start.1 = (f32[8,64,128]{2,1,0:T(8,128)S(1)}, f32[8,64,128]{2,1,0:T(8,128)}, u32[]{:S(2)}) copy-start(f32[8,64,128]{2,1,0:T(8,128)} %param.12) | copy-start | bytes 786436
  36.1 6.9 %copy-start = (f32[8,64,128]{2,1,0:T(8,128)S(1)}, f32[8,64,128]{2,1,0:T(8,128)}, u32[]{:S(2)}) copy-start(f32[8,64,128]{2,1,0:T(8,128)} %start.3) | copy-start | bytes 786436
  40.9 22.2 %collective-permute-start = (f32[13,64,128]{2,1,0:T(8,128)S(1)}, f32[13,64,128]{2,1,0:T(8,128)S(1)}, u32[]{:S(2)}, u32[]{:S(2)}) collective-permute-start(f32[13,64,128]{2,1,0:T(8,128)S(1)} %bitcast.23), channel_id=1, source_target_pairs={{0,8},{8,16},{16,24},{24,32},{32,40},{40,48},{48,56},{56,64},{64,7... | collective-permute-start | bytes 1277960 | tf_op jit(solution)/shard_map/ppermute | solution.py:846
  43.1 11.6 %collective-permute-start.4 = (f32[7,64,128]{2,1,0:T(8,128)S(1)}, f32[7,64,128]{2,1,0:T(8,128)S(1)}, u32[]{:S(2)}, u32[]{:S(2)}) collective-permute-start(f32[7,64,128]{2,1,0:T(8,128)S(1)} %get-tuple-element.34), channel_id=1, source_target_pairs={{8,0},{16,8},{24,16},{32,24},{40,32},{48,40},{56,48},{64,56},{72,6... | collective-permute-start | bytes 688136 | tf_op jit(solution)/shard_map/ppermute | solution.py:846
  44.4 11.3 %collective-permute-start.3 = (f32[7,64,128]{2,1,0:T(8,128)S(1)}, f32[7,64,128]{2,1,0:T(8,128)S(1)}, u32[]{:S(2)}, u32[]{:S(2)}) collective-permute-start(f32[7,64,128]{2,1,0:T(8,128)S(1)} %get-tuple-element.35), channel_id=1, source_target_pairs={{0,8},{8,16},{16,24},{24,32},{32,40},{40,48},{48,56},{56,64},{64,7... | collective-permute-start | bytes 688136 | tf_op jit(solution)/shard_map/ppermute | solution.py:846
  48.4 14.7 %collective-permute-start.2 = (f32[6,64,128]{2,1,0:T(8,128)S(1)}, f32[6,64,128]{2,1,0:T(8,128)S(1)}, u32[]{:S(2)}, u32[]{:S(2)}) collective-permute-start(f32[6,64,128]{2,1,0:T(8,128)S(1)} %bitcast.20), channel_id=1, source_target_pairs={{8,0},{16,8},{24,16},{32,24},{40,32},{48,40},{56,48},{64,56},{72,6... | collective-permute-start | bytes 589832 | tf_op jit(solution)/shard_map/ppermute | solution.py:846
  49.7 13.4 %collective-permute-start.1 = (f32[5,64,128]{2,1,0:T(8,128)S(1)}, f32[5,64,128]{2,1,0:T(8,128)S(1)}, u32[]{:S(2)}, u32[]{:S(2)}) collective-permute-start(f32[5,64,128]{2,1,0:T(8,128)S(1)} %bitcast.21), channel_id=1, source_target_pairs={{0,16},{8,24},{16,32},{24,40},{32,48},{40,56},{48,64},{56,72},{64,... | collective-permute-start | bytes 491528 | tf_op jit(solution)/shard_map/ppermute | solution.py:846
  55.9 12.5 %collective-permute-start.5 = (f32[3,64,128]{2,1,0:T(8,128)S(1)}, f32[3,64,128]{2,1,0:T(8,128)S(1)}, u32[]{:S(2)}, u32[]{:S(2)}) collective-permute-start(f32[3,64,128]{2,1,0:T(8,128)S(1)} %get-tuple-element.24), channel_id=1, source_target_pairs={{0,1},{1,2},{2,3},{3,4},{4,5},{5,6},{6,7},{8,9},{9,10},{10,11},{11... | collective-permute-start | bytes 294920 | tf_op jit(solution)/shard_map/ppermute | solution.py:846
  60.5 7.8 %collective-permute-start.6 = (f32[3,64,128]{2,1,0:T(8,128)S(1)}, f32[3,64,128]{2,1,0:T(8,128)S(1)}, u32[]{:S(2)}, u32[]{:S(2)}) collective-permute-start(f32[3,64,128]{2,1,0:T(8,128)S(1)} %get-tuple-element.25), channel_id=1, source_target_pairs={{1,0},{2,1},{3,2},{4,3},{5,4},{6,5},{7,6},{9,8},{10,9},{11,10},{12... | collective-permute-start | bytes 294920 | tf_op jit(solution)/shard_map/ppermute | solution.py:846
  63.3 5.0 %collective-permute-start.7 = (f32[3,64,128]{2,1,0:T(8,128)S(1)}, f32[3,64,128]{2,1,0:T(8,128)S(1)}, u32[]{:S(2)}, u32[]{:S(2)}) collective-permute-start(f32[3,64,128]{2,1,0:T(8,128)S(1)} %get-tuple-element.26), channel_id=1, source_target_pairs={{0,1},{1,2},{2,3},{3,4},{4,5},{5,6},{6,7},{8,9},{9,10},{10,11},{11... | collective-permute-start | bytes 294920 | tf_op jit(solution)/shard_map/ppermute | solution.py:846
  66.3 5.9 %collective-permute-start.8 = (f32[3,64,128]{2,1,0:T(8,128)S(1)}, f32[3,64,128]{2,1,0:T(8,128)S(1)}, u32[]{:S(2)}, u32[]{:S(2)}) collective-permute-start(f32[3,64,128]{2,1,0:T(8,128)S(1)} %get-tuple-element.27), channel_id=1, source_target_pairs={{1,0},{2,1},{3,2},{4,3},{5,4},{6,5},{7,6},{9,8},{10,9},{11,10},{12... | collective-permute-start | bytes 294920 | tf_op jit(solution)/shard_map/ppermute | solution.py:846
  77.2 23.1 %copy-start.2 = (f32[128,128]{1,0:T(8,128)S(1)}, f32[128,128]{1,0:T(8,128)}, u32[]{:S(2)}) copy-start(f32[128,128]{1,0:T(8,128)} %constant.30.clone.scale) | copy-start | bytes 196612
  77.3 23.1 %copy-start.3 = (f32[128,128]{1,0:T(8,128)S(1)}, f32[128,128]{1,0:T(8,128)}, u32[]{:S(2)}) copy-start(f32[128,128]{1,0:T(8,128)} %constant.29.clone.tz) | copy-start | bytes 196612
  77.3 23.1 %copy-start.4 = (f32[128,128]{1,0:T(8,128)S(1)}, f32[128,128]{1,0:T(8,128)}, u32[]{:S(2)}) copy-start(f32[128,128]{1,0:T(8,128)} %constant.28.clone.txy_t) | copy-start | bytes 196612
  77.3 23.1 %copy-start.5 = (f32[128,128]{1,0:T(8,128)S(1)}, f32[128,128]{1,0:T(8,128)}, u32[]{:S(2)}) copy-start(f32[128,128]{1,0:T(8,128)} %constant.27.clone.txy) | copy-start | bytes 196612
  78.1 22.2 %all-to-all-start.1 = ((f32[128,8,128]{2,1,0:T(8,128)}), f32[128,8,128]{2,1,0:T(8,128)S(1)}, u32[]{:S(2)}, u32[]{:S(2)}) async-start(f32[128,8,128]{2,1,0:T(8,128)} %broadcast_in_dim.2), calls=%async_computation.1 | async-start | bytes 1048576 | tf_op jit(solution)/shard_map/all_to_all | solution.py:874
  86.8 8.7 %collective-permute-start.10 = (f32[3,32,128]{2,1,0:T(8,128)S(1)}, f32[3,32,128]{2,1,0:T(8,128)S(1)}, u32[]{:S(2)}, u32[]{:S(2)}) collective-permute-start(f32[3,32,128]{2,1,0:T(8,128)S(1)} %get-tuple-element.36), channel_id=1, source_target_pairs={{8,0},{16,8},{24,16},{32,24},{40,32},{48,40},{56,48},{64,56},{72,6... | collective-permute-start | bytes 147464 | tf_op jit(solution)/shard_map/ppermute | solution.py:846
  88.1 7.4 %collective-permute-start.9 = (f32[3,32,128]{2,1,0:T(8,128)S(1)}, f32[3,32,128]{2,1,0:T(8,128)S(1)}, u32[]{:S(2)}, u32[]{:S(2)}) collective-permute-start(f32[3,32,128]{2,1,0:T(8,128)S(1)} %get-tuple-element.37), channel_id=1, source_target_pairs={{0,8},{8,16},{16,24},{24,32},{32,40},{40,48},{48,56},{56,64},{64,7... | collective-permute-start | bytes 147464 | tf_op jit(solution)/shard_map/ppermute | solution.py:846
